TPU v7x, 32 devices: a whole 2x2x4 slice. The times are simulated.
32 devices in a mesh: vel: 4 (over x, core), gx: 4 (over z), gy: 2 (over y).
Axes of the slice: x: 2, y: 2, z: 4, core: 2. Of those that a mesh axis runs over, the one named last changes fastest.
Arguments:
- previous: bfloat16 [4096, 32, 256], P('vel', 'gx', 'gy'), may hold values from 0 to 4, as said below
- relax_time: float32 [32, 256], P('gx', 'gy'), may hold values from 0.05 to 20
- left_right_kind: int32 [2, 256], P(None, 'gy'), may hold values from 0 to 1
- bottom_top_kind: int32 [2, 32], P(None, 'gx'), may hold values from 0 to 1
- left_right_inflow: bfloat16 [4096, 2, 256], P('vel', None, 'gy'), may hold values from 0.049804688 to 1
- bottom_top_inflow: bfloat16 [4096, 2, 32], P('vel', None, 'gx'), may hold values from 0.049804688 to 1
Outputs:
- updated: bfloat16 [4096, 32, 256], P('vel', 'gx', 'gy')
Inputs may be any that keep to these rules, and one draw needn't show every extreme that they name: previous is positive in every entry. `left_right_kind`: 1 marks an inflow edge cell, 0 a diffuse wall. `bottom_top_kind`: 1 marks an inflow edge cell, 0 a diffuse wall.
All inputs are finite; a program needn't handle non-finite values.
Results may differ from a plain program's by a relative error of at most 0.0042.
Values may be sent and summed in bfloat16 or wider, within the bound.
No kernel may reach another device: no remote copies, remote signals or barrier semaphores. Data moves between devices by JAX's collectives and lax.ppermute only.
A program may use at most 128 MiB of HBM per device.

v0:
```python
import functools
import math

import jax
import jax.numpy as jnp
import numpy as np
from jax import lax
from jax.experimental import pallas as pl
from jax.experimental.pallas import tpu as pltpu
from jax.sharding import PartitionSpec as P

NVX = 64
HALF = NVX // 2
NEWTON = 2
SWEEPS = 4
COURANT = 100.0
STEP = 12.0 / NVX
UNIT = STEP / 2.0
WEIGHT = STEP * STEP / (2.0 * math.pi)
TIME_STEP = COURANT / ((NVX - 1) * STEP)
LANES = 128
HIGHEST = lax.Precision.HIGHEST
F32 = jnp.float32
BF16 = jnp.bfloat16


def wall_norm_value():
    line = (np.arange(NVX) - (NVX - 1) / 2.0) * STEP
    gauss = np.exp(-line * line / 2.0)
    return float(np.sum(np.maximum(line, 0.0) * gauss) * np.sum(gauss) * WEIGHT)


FLUX_SCALE = WEIGHT * UNIT / wall_norm_value()


def nn(a, b, precision=None):
    return lax.dot_general(a, b, (((1,), (0,)), ((), ())), precision=precision, preferred_element_type=F32)


def nt(a, b, precision=None):
    return lax.dot_general(a, b, (((1,), (1,)), ((), ())), precision=precision, preferred_element_type=F32)


def tn(a, b, precision=None):
    return lax.dot_general(a, b, (((0,), (0,)), ((), ())), precision=precision, preferred_element_type=F32)


def iota(shape, dim):
    return lax.broadcasted_iota(jnp.int32, shape, dim)


def lane_ints(first_ky, sign, start, shape):
    lane = iota(shape, len(shape) - 1) + start
    ix = 2 * (lane % HALF + HALF * sign) - (NVX - 1)
    iy = 2 * (first_ky + lane // HALF) - (NVX - 1)
    return ix, iy


def flip_matrix(up, size):
    row, col = iota((size, size), 0), iota((size, size), 1)
    return (col == jnp.where(up, row, size - 1 - row)).astype(F32)


def reverse_rows(a):
    return jnp.concatenate([a[i : i + 1] for i in range(a.shape[0] - 1, -1, -1)], axis=0)


def pieces(a):
    high = a.astype(BF16).astype(F32)
    rest = a - high
    middle = rest.astype(BF16).astype(F32)
    return [high, middle, rest - middle]


def moments_kernel(info, pt, pay, ymsg):
    cells_x, _, count, cells_y = pt.shape
    first_ky, up = info[0], info[1] == 1
    y_out = jnp.where(up, cells_y - 1, 0)
    row = iota((16, count), 0)
    weights = []
    for sign in range(2):
        ix, iy = lane_ints(first_ky, sign, 0, (16, count))
        energy = ix * ix + iy * iy
        low = energy % 64
        table = jnp.where(row == 0, 1, jnp.where(row == 1, ix, jnp.where(row == 2, iy, jnp.where(
            row == 3, energy - low, jnp.where(row == 4, low, jnp.where(row == 5, jnp.abs(ix), 0))))))
        weights.append(table.astype(F32).astype(BF16))
    edge = [jnp.zeros((16, count), F32) for _ in range(2)]
    out_row = [None, None]
    pick_row, pick_col = iota((16, cells_y), 0), iota((16, cells_y), 1)
    for x in range(cells_x):
        total = None
        for sign in range(2):
            block = pt[x, sign]
            part = nn(weights[sign], block)
            if x == (cells_x - 1) * sign:
                out_row[sign] = part[5:6]
            total = part if total is None else total + part
            at = x if sign else cells_x - 1 - x
            pick = ((pick_row == at) & (pick_col == y_out)).astype(F32).astype(BF16)
            edge[sign] = edge[sign] + nt(pick, block)
        pay[0, x : x + 1, :] = total[0:1]
        pay[1, x : x + 1, :] = total[1:2]
        pay[2, x : x + 1, :] = total[2:3]
        pay[3, x : x + 1, :] = total[3:4] + total[4:5]
    flip = flip_matrix(up, cells_y)
    fx = jnp.concatenate([out_row[0], out_row[1], jnp.zeros((6, cells_y), F32)], axis=0)
    pay[4] = nt(fx, flip, HIGHEST)
    for sign in range(2):
        total = jnp.zeros((cells_x, LANES), F32)
        for at in range(count // LANES):
            _, iy = lane_ints(first_ky, sign, at * LANES, (cells_x, LANES))
            total += jnp.abs(iy).astype(F32) * edge[sign][:cells_x, at * LANES : (at + 1) * LANES]
        pay[6 - sign] = total
        ymsg[sign] = edge[sign][:cells_x].astype(BF16)


def newton_params(u0, u1, u2, u3):
    ux, uy = u1 / u0, u2 / u0
    square = ux * ux + uy * uy
    temperature = u3 / u0 - square / 2.0
    p = [jnp.log(u0 / temperature) - square / (2.0 * temperature), ux / temperature, uy / temperature, -1.0 / temperature]
    line = [float((i - (NVX - 1) / 2.0) * STEP) for i in range(NVX)]
    for _ in range(NEWTON):
        half_p3 = p[3] * 0.5
        sums, tops = [], []
        for slope in (p[1], p[2]):
            top = None
            for value in line:
                arg = value * (slope + value * half_p3)
                top = arg if top is None else jnp.maximum(top, arg)
            total = [None] * 5
            for value in line:
                term = jnp.exp(value * (slope + value * half_p3) - top)
                for power in range(5):
                    total[power] = term if total[power] is None else total[power] + term
                    term = term * value
            sums.append(total)
            tops.append(top)
        scale = jnp.exp(p[0] + (tops[0] + tops[1])) * WEIGHT
        x = sums[0]
        y = [scale * t for t in sums[1]]
        x2, y2 = x[2] * y[0], x[0] * y[2]
        n = [x[0] * y[0], x[1] * y[0], x[0] * y[1], (x2 + y2) * 0.5, x2, x[1] * y[1],
             (x[3] * y[0] + x[1] * y[2]) * 0.5, y2, (x[2] * y[1] + x[0] * y[3]) * 0.5,
             (x[4] * y[0] + 2.0 * (x[2] * y[2]) + x[0] * y[4]) * 0.25]
        layout = [[0, 1, 2, 3], [1, 4, 5, 6], [2, 5, 7, 8], [3, 6, 8, 9]]
        matrix = [[n[layout[r][c]] for c in range(4)] for r in range(4)]
        target = [n[0] - u0, n[1] - u1, n[2] - u2, n[3] - u3]
        for pivot in range(4):
            for lower in range(pivot + 1, 4):
                factor = matrix[lower][pivot] / matrix[pivot][pivot]
                for col in range(pivot, 4):
                    matrix[lower][col] = matrix[lower][col] - factor * matrix[pivot][col]
                target[lower] = target[lower] - factor * target[pivot]
        result = [None] * 4
        for pivot in (3, 2, 1, 0):
            accum = target[pivot]
            for col in range(pivot + 1, 4):
                accum = accum - matrix[pivot][col] * result[col]
            result[pivot] = accum / matrix[pivot][pivot]
        p = [a - b for a, b in zip(p, result)]
    return p


def block_speeds(first_ky, block, per_sign, shape):
    ix, iy = lane_ints(first_ky, block // per_sign, (block % per_sign) * LANES, shape)
    return jnp.abs(ix).astype(F32) * UNIT, jnp.abs(iy).astype(F32) * UNIT


def fill_inflow(info, kindy, flux, g, xin, yin, xw, yw, kx):
    blocks, slots, padded, _ = g.shape
    cells_x, cells_y = slots - 1, padded - 8
    per_sign = blocks // 2
    first_ky, up = info[0], info[1] == 1
    devices = flux.shape[0]
    lo = [sum(flux[d, at] for d in range(devices // 2)) for at in range(3)]
    hi = [sum(flux[d, at] for d in range(devices // 2, devices)) for at in range(3)]
    same = jnp.where(up, hi[0], lo[0])
    other = [jnp.where(up, a, b) for a, b in zip(lo, hi)]
    anti = flip_matrix(False, cells_y)
    fx = (same + nn(other[0], anti, HIGHEST)) * FLUX_SCALE
    fy = jnp.sum(other[1], axis=1, keepdims=True) + reverse_rows(jnp.sum(other[2], axis=1, keepdims=True))
    fy = fy * FLUX_SCALE
    fy = [reverse_rows(fy), fy]
    side = jnp.where(up, 0, 1)
    cell = iota((cells_x, LANES), 0)
    y_wall = info[4] == 1
    for sign in range(2):
        pick = (iota((8, LANES), 0) == 1 - sign).astype(F32)
        column = tn(fx, pick, HIGHEST)
        x_wall = info[3 - sign] == 1
        ky_kind = jnp.zeros((cells_x, LANES), jnp.int32)
        for x in range(cells_x):
            ky_kind = jnp.where(cell == (x if sign else cells_x - 1 - x), kindy[side, x], ky_kind)
        fy_wide = jnp.broadcast_to(fy[sign], (cells_x, LANES))
        for at in range(per_sign):
            block = sign * per_sign + at
            ix, iy = lane_ints(first_ky, sign, at * LANES, (8, LANES))
            maxwell = jnp.exp((ix * ix + iy * iy).astype(F32) * (-UNIT * UNIT / 2.0))
            ghost = jnp.where(kx[sign] == 1.0, xw[block], column * maxwell[0:1])
            g[block, 0, 8:, :] = jnp.where(x_wall, ghost, xin(block))
            ghost_y = jnp.where(ky_kind == 1, yw[block], fy_wide * maxwell)
            value = jnp.where(y_wall, ghost_y, yin(block))
            for x in range(cells_x):
                g[block, 1 + x, 7:8, :] = value[x : x + 1]


def sweep(info, g, s, r):
    blocks, slots, padded, _ = g.shape
    cells_x, cells_y = slots - 1, padded - 8
    first_ky = info[0]

    def step(block, carry):
        ax, ay = block_speeds(first_ky, block, blocks // 2, (8, LANES))
        for x in range(cells_x - 1, -1, -1):
            for at in range(cells_y // 8 - 1, -1, -1):
                here = pl.ds(8 * at, 8)
                value = s[block, x, here, :] + ax * g[block, x, pl.ds(8 + 8 * at, 8), :]
                value += ay * g[block, 1 + x, pl.ds(7 + 8 * at, 8), :]
                value = (value * r[block, x, here, :]).astype(BF16).astype(F32)
                g[block, 1 + x, pl.ds(8 + 8 * at, 8), :] = value
        return carry

    lax.fori_loop(0, blocks, step, 0)


def send_out(info, g, xmsg, ymsg, flux):
    blocks, slots, padded, _ = g.shape
    cells_x, cells_y = slots - 1, padded - 8
    per_sign = blocks // 2
    fx = None
    for sign in range(2):
        total = jnp.zeros((cells_y, LANES), F32)
        total_y = jnp.zeros((cells_x, LANES), F32)
        for at in range(per_sign):
            block = sign * per_sign + at
            ix, iy = lane_ints(info[0], sign, at * LANES, (8, LANES))
            ix, iy = jnp.abs(ix).astype(F32), jnp.abs(iy).astype(F32)
            row = g[block, cells_x, 8:, :]
            xmsg[sign][at] = row.astype(BF16)
            total += row * ix[0:1]
            edge = jnp.concatenate([g[block, 1 + x, padded - 1 : padded, :] for x in range(cells_x)], axis=0)
            ymsg[block] = edge.astype(BF16)
            total_y += edge * iy
        pick = (iota((8, LANES), 0) == sign).astype(F32)
        part = nt(pick, total, HIGHEST)
        fx = part if fx is None else fx + part
        flux[2 - sign] = total_y
    flux[0] = fx


def first_kernel(info, kindy, ag, relax, kindx, pt, from_left, from_right, yrecv, lri, bti,
                 g, s, r, xw, yw, kx, xmsg0, xmsg1, ymsg, flux, ps):
    cells_x, _, count, cells_y = pt.shape
    per_sign = count // LANES
    blocks = 2 * per_sign
    first_ky, up = info[0], info[1] == 1
    total = [sum(ag[d, q] for d in range(ag.shape[0])) for q in range(4)]
    tau = relax[...]
    p = newton_params(total[0] * WEIGHT, total[1] * (WEIGHT * UNIT), total[2] * (WEIGHT * UNIT),
                      total[3] * (WEIGHT * UNIT * UNIT / 2.0))
    lead = p[0] - jnp.log(tau)
    rows = pieces(lead) + pieces(p[1] * UNIT) + pieces(p[2] * UNIT) + pieces(p[3] * (UNIT * UNIT / 2.0))
    rows += pieces(1.0 / TIME_STEP + 1.0 / tau)
    flip = flip_matrix(up, cells_y).astype(BF16)
    for at, piece in enumerate(rows):
        for x in range(cells_x):
            ps[x, at : at + 1, :] = piece[x : x + 1]
    for x in range(cells_x):
        ps[x, 15:16, :] = jnp.zeros((1, cells_y), F32)
    kind = jnp.concatenate([kindx[1:2], kindx[0:1], jnp.zeros((6, cells_y), jnp.int32)], axis=0).astype(F32)
    kind = nt(kind.astype(BF16), flip).astype(BF16)
    for sign in range(2):
        kx[sign] = tn(kind, (iota((8, LANES), 0) == sign).astype(F32).astype(BF16))
        for at in range(per_sign):
            block = sign * per_sign + at
            chunk = [(at * (LANES // HALF) + i) * NVX + HALF * sign for i in range(LANES // HALF)]
            part = jnp.concatenate(
                [lri[c : c + HALF, (1 - sign) * cells_y : (2 - sign) * cells_y] for c in chunk], axis=0)
            xw[block] = nt(flip, part)
            part = jnp.concatenate([bti[c : c + HALF, :] for c in chunk], axis=0)
            row, col = iota((16, cells_x), 0), iota((16, cells_x), 1)
            order = (col == (row if sign else cells_x - 1 - row)).astype(F32).astype(BF16)
            yw[block] = nt(order, part)[:cells_x]
    row = iota((16, LANES), 0)

    def build(xt, carry):
        for sign in range(2):
            x = xt if sign else cells_x - 1 - xt
            mine = nt(ps[x].astype(BF16), flip)
            table = mine.astype(BF16)
            base = tn(table, ((row >= 12) & (row < 15)).astype(F32).astype(BF16))
            for at in range(per_sign):
                block = sign * per_sign + at
                ix, iy = lane_ints(first_ky, sign, at * LANES, (16, LANES))
                energy = ix * ix + iy * iy
                basis = jnp.where(row < 3, 1, jnp.where(row < 6, ix, jnp.where(row < 9, iy, jnp.where(row < 12, energy - energy % 64, 0))))
                basis2 = jnp.where((row >= 9) & (row < 12), energy % 64, 0)
                basis = jnp.concatenate([basis, basis2], axis=0).astype(F32).astype(BF16)
                arg = tn(jnp.concatenate([table, table], axis=0), basis)
                value = nt(flip, pt[x, sign, at * LANES : (at + 1) * LANES, :])
                g[block, 1 + xt, 8:, :] = value
                s[block, xt] = value * (1.0 / TIME_STEP) + jnp.exp(arg)
                ax, ay = block_speeds(first_ky, block, per_sign, (8, LANES))
                r[block, xt] = 1.0 / (base + (ax + ay)[0:1])
        return carry

    lax.fori_loop(0, cells_x, build, 0)

    def xin(block):
        source = from_left if block >= per_sign else from_right
        at = block % per_sign
        return nt(flip, source[at * LANES : (at + 1) * LANES, :])

    def yin(block):
        at = block % per_sign
        return yrecv[block // per_sign, :, at * LANES : (at + 1) * LANES].astype(F32)

    fill_inflow(info, kindy, ag.at[:, 4:7], g, xin, yin, xw, yw, kx)
    sweep(info, g, s, r)
    send_out(info, g, (xmsg0, xmsg1), ymsg, flux)


def next_kernel(last, info, kindy, ag, from_left, from_right, yrecv, xw, yw, kx, s, r, g_in, *outs):
    blocks, slots, padded, _ = g_in.shape
    per_sign = blocks // 2
    if last:
        out, g = outs
    else:
        g, xmsg0, xmsg1, ymsg, flux = outs

    def xin(block):
        source = from_left if block >= per_sign else from_right
        return source[block % per_sign].astype(F32)

    def yin(block):
        return yrecv[block].astype(F32)

    fill_inflow(info, kindy, ag, g, xin, yin, xw, yw, kx)
    sweep(info, g, s, r)
    if not last:
        send_out(info, g, (xmsg0, xmsg1), ymsg, flux)
        return
    cells_x, cells_y = slots - 1, padded - 8
    flip = flip_matrix(info[1] == 1, cells_y).astype(BF16)

    def emit(xt, carry):
        for sign in range(2):
            x = xt if sign else cells_x - 1 - xt
            for at in range(per_sign):
                value = g[sign * per_sign + at, 1 + xt, 8:, :].astype(BF16)
                out[x, sign, at * LANES : (at + 1) * LANES, :] = tn(value, flip).astype(BF16)
        return carry

    lax.fori_loop(0, cells_x, emit, 0)


def call(kernel, outs, n_smem, ins, scratch=(), aliases=None, mib=20):
    vmem = pl.BlockSpec(memory_space=pltpu.VMEM)
    smem = pl.BlockSpec(memory_space=pltpu.SMEM)
    return pl.pallas_call(
        kernel,
        out_shape=outs,
        in_specs=[smem] * n_smem + [vmem] * (len(ins) - n_smem),
        out_specs=jax.tree.map(lambda _: vmem, outs),
        scratch_shapes=list(scratch),
        input_output_aliases=aliases or {},
        compiler_params=pltpu.CompilerParams(vmem_limit_bytes=mib << 20),
    )(*ins)


def body(previous, relax_time, left_right_kind, bottom_top_kind, left_right_inflow, bottom_top_inflow):
    vel_rows, cells_x, cells_y = previous.shape
    local_ky = vel_rows // NVX
    count = local_ky * HALF
    per_sign = count // LANES
    blocks = 2 * per_sign
    nvel, ngx, ngy = lax.axis_size("vel"), lax.axis_size("gx"), lax.axis_size("gy")
    v, ix, iy = lax.axis_index("vel"), lax.axis_index("gx"), lax.axis_index("gy")
    up = v >= nvel // 2
    y_wall = jnp.where(up, iy == 0, iy == ngy - 1)
    info = jnp.stack([v * local_ky, up.astype(jnp.int32), (ix == 0).astype(jnp.int32),
                      (ix == ngx - 1).astype(jnp.int32), y_wall.astype(jnp.int32)])
    right = [(i, i + 1) for i in range(ngx - 1)]
    left = [(i + 1, i) for i in range(ngx - 1)]
    along = []
    for d in range(nvel):
        for j in range(ngy - 1):
            along.append((d * ngy + j, d * ngy + j + 1) if d >= nvel // 2 else (d * ngy + j + 1, d * ngy + j))

    def shift_y(a):
        return lax.ppermute(a, ("vel", "gy"), along)

    pt = previous.reshape(local_ky, 2, HALF, cells_x, cells_y).transpose(3, 1, 0, 2, 4)
    pt = pt.reshape(cells_x, 2, count, cells_y)
    from_left = lax.ppermute(pt[cells_x - 1, 1], "gx", right)
    from_right = lax.ppermute(pt[0, 0], "gx", left)
    sds = jax.ShapeDtypeStruct
    pay, ymsg = call(
        moments_kernel,
        (sds((7, 8, LANES), F32), sds((2, cells_x, count), BF16)),
        1, (info, pt), mib=16)
    yrecv = shift_y(ymsg)
    ag = lax.all_gather(pay, "vel")
    lri = left_right_inflow.reshape(vel_rows, 2 * cells_y)
    bti = jnp.where(up, bottom_top_inflow[:, 0, :], bottom_top_inflow[:, 1, :])
    g_shape = sds((blocks, cells_x + 1, cells_y + 8, LANES), F32)
    full = sds((blocks, cells_x, cells_y, LANES), F32)
    messages = (sds((per_sign, cells_y, LANES), BF16), sds((per_sign, cells_y, LANES), BF16),
                sds((blocks, cells_x, LANES), BF16), sds((3, 8, LANES), F32))
    g, s, r, xw, yw, kx, xmsg0, xmsg1, ymsg, flux = call(
        first_kernel,
        (g_shape, full, full, sds((blocks, cells_y, LANES), F32), sds((blocks, cells_x, LANES), F32),
         sds((2, cells_y, LANES), F32)) + messages,
        2,
        (info, bottom_top_kind, ag, relax_time, left_right_kind, pt, from_left, from_right, yrecv, lri, bti),
        scratch=[pltpu.VMEM((cells_x, 16, cells_y), F32)], mib=32)
    for number in range(1, SWEEPS):
        from_left = lax.ppermute(xmsg1, "gx", right)
        from_right = lax.ppermute(xmsg0, "gx", left)
        yrecv = shift_y(ymsg)
        ag = lax.all_gather(flux, "vel")
        last = number == SWEEPS - 1
        ins = (info, bottom_top_kind, ag, from_left, from_right, yrecv, xw, yw, kx, s, r, g)
        if last:
            out, _ = call(functools.partial(next_kernel, True),
                          (sds((cells_x, 2, count, cells_y), BF16), g_shape), 2, ins, aliases={11: 1}, mib=32)
        else:
            g, xmsg0, xmsg1, ymsg, flux = call(
                functools.partial(next_kernel, False), (g_shape,) + messages, 2, ins, aliases={11: 0}, mib=32)
    out = out.reshape(cells_x, 2, local_ky, HALF, cells_y).transpose(2, 1, 3, 0, 4)
    return out.reshape(vel_rows, cells_x, cells_y)


def solution(mesh):
    return jax.shard_map(
        body,
        mesh=mesh,
        in_specs=(P("vel", "gx", "gy"), P("gx", "gy"), P(None, "gy"), P(None, "gx"), P("vel", None, "gy"), P("vel", None, "gx")),
        out_specs=P("vel", "gx", "gy"),
        check_vma=False,
    )
```

profile of v0, /device:TPU:0, one launch (start us, length us, event | category | flops | bytes accessed | tf_op | source)
XLA Modules:
  0.0 82.8 jit_solution(1455718041791482077)
XLA Ops:
  0.0 0.0 copy-start.4
  0.0 0.0 copy-start.3
  0.0 0.0 copy-start
  0.0 2.0 %copy.14 = bf16[16,2,32,8,128]{4,2,0,1,3:T(8,128)(2,1)S(1)} copy(bf16[16,2,32,8,128]{4,3,2,1,0:T(8,128)(2,1)} %bitcast.36) | data formatting | bytes 4194304 | tf_op jit(solution)/shard_map/reshape | solution.py:395
  2.1 0.1 stack.39.info
  2.2 1.7 %shard_map.64 = (f32[7,8,128]{2,1,0:T(8,128)S(1)}, bf16[2,8,512]{2,1,0:T(8,128)(2,1)S(1)}) custom-call(s32[5]{0:T(128)S(1)} %stack.39.info, bf16[8,2,512,128]{3,2,1,0:T(8,128)(2,1)S(1)} %bitcast.27), custom_call_target="tpu_custom_call" | custom-call | tf_op jit(solution)/shard_map/pallas_call | solution.py:362
  3.9 1.3 %collective-permute-start.2 = (bf16[2,8,512]{2,1,0:T(8,128)(2,1)S(1)}, bf16[2,8,512]{2,1,0:T(8,128)(2,1)S(1)}, u32[]{:S(2)}, u32[]{:S(2)}) collective-permute-start(bf16[2,8,512]{2,1,0:T(8,128)(2,1)S(1)} %get-tuple-element.29), channel_id=1, source_target_pairs={{1,0},{9,8},{16,17},{24,25},{3,2},{11,10},{18,19},{26,27},{5,4},{1... | collective-permute-start | bytes 49160 | tf_op jit(solution)/shard_map/ppermute | solution.py:393
  5.2 0.7 slice_bitcast_fusion
  5.9 1.3 %collective-permute-start.1 = (bf16[512,128]{1,0:T(8,128)(2,1)}, bf16[512,128]{1,0:T(8,128)(2,1)S(1)}, u32[]{:S(2)}, u32[]{:S(2)}) collective-permute-start(bf16[512,128]{1,0:T(8,128)(2,1)} %get-tuple-element.51), channel_id=1, source_target_pairs={{2,0},{4,2},{6,4},{3,1},{5,3},{7,5},{10,8},{12,10},{14,12},{11,9},... | collective-permute-start | bytes 393224 | tf_op jit(solution)/shard_map/ppermute | solution.py:398
  7.2 5.6 %collective-permute-start = (bf16[512,128]{1,0:T(8,128)(2,1)}, bf16[512,128]{1,0:T(8,128)(2,1)S(1)}, u32[]{:S(2)}, u32[]{:S(2)}) collective-permute-start(bf16[512,128]{1,0:T(8,128)(2,1)} %get-tuple-element.52), channel_id=1, source_target_pairs={{0,2},{2,4},{4,6},{1,3},{3,5},{5,7},{8,10},{10,12},{12,14},{9,11},... | collective-permute-start | bytes 393224 | tf_op jit(solution)/shard_map/ppermute | solution.py:397
  12.8 0.0 copy-done.4
  12.9 0.2 copy.16
  13.0 0.2 copy.15
  13.2 7.5 %all-gather = f32[28,8,128]{2,1,0:T(8,128)S(1)} all-gather(f32[7,8,128]{2,1,0:T(8,128)S(1)} %get-tuple-element.28), channel_id=2, replica_groups=mesh['vel'=4,'gx'=4,'gy'=2] {'vel'}, dimensions={0}, use_global_device_ids=true | all-gather | bytes 143360 | tf_op jit(solution)/shard_map/all_gather | solution.py:405
  20.8 0.0 copy-done.3
  20.8 0.1 copy.20
  20.9 0.0 collective-permute-done.2.yrecv
  20.9 0.0 collective-permute-done.1.from_right
  20.9 0.0 collective-permute-done.from_left
  20.9 0.0 copy-done
  20.9 0.0 copy-done.1
  20.9 0.0 copy-done.2
  20.9 10.3 %shard_map.65 = (f32[8,9,136,128]{3,2,1,0:T(8,128)S(1)}, f32[8,8,128,128]{3,2,1,0:T(8,128)S(1)}, f32[8,8,128,128]{3,2,1,0:T(8,128)S(1)}, f32[8,128,128]{2,1,0:T(...) custom-call(s32[5]{0:T(128)S(1)} %stack.39.info, ...), custom_call_target="tpu_custom_call" | custom-call | tf_op jit(solution)/shard_map/pallas_call | solution.py:362
  31.2 3.5 %collective-permute-start.3 = (bf16[4,128,128]{2,1,0:T(8,128)(2,1)S(1)}, bf16[4,128,128]{2,1,0:T(8,128)(2,1)S(1)}, u32[]{:S(2)}, u32[]{:S(2)}) collective-permute-start(bf16[4,128,128]{2,1,0:T(8,128)(2,1)S(1)} %get-tuple-element.31), channel_id=1, source_target_pairs={{0,2},{2,4},{4,6},{1,3},{3,5},{5,7},{8,10},{10,12},{12,14},{9,11},... | collective-permute-start | bytes 393224 | tf_op jit(solution)/shard_map/ppermute | solution.py:420
  34.7 1.3 %collective-permute-start.4 = (bf16[4,128,128]{2,1,0:T(8,128)(2,1)S(1)}, bf16[4,128,128]{2,1,0:T(8,128)(2,1)S(1)}, u32[]{:S(2)}, u32[]{:S(2)}) collective-permute-start(bf16[4,128,128]{2,1,0:T(8,128)(2,1)S(1)} %get-tuple-element.32), channel_id=1, source_target_pairs={{2,0},{4,2},{6,4},{3,1},{5,3},{7,5},{10,8},{12,10},{14,12},{11,9},... | collective-permute-start | bytes 393224 | tf_op jit(solution)/shard_map/ppermute | solution.py:421
  36.0 1.3 %collective-permute-start.5 = (bf16[8,8,128]{2,1,0:T(8,128)(2,1)S(1)}, bf16[8,8,128]{2,1,0:T(8,128)(2,1)S(1)}, u32[]{:S(2)}, u32[]{:S(2)}) collective-permute-start(bf16[8,8,128]{2,1,0:T(8,128)(2,1)S(1)} %get-tuple-element.33), channel_id=1, source_target_pairs={{1,0},{9,8},{16,17},{24,25},{3,2},{11,10},{18,19},{26,27},{5,4},{1... | collective-permute-start | bytes 49160 | tf_op jit(solution)/shard_map/ppermute | solution.py:393
  37.3 5.2 %all-gather.1 = f32[12,8,128]{2,1,0:T(8,128)S(1)} all-gather(f32[3,8,128]{2,1,0:T(8,128)S(1)} %get-tuple-element.30), channel_id=3, replica_groups=mesh['vel'=4,'gx'=4,'gy'=2] {'vel'}, dimensions={0}, use_global_device_ids=true | all-gather | bytes 61440 | tf_op jit(solution)/shard_map/all_gather | solution.py:423
  42.5 0.0 collective-permute-done.5.yrecv
  42.5 0.0 collective-permute-done.3.from_left
  42.5 0.0 collective-permute-done.4.from_right
  42.5 2.9 %shard_map.66 = (f32[8,9,136,128]{3,2,1,0:T(8,128)S(1)}, bf16[4,128,128]{2,1,0:T(8,128)(2,1)S(1)}, bf16[4,128,128]{2,1,0:T(8,128)(2,1)S(1)}, bf16[8,8,128]{2,1,0:T(8,128)(2,1)S(1)}, f32[3,8,128]{2,1,0:T(8,128)S(1)}) custom-call(s32[5]{0:T(128)S(1)} %stack.39.info, s32[2,8]{1,0:T(2,128)S(1)} %copy-done, ...), custom_call_target="tpu_custom_call", output_to_operand_aliasing={{0}: (11, {})} | custom-call | tf_op jit(solution)/shard_map/pallas_call | solution.py:362
  45.4 4.6 %collective-permute-start.6 = (bf16[4,128,128]{2,1,0:T(8,128)(2,1)S(1)}, bf16[4,128,128]{2,1,0:T(8,128)(2,1)S(1)}, u32[]{:S(2)}, u32[]{:S(2)}) collective-permute-start(bf16[4,128,128]{2,1,0:T(8,128)(2,1)S(1)} %get-tuple-element.41), channel_id=1, source_target_pairs={{0,2},{2,4},{4,6},{1,3},{3,5},{5,7},{8,10},{10,12},{12,14},{9,11},... | collective-permute-start | bytes 393224 | tf_op jit(solution)/shard_map/ppermute | solution.py:420
  50.0 1.3 %collective-permute-start.7 = (bf16[4,128,128]{2,1,0:T(8,128)(2,1)S(1)}, bf16[4,128,128]{2,1,0:T(8,128)(2,1)S(1)}, u32[]{:S(2)}, u32[]{:S(2)}) collective-permute-start(bf16[4,128,128]{2,1,0:T(8,128)(2,1)S(1)} %get-tuple-element.42), channel_id=1, source_target_pairs={{2,0},{4,2},{6,4},{3,1},{5,3},{7,5},{10,8},{12,10},{14,12},{11,9},... | collective-permute-start | bytes 393224 | tf_op jit(solution)/shard_map/ppermute | solution.py:421
  51.3 1.3 %collective-permute-start.8 = (bf16[8,8,128]{2,1,0:T(8,128)(2,1)S(1)}, bf16[8,8,128]{2,1,0:T(8,128)(2,1)S(1)}, u32[]{:S(2)}, u32[]{:S(2)}) collective-permute-start(bf16[8,8,128]{2,1,0:T(8,128)(2,1)S(1)} %get-tuple-element.43), channel_id=1, source_target_pairs={{1,0},{9,8},{16,17},{24,25},{3,2},{11,10},{18,19},{26,27},{5,4},{1... | collective-permute-start | bytes 49160 | tf_op jit(solution)/shard_map/ppermute | solution.py:393
  52.6 6.5 %all-gather.2 = f32[12,8,128]{2,1,0:T(8,128)S(1)} all-gather(f32[3,8,128]{2,1,0:T(8,128)S(1)} %get-tuple-element.40), channel_id=4, replica_groups=mesh['vel'=4,'gx'=4,'gy'=2] {'vel'}, dimensions={0}, use_global_device_ids=true | all-gather | bytes 61440 | tf_op jit(solution)/shard_map/all_gather | solution.py:423
  59.1 0.0 collective-permute-done.8.yrecv
  59.1 0.0 collective-permute-done.6.from_left
  59.1 0.0 collective-permute-done.7.from_right
  59.1 2.9 %shard_map.67 = (f32[8,9,136,128]{3,2,1,0:T(8,128)S(1)}, bf16[4,128,128]{2,1,0:T(8,128)(2,1)S(1)}, bf16[4,128,128]{2,1,0:T(8,128)(2,1)S(1)}, bf16[8,8,128]{2,1,0:T(8,128)(2,1)S(1)}, f32[3,8,128]{2,1,0:T(8,128)S(1)}) custom-call(s32[5]{0:T(128)S(1)} %stack.39.info, s32[2,8]{1,0:T(2,128)S(1)} %copy-done, ...), custom_call_target="tpu_custom_call", output_to_operand_aliasing={{0}: (11, {})} | custom-call | tf_op jit(solution)/shard_map/pallas_call | solution.py:362
  62.0 4.6 %collective-permute-start.9 = (bf16[4,128,128]{2,1,0:T(8,128)(2,1)S(1)}, bf16[4,128,128]{2,1,0:T(8,128)(2,1)S(1)}, u32[]{:S(2)}, u32[]{:S(2)}) collective-permute-start(bf16[4,128,128]{2,1,0:T(8,128)(2,1)S(1)} %get-tuple-element.46), channel_id=1, source_target_pairs={{0,2},{2,4},{4,6},{1,3},{3,5},{5,7},{8,10},{10,12},{12,14},{9,11},... | collective-permute-start | bytes 393224 | tf_op jit(solution)/shard_map/ppermute | solution.py:420
  66.6 1.3 %collective-permute-start.10 = (bf16[4,128,128]{2,1,0:T(8,128)(2,1)S(1)}, bf16[4,128,128]{2,1,0:T(8,128)(2,1)S(1)}, u32[]{:S(2)}, u32[]{:S(2)}) collective-permute-start(bf16[4,128,128]{2,1,0:T(8,128)(2,1)S(1)} %get-tuple-element.47), channel_id=1, source_target_pairs={{2,0},{4,2},{6,4},{3,1},{5,3},{7,5},{10,8},{12,10},{14,12},{11,9},... | collective-permute-start | bytes 393224 | tf_op jit(solution)/shard_map/ppermute | solution.py:421
  67.9 1.3 %collective-permute-start.11 = (bf16[8,8,128]{2,1,0:T(8,128)(2,1)S(1)}, bf16[8,8,128]{2,1,0:T(8,128)(2,1)S(1)}, u32[]{:S(2)}, u32[]{:S(2)}) collective-permute-start(bf16[8,8,128]{2,1,0:T(8,128)(2,1)S(1)} %get-tuple-element.48), channel_id=1, source_target_pairs={{1,0},{9,8},{16,17},{24,25},{3,2},{11,10},{18,19},{26,27},{5,4},{1... | collective-permute-start | bytes 49160 | tf_op jit(solution)/shard_map/ppermute | solution.py:393
  69.2 5.2 %all-gather.3 = f32[12,8,128]{2,1,0:T(8,128)S(1)} all-gather(f32[3,8,128]{2,1,0:T(8,128)S(1)} %get-tuple-element.45), channel_id=5, replica_groups=mesh['vel'=4,'gx'=4,'gy'=2] {'vel'}, dimensions={0}, use_global_device_ids=true | all-gather | bytes 61440 | tf_op jit(solution)/shard_map/all_gather | solution.py:423
  74.4 0.0 collective-permute-done.11.yrecv
  74.4 0.0 collective-permute-done.9.from_left
  74.4 0.0 collective-permute-done.10.from_right
  74.4 4.7 %shard_map.68 = (bf16[8,2,512,128]{3,2,1,0:T(8,128)(2,1)S(1)}, f32[8,9,136,128]{3,2,1,0:T(8,128)S(1)}) custom-call(s32[5]{0:T(128)S(1)} %stack.39.info, s32[2,8]{1,0:T(2,128)S(1)} %copy-done, f32[4,3,8,128]{3,2,1,0:T(8,128)S(1)} %bitcast.33, bf16[4,128,128]{2,1,0:T(8,128)(2,1)S(1)} %collective-permute-done.9.from_left, ...), custom_call_target="tpu_custom_call", output_to_operand_aliasing={{1}: (11, {})} | custom-call | tf_op jit(solution)/shard_map/pallas_call | solution.py:362
  79.1 3.8 %copy.17 = bf16[16,2,32,8,128]{4,3,2,1,0:T(8,128)(2,1)} copy(bf16[16,2,32,8,128]{4,2,0,1,3:T(8,128)(2,1)S(1)} %bitcast.31) | data formatting | bytes 4194304 | tf_op jit(solution)/shard_map/transpose | solution.py:432
  (4 shorter events, 0.0 us)
Async XLA Ops:
  0.0 12.8 %copy-start.4 = (bf16[1024,2,8]{0,2,1:T(8,128)(2,1)S(1)}, bf16[1024,2,8]{0,2,1:T(8,128)(2,1)}, u32[]{:S(2)}) copy-start(bf16[1024,2,8]{0,2,1:T(8,128)(2,1)} %param.11) | copy-start | bytes 98308
  0.0 20.8 %copy-start.3 = (bf16[1024,2,128]{2,1,0:T(2,128)(2,1)S(1)}, bf16[1024,2,128]{2,1,0:T(2,128)(2,1)}, u32[]{:S(2)}) copy-start(bf16[1024,2,128]{2,1,0:T(2,128)(2,1)} %param.10) | copy-start | bytes 1572868
  0.0 20.9 %copy-start = (s32[2,8]{1,0:T(2,128)S(1)}, s32[2,8]{1,0:T(2,128)}, u32[]{:S(2)}) copy-start(s32[2,8]{1,0:T(2,128)} %kindy.7) | copy-start | bytes 196
  0.0 20.9 %copy-start.1 = (f32[8,128]{1,0:T(8,128)S(1)}, f32[8,128]{1,0:T(8,128)}, u32[]{:S(2)}) copy-start(f32[8,128]{1,0:T(8,128)} %relax.1) | copy-start | bytes 12292
  0.0 20.9 %copy-start.2 = (s32[2,128]{1,0:T(2,128)S(1)}, s32[2,128]{1,0:T(2,128)}, u32[]{:S(2)}) copy-start(s32[2,128]{1,0:T(2,128)} %kindx.1) | copy-start | bytes 3076
  3.9 17.0 %collective-permute-start.2 = (bf16[2,8,512]{2,1,0:T(8,128)(2,1)S(1)}, bf16[2,8,512]{2,1,0:T(8,128)(2,1)S(1)}, u32[]{:S(2)}, u32[]{:S(2)}) collective-permute-start(bf16[2,8,512]{2,1,0:T(8,128)(2,1)S(1)} %get-tuple-element.29), channel_id=1, source_target_pairs={{1,0},{9,8},{16,17},{24,25},{3,2},{11,10},{18,19},{26,27},{5,4},{1... | collective-permute-start | bytes 49160 | tf_op jit(solution)/shard_map/ppermute | solution.py:393
  5.9 14.9 %collective-permute-start.1 = (bf16[512,128]{1,0:T(8,128)(2,1)}, bf16[512,128]{1,0:T(8,128)(2,1)S(1)}, u32[]{:S(2)}, u32[]{:S(2)}) collective-permute-start(bf16[512,128]{1,0:T(8,128)(2,1)} %get-tuple-element.51), channel_id=1, source_target_pairs={{2,0},{4,2},{6,4},{3,1},{5,3},{7,5},{10,8},{12,10},{14,12},{11,9},... | collective-permute-start | bytes 393224 | tf_op jit(solution)/shard_map/ppermute | solution.py:398
  7.2 13.7 %collective-permute-start = (bf16[512,128]{1,0:T(8,128)(2,1)}, bf16[512,128]{1,0:T(8,128)(2,1)S(1)}, u32[]{:S(2)}, u32[]{:S(2)}) collective-permute-start(bf16[512,128]{1,0:T(8,128)(2,1)} %get-tuple-element.52), channel_id=1, source_target_pairs={{0,2},{2,4},{4,6},{1,3},{3,5},{5,7},{8,10},{10,12},{12,14},{9,11},... | collective-permute-start | bytes 393224 | tf_op jit(solution)/shard_map/ppermute | solution.py:397
  31.2 11.3 %collective-permute-start.3 = (bf16[4,128,128]{2,1,0:T(8,128)(2,1)S(1)}, bf16[4,128,128]{2,1,0:T(8,128)(2,1)S(1)}, u32[]{:S(2)}, u32[]{:S(2)}) collective-permute-start(bf16[4,128,128]{2,1,0:T(8,128)(2,1)S(1)} %get-tuple-element.31), channel_id=1, source_target_pairs={{0,2},{2,4},{4,6},{1,3},{3,5},{5,7},{8,10},{10,12},{12,14},{9,11},... | collective-permute-start | bytes 393224 | tf_op jit(solution)/shard_map/ppermute | solution.py:420
  34.7 7.8 %collective-permute-start.4 = (bf16[4,128,128]{2,1,0:T(8,128)(2,1)S(1)}, bf16[4,128,128]{2,1,0:T(8,128)(2,1)S(1)}, u32[]{:S(2)}, u32[]{:S(2)}) collective-permute-start(bf16[4,128,128]{2,1,0:T(8,128)(2,1)S(1)} %get-tuple-element.32), channel_id=1, source_target_pairs={{2,0},{4,2},{6,4},{3,1},{5,3},{7,5},{10,8},{12,10},{14,12},{11,9},... | collective-permute-start | bytes 393224 | tf_op jit(solution)/shard_map/ppermute | solution.py:421
  36.0 6.5 %collective-permute-start.5 = (bf16[8,8,128]{2,1,0:T(8,128)(2,1)S(1)}, bf16[8,8,128]{2,1,0:T(8,128)(2,1)S(1)}, u32[]{:S(2)}, u32[]{:S(2)}) collective-permute-start(bf16[8,8,128]{2,1,0:T(8,128)(2,1)S(1)} %get-tuple-element.33), channel_id=1, source_target_pairs={{1,0},{9,8},{16,17},{24,25},{3,2},{11,10},{18,19},{26,27},{5,4},{1... | collective-permute-start | bytes 49160 | tf_op jit(solution)/shard_map/ppermute | solution.py:393
  45.4 13.7 %collective-permute-start.6 = (bf16[4,128,128]{2,1,0:T(8,128)(2,1)S(1)}, bf16[4,128,128]{2,1,0:T(8,128)(2,1)S(1)}, u32[]{:S(2)}, u32[]{:S(2)}) collective-permute-start(bf16[4,128,128]{2,1,0:T(8,128)(2,1)S(1)} %get-tuple-element.41), channel_id=1, source_target_pairs={{0,2},{2,4},{4,6},{1,3},{3,5},{5,7},{8,10},{10,12},{12,14},{9,11},... | collective-permute-start | bytes 393224 | tf_op jit(solution)/shard_map/ppermute | solution.py:420
  50.0 9.2 %collective-permute-start.7 = (bf16[4,128,128]{2,1,0:T(8,128)(2,1)S(1)}, bf16[4,128,128]{2,1,0:T(8,128)(2,1)S(1)}, u32[]{:S(2)}, u32[]{:S(2)}) collective-permute-start(bf16[4,128,128]{2,1,0:T(8,128)(2,1)S(1)} %get-tuple-element.42), channel_id=1, source_target_pairs={{2,0},{4,2},{6,4},{3,1},{5,3},{7,5},{10,8},{12,10},{14,12},{11,9},... | collective-permute-start | bytes 393224 | tf_op jit(solution)/shard_map/ppermute | solution.py:421
  51.3 7.8 %collective-permute-start.8 = (bf16[8,8,128]{2,1,0:T(8,128)(2,1)S(1)}, bf16[8,8,128]{2,1,0:T(8,128)(2,1)S(1)}, u32[]{:S(2)}, u32[]{:S(2)}) collective-permute-start(bf16[8,8,128]{2,1,0:T(8,128)(2,1)S(1)} %get-tuple-element.43), channel_id=1, source_target_pairs={{1,0},{9,8},{16,17},{24,25},{3,2},{11,10},{18,19},{26,27},{5,4},{1... | collective-permute-start | bytes 49160 | tf_op jit(solution)/shard_map/ppermute | solution.py:393
  62.0 12.4 %collective-permute-start.9 = (bf16[4,128,128]{2,1,0:T(8,128)(2,1)S(1)}, bf16[4,128,128]{2,1,0:T(8,128)(2,1)S(1)}, u32[]{:S(2)}, u32[]{:S(2)}) collective-permute-start(bf16[4,128,128]{2,1,0:T(8,128)(2,1)S(1)} %get-tuple-element.46), channel_id=1, source_target_pairs={{0,2},{2,4},{4,6},{1,3},{3,5},{5,7},{8,10},{10,12},{12,14},{9,11},... | collective-permute-start | bytes 393224 | tf_op jit(solution)/shard_map/ppermute | solution.py:420
  66.6 7.8 %collective-permute-start.10 = (bf16[4,128,128]{2,1,0:T(8,128)(2,1)S(1)}, bf16[4,128,128]{2,1,0:T(8,128)(2,1)S(1)}, u32[]{:S(2)}, u32[]{:S(2)}) collective-permute-start(bf16[4,128,128]{2,1,0:T(8,128)(2,1)S(1)} %get-tuple-element.47), channel_id=1, source_target_pairs={{2,0},{4,2},{6,4},{3,1},{5,3},{7,5},{10,8},{12,10},{14,12},{11,9},... | collective-permute-start | bytes 393224 | tf_op jit(solution)/shard_map/ppermute | solution.py:421
  67.9 6.5 %collective-permute-start.11 = (bf16[8,8,128]{2,1,0:T(8,128)(2,1)S(1)}, bf16[8,8,128]{2,1,0:T(8,128)(2,1)S(1)}, u32[]{:S(2)}, u32[]{:S(2)}) collective-permute-start(bf16[8,8,128]{2,1,0:T(8,128)(2,1)S(1)} %get-tuple-element.48), channel_id=1, source_target_pairs={{1,0},{9,8},{16,17},{24,25},{3,2},{11,10},{18,19},{26,27},{5,4},{1... | collective-permute-start | bytes 49160 | tf_op jit(solution)/shard_map/ppermute | solution.py:393
where the time goes:
time: 84.5 us; the launch traced here: 82.8 us
  starting transfers between devices  28.6 us (34%)
  blocking collectives  24.5 us (29%)
  Pallas kernels  22.4 us (27%)
  local copies, waits for them, and re-layouts  7.05 us (8%)
    pallas_call x5, Pallas kernels, call(): pl.pallas_call(kernel, out_shape=outs, in_specs=[smem] * n_smem + [vmem]...  22.4 us
    all_gather x3, blocking collectives, body(): ag = lax.all_gather(flux, 'vel')  17 us
    ppermute x3, starting transfers between devices, body(): from_left = lax.ppermute(xmsg1, 'gx', right)  12.6 us
    all_gather x1, blocking collectives, body(): ag = lax.all_gather(pay, 'vel')  7.51 us
    ppermute x1, starting transfers between devices, body(): from_left = lax.ppermute(pt[cells_x - 1, 1], 'gx', right)  5.6 us
    ppermute x4, starting transfers between devices, shift_y(): return lax.ppermute(a, ('vel', 'gy'), along)  5.19 us
    ppermute x3, starting transfers between devices, body(): from_right = lax.ppermute(xmsg0, 'gx', left)  3.88 us
    transpose x1, local copies, waits for them, and re-layouts, body(): out.reshape(cells_x, 2, local_ky, HALF, cells_y).transpose(2, 1, 3, 0, 4)  3.75 us
  transfers between devices with their start and end apart: 12, of which 0 were waited for; matrix products, arithmetic and copies ran while one was open for 1% of the time, Pallas kernels for 0%

commit v1 on v0

--- a/solution.py
+++ b/solution.py
@@ -72,8 +72,19 @@
     return [high, middle, rest - middle]
 
 
-def moments_kernel(info, pt, pay, ymsg):
+def moments_kernel(info, prev, pay, ymsg, pt, xmsg0, xmsg1, rows):
     cells_x, _, count, cells_y = pt.shape
+    span = HALF * cells_x
+    for sign in range(2):
+        for at in range(count // LANES):
+            for i in range(LANES // HALF):
+                start = ((at * (LANES // HALF) + i) * NVX + sign * HALF) * cells_x
+                rows[i * span : (i + 1) * span, :] = prev[start : start + span, :].astype(F32)
+            for x in range(cells_x):
+                pt[x, sign, at * LANES : (at + 1) * LANES, :] = rows[pl.ds(x, LANES, stride=cells_x), :].astype(BF16)
+    even = info[5]
+    xmsg0[...] = pt[(cells_x - 1) * even, even]
+    xmsg1[...] = pt[(cells_x - 1) * (1 - even), 1 - even]
     first_ky, up = info[0], info[1] == 1
     y_out = jnp.where(up, cells_y - 1, 0)
     row = iota((16, count), 0)
@@ -168,18 +179,13 @@
     return jnp.abs(ix).astype(F32) * UNIT, jnp.abs(iy).astype(F32) * UNIT
 
 
-def fill_inflow(info, kindy, flux, g, xin, yin, xw, yw, kx):
+def fill_inflow(info, kindy, same, other, g, xin, yin, xw, yw, kx):
     blocks, slots, padded, _ = g.shape
     cells_x, cells_y = slots - 1, padded - 8
     per_sign = blocks // 2
     first_ky, up = info[0], info[1] == 1
-    devices = flux.shape[0]
-    lo = [sum(flux[d, at] for d in range(devices // 2)) for at in range(3)]
-    hi = [sum(flux[d, at] for d in range(devices // 2, devices)) for at in range(3)]
-    same = jnp.where(up, hi[0], lo[0])
-    other = [jnp.where(up, a, b) for a, b in zip(lo, hi)]
     anti = flip_matrix(False, cells_y)
-    fx = (same + nn(other[0], anti, HIGHEST)) * FLUX_SCALE
+    fx = (same[0] + nn(other[0], anti, HIGHEST)) * FLUX_SCALE
     fy = jnp.sum(other[1], axis=1, keepdims=True) + reverse_rows(jnp.sum(other[2], axis=1, keepdims=True))
     fy = fy * FLUX_SCALE
     fy = [reverse_rows(fy), fy]
@@ -238,11 +244,13 @@
             ix, iy = lane_ints(info[0], sign, at * LANES, (8, LANES))
             ix, iy = jnp.abs(ix).astype(F32), jnp.abs(iy).astype(F32)
             row = g[block, cells_x, 8:, :]
-            xmsg[sign][at] = row.astype(BF16)
             total += row * ix[0:1]
             edge = jnp.concatenate([g[block, 1 + x, padded - 1 : padded, :] for x in range(cells_x)], axis=0)
             ymsg[block] = edge.astype(BF16)
             total_y += edge * iy
+        for at in range(per_sign):
+            take = sign * (1 - info[5]) + (1 - sign) * info[5]
+            xmsg[sign][at] = g[take * per_sign + at, cells_x, 8:, :].astype(BF16)
         pick = (iota((8, LANES), 0) == sign).astype(F32)
         part = nt(pick, total, HIGHEST)
         fx = part if fx is None else fx + part
@@ -250,25 +258,35 @@
     flux[0] = fx
 
 
-def first_kernel(info, kindy, ag, relax, kindx, pt, from_left, from_right, yrecv, lri, bti,
-                 g, s, r, xw, yw, kx, xmsg0, xmsg1, ymsg, flux, ps):
+def first_kernel(info, kindy, same, other, relax, kindx, pt, pair0, pair1, yrecv, lri, bti,
+                 g, s, r, xw, yw, kx, xmsg0, xmsg1, ymsg, flux, ta, tb, tr, fa, fb):
     cells_x, _, count, cells_y = pt.shape
     per_sign = count // LANES
     blocks = 2 * per_sign
     first_ky, up = info[0], info[1] == 1
-    total = [sum(ag[d, q] for d in range(ag.shape[0])) for q in range(4)]
+    total = [same[q] + other[q] for q in range(4)]
     tau = relax[...]
     p = newton_params(total[0] * WEIGHT, total[1] * (WEIGHT * UNIT), total[2] * (WEIGHT * UNIT),
                       total[3] * (WEIGHT * UNIT * UNIT / 2.0))
     lead = p[0] - jnp.log(tau)
-    rows = pieces(lead) + pieces(p[1] * UNIT) + pieces(p[2] * UNIT) + pieces(p[3] * (UNIT * UNIT / 2.0))
-    rows += pieces(1.0 / TIME_STEP + 1.0 / tau)
     flip = flip_matrix(up, cells_y).astype(BF16)
-    for at, piece in enumerate(rows):
-        for x in range(cells_x):
-            ps[x, at : at + 1, :] = piece[x : x + 1]
+    local_ky = count // HALF
+    vx = (2 * iota((NVX, cells_y), 0) - (NVX - 1)).astype(F32) * UNIT
+    vy = (2 * (first_ky + iota((local_ky, cells_y), 0)) - (NVX - 1)).astype(F32) * UNIT
+    steps = iota((NVX, cells_y), 0).astype(F32) * STEP
+    half_p3 = p[3] * 0.5
+    base = 1.0 / TIME_STEP + 1.0 / tau
     for x in range(cells_x):
-        ps[x, 15:16, :] = jnp.zeros((1, cells_y), F32)
+        here = slice(x, x + 1)
+        arg = vy * (p[2][here] + vy * half_p3[here])
+        top = jnp.max(arg, axis=0, keepdims=True)
+        along_y = jnp.exp(arg - top)
+        along_x = jnp.exp((lead[here] + top) + vx * (p[1][here] + vx * half_p3[here]))
+        inverse = 1.0 / (base[here] + steps)
+        for table, ref in ((along_x, ta), (along_y, tb), (inverse, tr)):
+            wide = nt(flip, jnp.concatenate(pieces(table), axis=0).astype(BF16)).astype(BF16)
+            ref[1, x * cells_y : (x + 1) * cells_y, :] = wide
+            ref[0, (cells_x - 1 - x) * cells_y : (cells_x - x) * cells_y, :] = wide
     kind = jnp.concatenate([kindx[1:2], kindx[0:1], jnp.zeros((6, cells_y), jnp.int32)], axis=0).astype(F32)
     kind = nt(kind.astype(BF16), flip).astype(BF16)
     for sign in range(2):
@@ -283,61 +301,55 @@
             row, col = iota((16, cells_x), 0), iota((16, cells_x), 1)
             order = (col == (row if sign else cells_x - 1 - row)).astype(F32).astype(BF16)
             yw[block] = nt(order, part)[:cells_x]
-    row = iota((16, LANES), 0)
-
-    def build(xt, carry):
-        for sign in range(2):
-            x = xt if sign else cells_x - 1 - xt
-            mine = nt(ps[x].astype(BF16), flip)
-            table = mine.astype(BF16)
-            base = tn(table, ((row >= 12) & (row < 15)).astype(F32).astype(BF16))
-            for at in range(per_sign):
-                block = sign * per_sign + at
-                ix, iy = lane_ints(first_ky, sign, at * LANES, (16, LANES))
-                energy = ix * ix + iy * iy
-                basis = jnp.where(row < 3, 1, jnp.where(row < 6, ix, jnp.where(row < 9, iy, jnp.where(row < 12, energy - energy % 64, 0))))
-                basis2 = jnp.where((row >= 9) & (row < 12), energy % 64, 0)
-                basis = jnp.concatenate([basis, basis2], axis=0).astype(F32).astype(BF16)
-                arg = tn(jnp.concatenate([table, table], axis=0), basis)
+    def spread(ref, sign, choice, size):
+        row = iota((3 * size, LANES), 0) % size
+        return nn(ref[sign], (row == choice).astype(F32).astype(BF16))
+
+    for sign in range(2):
+        fa[...] = spread(ta, sign, iota((1, LANES), 1) % HALF + HALF * sign, NVX)
+        for at in range(per_sign):
+            block = sign * per_sign + at
+            ix, iy = lane_ints(first_ky, sign, at * LANES, (1, LANES))
+            r[block] = spread(tr, sign, (jnp.abs(ix) + jnp.abs(iy)) // 2, NVX).reshape(cells_x, cells_y, LANES)
+            fb[...] = spread(tb, sign, iota((1, LANES), 1) // HALF + at * (LANES // HALF), local_ky)
+            for xt in range(cells_x):
+                x = xt if sign else cells_x - 1 - xt
+                here = slice(xt * cells_y, (xt + 1) * cells_y)
                 value = nt(flip, pt[x, sign, at * LANES : (at + 1) * LANES, :])
                 g[block, 1 + xt, 8:, :] = value
-                s[block, xt] = value * (1.0 / TIME_STEP) + jnp.exp(arg)
-                ax, ay = block_speeds(first_ky, block, per_sign, (8, LANES))
-                r[block, xt] = 1.0 / (base + (ax + ay)[0:1])
-        return carry
-
-    lax.fori_loop(0, cells_x, build, 0)
+                s[block, xt] = value * (1.0 / TIME_STEP) + fa[here, :] * fb[here, :]
 
     def xin(block):
-        source = from_left if block >= per_sign else from_right
         at = block % per_sign
-        return nt(flip, source[at * LANES : (at + 1) * LANES, :])
+        first = (info[5] == 1) == (block < per_sign)
+        here = slice(at * LANES, (at + 1) * LANES)
+        return nt(flip, jnp.where(first, pair0[here, :], pair1[here, :]))
 
     def yin(block):
         at = block % per_sign
         return yrecv[block // per_sign, :, at * LANES : (at + 1) * LANES].astype(F32)
 
-    fill_inflow(info, kindy, ag.at[:, 4:7], g, xin, yin, xw, yw, kx)
+    fill_inflow(info, kindy, same.at[4:7], other.at[4:7], g, xin, yin, xw, yw, kx)
     sweep(info, g, s, r)
     send_out(info, g, (xmsg0, xmsg1), ymsg, flux)
 
 
-def next_kernel(last, info, kindy, ag, from_left, from_right, yrecv, xw, yw, kx, s, r, g_in, *outs):
+def next_kernel(last, info, kindy, same, other, pair0, pair1, yrecv, xw, yw, kx, s, r, g_in, *outs):
     blocks, slots, padded, _ = g_in.shape
     per_sign = blocks // 2
     if last:
-        out, g = outs
+        out, g, rows = outs
     else:
         g, xmsg0, xmsg1, ymsg, flux = outs
 
     def xin(block):
-        source = from_left if block >= per_sign else from_right
-        return source[block % per_sign].astype(F32)
+        first = (info[5] == 1) == (block < per_sign)
+        return jnp.where(first, pair0[block % per_sign].astype(F32), pair1[block % per_sign].astype(F32))
 
     def yin(block):
         return yrecv[block].astype(F32)
 
-    fill_inflow(info, kindy, ag, g, xin, yin, xw, yw, kx)
+    fill_inflow(info, kindy, same, other, g, xin, yin, xw, yw, kx)
     sweep(info, g, s, r)
     if not last:
         send_out(info, g, (xmsg0, xmsg1), ymsg, flux)
@@ -345,15 +357,16 @@
     cells_x, cells_y = slots - 1, padded - 8
     flip = flip_matrix(info[1] == 1, cells_y).astype(BF16)
 
-    def emit(xt, carry):
-        for sign in range(2):
-            x = xt if sign else cells_x - 1 - xt
-            for at in range(per_sign):
+    span = HALF * cells_x
+    for sign in range(2):
+        for at in range(per_sign):
+            for x in range(cells_x):
+                xt = x if sign else cells_x - 1 - x
                 value = g[sign * per_sign + at, 1 + xt, 8:, :].astype(BF16)
-                out[x, sign, at * LANES : (at + 1) * LANES, :] = tn(value, flip).astype(BF16)
-        return carry
-
-    lax.fori_loop(0, cells_x, emit, 0)
+                rows[pl.ds(x, LANES, stride=cells_x), :] = tn(value, flip)
+            for i in range(LANES // HALF):
+                start = ((at * (LANES // HALF) + i) * NVX + sign * HALF) * cells_x
+                out[start : start + span, :] = rows[i * span : (i + 1) * span, :].astype(BF16)
 
 
 def call(kernel, outs, n_smem, ins, scratch=(), aliases=None, mib=20):
@@ -381,28 +394,35 @@
     up = v >= nvel // 2
     y_wall = jnp.where(up, iy == 0, iy == ngy - 1)
     info = jnp.stack([v * local_ky, up.astype(jnp.int32), (ix == 0).astype(jnp.int32),
-                      (ix == ngx - 1).astype(jnp.int32), y_wall.astype(jnp.int32)])
-    right = [(i, i + 1) for i in range(ngx - 1)]
-    left = [(i + 1, i) for i in range(ngx - 1)]
-    along = []
-    for d in range(nvel):
-        for j in range(ngy - 1):
-            along.append((d * ngy + j, d * ngy + j + 1) if d >= nvel // 2 else (d * ngy + j + 1, d * ngy + j))
-
-    def shift_y(a):
-        return lax.ppermute(a, ("vel", "gy"), along)
-
-    pt = previous.reshape(local_ky, 2, HALF, cells_x, cells_y).transpose(3, 1, 0, 2, 4)
-    pt = pt.reshape(cells_x, 2, count, cells_y)
-    from_left = lax.ppermute(pt[cells_x - 1, 1], "gx", right)
-    from_right = lax.ppermute(pt[0, 0], "gx", left)
+                      (ix == ngx - 1).astype(jnp.int32), y_wall.astype(jnp.int32), (ix % 2 == 0).astype(jnp.int32)])
+    def pairs(count, start):
+        low = range(start, count - 1, 2)
+        return [(i, i + 1) for i in low] + [(i + 1, i) for i in low]
+
+    def swap_x(first, second):
+        return lax.ppermute(first, "gx", pairs(ngx, 0)), lax.ppermute(second, "gx", pairs(ngx, 1))
+
+    def swap_y(a):
+        return lax.ppermute(a, "gy", pairs(ngy, 0))
+
+    def sum_vel(a):
+        reach = 1
+        while reach < nvel // 2:
+            a = a + lax.ppermute(a, "vel", [(i, i ^ reach) for i in range(nvel)])
+            reach *= 2
+        return a, lax.ppermute(a, "vel", [(i, i ^ reach) for i in range(nvel)])
+
+    assert ngy == 2 and nvel & (nvel - 1) == 0, "mesh shape"
     sds = jax.ShapeDtypeStruct
-    pay, ymsg = call(
+    pay, ymsg, pt, xmsg0, xmsg1 = call(
         moments_kernel,
-        (sds((7, 8, LANES), F32), sds((2, cells_x, count), BF16)),
-        1, (info, pt), mib=16)
-    yrecv = shift_y(ymsg)
-    ag = lax.all_gather(pay, "vel")
+        (sds((7, 8, LANES), F32), sds((2, cells_x, count), BF16), sds((cells_x, 2, count, cells_y), BF16),
+         sds((count, cells_y), BF16), sds((count, cells_y), BF16)),
+        1, (info, previous.reshape(vel_rows * cells_x, cells_y)),
+        scratch=[pltpu.VMEM((LANES * cells_x, cells_y), F32)], mib=8)
+    halo = swap_x(xmsg0, xmsg1)
+    yrecv = swap_y(ymsg)
+    sums = sum_vel(pay)
     lri = left_right_inflow.reshape(vel_rows, 2 * cells_y)
     bti = jnp.where(up, bottom_top_inflow[:, 0, :], bottom_top_inflow[:, 1, :])
     g_shape = sds((blocks, cells_x + 1, cells_y + 8, LANES), F32)
@@ -414,22 +434,24 @@
         (g_shape, full, full, sds((blocks, cells_y, LANES), F32), sds((blocks, cells_x, LANES), F32),
          sds((2, cells_y, LANES), F32)) + messages,
         2,
-        (info, bottom_top_kind, ag, relax_time, left_right_kind, pt, from_left, from_right, yrecv, lri, bti),
-        scratch=[pltpu.VMEM((cells_x, 16, cells_y), F32)], mib=32)
+        (info, bottom_top_kind, *sums, relax_time, left_right_kind, pt, *halo, yrecv, lri, bti),
+        scratch=[
+            pltpu.VMEM((2, cells_x * cells_y, 3 * NVX), BF16), pltpu.VMEM((2, cells_x * cells_y, 3 * local_ky), BF16),
+            pltpu.VMEM((2, cells_x * cells_y, 3 * NVX), BF16), pltpu.VMEM((cells_x * cells_y, LANES), F32),
+            pltpu.VMEM((cells_x * cells_y, LANES), F32)], mib=24)
     for number in range(1, SWEEPS):
-        from_left = lax.ppermute(xmsg1, "gx", right)
-        from_right = lax.ppermute(xmsg0, "gx", left)
-        yrecv = shift_y(ymsg)
-        ag = lax.all_gather(flux, "vel")
+        halo = swap_x(xmsg0, xmsg1)
+        yrecv = swap_y(ymsg)
+        sums = sum_vel(flux)
         last = number == SWEEPS - 1
-        ins = (info, bottom_top_kind, ag, from_left, from_right, yrecv, xw, yw, kx, s, r, g)
+        ins = (info, bottom_top_kind, *sums, *halo, yrecv, xw, yw, kx, s, r, g)
         if last:
             out, _ = call(functools.partial(next_kernel, True),
-                          (sds((cells_x, 2, count, cells_y), BF16), g_shape), 2, ins, aliases={11: 1}, mib=32)
+                          (sds((vel_rows * cells_x, cells_y), BF16), g_shape), 2, ins, aliases={12: 1},
+                          scratch=[pltpu.VMEM((LANES * cells_x, cells_y), F32)], mib=22)
         else:
             g, xmsg0, xmsg1, ymsg, flux = call(
-                functools.partial(next_kernel, False), (g_shape,) + messages, 2, ins, aliases={11: 0}, mib=32)
-    out = out.reshape(cells_x, 2, local_ky, HALF, cells_y).transpose(2, 1, 3, 0, 4)
+                functools.partial(next_kernel, False), (g_shape,) + messages, 2, ins, aliases={12: 0}, mib=22)
     return out.reshape(vel_rows, cells_x, cells_y)
 
 

time: 84.5 us -> 60.1 us (0.71); the launches traced: 82.8 us -> 59.8 us
  blocking collectives: 24.5 us -> 0 us
  waiting for transfers between devices: 0.03 us -> 8.86 us
  starting transfers between devices: 28.6 us -> 25 us
  local copies, waits for them, and re-layouts: 7.05 us -> 3.9 us
    all_gather x4 -> x0, blocking collectives: 24.5 us -> none  [the longest x3 17 us: body(): ag = lax.all_gather(flux, 'vel')]
    ppermute x12 -> x20, waiting for transfers between devices: 0.03 us -> 8.86 us  [the longest x4 4.39 us: sum_vel(): return (a, lax.ppermute(a, 'vel', [(i, i ^ reach) for i in range(nvel)]))]
    transpose x1 -> x0, local copies, waits for them, and re-layouts: 3.75 us -> none  [body(): out.reshape(cells_x, 2, local_ky, HALF, cells_y).transpose(2, 1, 3, 0, 4)]
    ppermute x12 -> x20, starting transfers between devices: 28.6 us -> 25 us  [the longest x4 10.6 us: swap_x(): lax.ppermute(first, 'gx', pairs(ngx, 0))]
    unnamed x11 -> x9, local copies, waits for them, and re-layouts: 0.1 us -> 2.73 us
    reshape x1 -> x0, local copies, waits for them, and re-layouts: 2.05 us -> none  [body(): previous.reshape(local_ky, 2, HALF, cells_x, cells_y)]
  transfers between devices with their start and end apart: 12 -> 20, of which waited for: 0 -> 10; matrix products, arithmetic and copies ran while one was open for 1% -> 4% of each run, Pallas kernels for 0% -> 0%
where the time goes in v1:
time: 60.1 us; the launch traced here: 59.8 us
  starting transfers between devices  25 us (42%)
  Pallas kernels  21.8 us (36%)
  waiting for transfers between devices  8.86 us (15%)
  local copies, waits for them, and re-layouts  3.9 us (6%)
    pallas_call x5, Pallas kernels, call(): pl.pallas_call(kernel, out_shape=outs, in_specs=[smem] * n_smem + [vmem]...  21.8 us
    ppermute x4, starting transfers between devices, swap_x(): lax.ppermute(first, 'gx', pairs(ngx, 0))  10.6 us
    ppermute x4, starting transfers between devices, sum_vel(): return (a, lax.ppermute(a, 'vel', [(i, i ^ reach) for i in range(nvel)]))  5.99 us
    ppermute x4, starting transfers between devices, swap_y(): return lax.ppermute(a, 'gy', pairs(ngy, 0))  5.57 us
    ppermute x4, waiting for transfers between devices, sum_vel(): return (a, lax.ppermute(a, 'vel', [(i, i ^ reach) for i in range(nvel)]))  4.39 us
    ppermute x4, waiting for transfers between devices, swap_y(): return lax.ppermute(a, 'gy', pairs(ngy, 0))  3.47 us
    unnamed x9, local copies, waits for them, and re-layouts  2.73 us
    ppermute x4, starting transfers between devices, swap_x(): lax.ppermute(second, 'gx', pairs(ngx, 1))  2.63 us
  transfers between devices with their start and end apart: 20, of which 10 were waited for; matrix products, arithmetic and copies ran while one was open for 4% of the time, Pallas kernels for 0%

profile of v1, /device:TPU:0, one launch (start us, length us, event | category | flops | bytes accessed | tf_op | source)
XLA Modules:
  0.0 59.8 jit_solution(7659315258467875393)
XLA Ops:
  0.0 0.1 stack.47.info
  0.1 1.6 %copy-done = bf16[1024,8,128]{2,1,0:T(8,128)(2,1)S(1)} copy-done((bf16[1024,8,128]{2,1,0:T(8,128)(2,1)S(1)}, bf16[1024,8,128]{2,1,0:T(8,128)(2,1)}, u32[]{:S(2)}) %copy-start) | copy-done | bytes 2097176
  1.7 2.8 %shard_map.64 = (f32[7,8,128]{2,1,0:T(8,128)S(1)}, bf16[2,8,512]{2,1,0:T(8,128)(2,1)S(1)}, bf16[8,2,512,128]{3,2,1,0:T(8,128)(2,1)S(1)}, bf16[512,128]{1,0:T(8,128)(2,1)S(1)}, bf16[512,128]{1,0:T(8,128)(2,1)S(1)}) custom-call(s32[6]{0:T(128)S(1)} %stack.47.info, bf16[8192,128]{1,0:T(8,128)(2,1)S(1)} %bitcast.14), custom_call_target="tpu_custom_call" | custom-call | tf_op jit(solution)/shard_map/pallas_call | solution.py:375
  4.5 3.1 %collective-permute-start.4 = (bf16[2,8,512]{2,1,0:T(8,128)(2,1)S(1)}, bf16[2,8,512]{2,1,0:T(8,128)(2,1)S(1)}, u32[]{:S(2)}, u32[]{:S(2)}) collective-permute-start(bf16[2,8,512]{2,1,0:T(8,128)(2,1)S(1)} %get-tuple-element.35), channel_id=1, source_target_pairs={{0,1},{1,0},{2,3},{3,2},{4,5},{5,4},{6,7},{7,6},{8,9},{9,8},{10,11... | collective-permute-start | bytes 49160 | tf_op jit(solution)/shard_map/ppermute | solution.py:406
  7.5 0.0 collective-permute-start
  7.5 1.6 %collective-permute-start.2 = (bf16[512,128]{1,0:T(8,128)(2,1)S(1)}, bf16[512,128]{1,0:T(8,128)(2,1)S(1)}, u32[]{:S(2)}, u32[]{:S(2)}) collective-permute-start(bf16[512,128]{1,0:T(8,128)(2,1)S(1)} %get-tuple-element.33), channel_id=1, source_target_pairs={{0,2},{4,6},{2,0},{6,4},{1,3},{5,7},{3,1},{7,5},{8,10},{12,14},{10... | collective-permute-start | bytes 393224 | tf_op jit(solution)/shard_map/ppermute | solution.py:403
  9.1 0.7 %collective-permute-start.3 = (bf16[512,128]{1,0:T(8,128)(2,1)S(1)}, bf16[512,128]{1,0:T(8,128)(2,1)S(1)}, u32[]{:S(2)}, u32[]{:S(2)}) collective-permute-start(bf16[512,128]{1,0:T(8,128)(2,1)S(1)} %get-tuple-element.34), channel_id=1, source_target_pairs={{2,4},{4,2},{3,5},{5,3},{10,12},{12,10},{11,13},{13,11},{18,20},{2... | collective-permute-start | bytes 393224 | tf_op jit(solution)/shard_map/ppermute | solution.py:403
  9.8 0.7 %fusion = (bf16[1024,1,8]{0,2,1:T(8,128)(2,1)S(1)}, bf16[1024,1,8]{0,2,1:T(8,128)(2,1)S(1)}) fusion(bf16[1024,2,8]{0,2,1:T(8,128)(2,1)} %param.11), kind=kLoop, calls=%fused_computation.2 | loop fusion | bytes 65536 | tf_op jit(solution)/shard_map/slice | solution.py:427
  10.5 0.2 copy.11
  10.7 0.2 copy.10
  10.9 0.0 collective-permute-done
  10.9 1.6 %collective-permute-start.1 = (f32[7,8,128]{2,1,0:T(8,128)S(1)}, f32[7,8,128]{2,1,0:T(8,128)S(1)}, u32[]{:S(2)}, u32[]{:S(2)}) collective-permute-start(f32[7,8,128]{2,1,0:T(8,128)S(1)} %add.17.same), channel_id=1, source_target_pairs={{0,16},{8,24},{16,0},{24,8},{1,17},{9,25},{17,1},{25,9},{2,18},{10... | collective-permute-start | bytes 86024 | tf_op jit(solution)/shard_map/ppermute | solution.py:413
  12.5 1.1 %copy.14 = bf16[128,8,2,128]{3,1,2,0:T(8,128)(2,1)S(1)} copy(bf16[128,8,2,128]{3,2,1,0:T(2,128)(2,1)} %bitcast.16) | data formatting | bytes 1048576
  13.6 1.2 %collective-permute-done.1.other = f32[7,8,128]{2,1,0:T(8,128)S(1)} collective-permute-done((f32[7,8,128]{2,1,0:T(8,128)S(1)}, f32[7,8,128]{2,1,0:T(8,128)S(1)}, u32[]{:S(2)}, u32[]{:S(2)}) %collective-permute-start.1) | collective-permute-done | bytes 28704 | tf_op jit(solution)/shard_map/ppermute | solution.py:413
  14.8 0.0 collective-permute-done.2.pair0
  14.9 0.0 collective-permute-done.3.pair1
  14.9 8.3 %shard_map.65 = (f32[8,9,136,128]{3,2,1,0:T(8,128)S(1)}, f32[8,8,128,128]{3,2,1,0:T(8,128)S(1)}, f32[8,8,128,128]{3,2,1,0:T(8,128)S(1)}, f32[8,128,128]{2,1,0:T(...) custom-call(s32[6]{0:T(128)S(1)} %stack.47.info, ...), custom_call_target="tpu_custom_call" | custom-call | tf_op jit(solution)/shard_map/pallas_call | solution.py:375
  23.2 4.5 %collective-permute-start.7 = (bf16[4,128,128]{2,1,0:T(8,128)(2,1)S(1)}, bf16[4,128,128]{2,1,0:T(8,128)(2,1)S(1)}, u32[]{:S(2)}, u32[]{:S(2)}) collective-permute-start(bf16[4,128,128]{2,1,0:T(8,128)(2,1)S(1)} %get-tuple-element.37), channel_id=1, source_target_pairs={{0,2},{4,6},{2,0},{6,4},{1,3},{5,7},{3,1},{7,5},{8,10},{12,14},{10... | collective-permute-start | bytes 393224 | tf_op jit(solution)/shard_map/ppermute | solution.py:403
  27.6 0.7 %collective-permute-start.8 = (bf16[4,128,128]{2,1,0:T(8,128)(2,1)S(1)}, bf16[4,128,128]{2,1,0:T(8,128)(2,1)S(1)}, u32[]{:S(2)}, u32[]{:S(2)}) collective-permute-start(bf16[4,128,128]{2,1,0:T(8,128)(2,1)S(1)} %get-tuple-element.38), channel_id=1, source_target_pairs={{2,4},{4,2},{3,5},{5,3},{10,12},{12,10},{11,13},{13,11},{18,20},{2... | collective-permute-start | bytes 393224 | tf_op jit(solution)/shard_map/ppermute | solution.py:403
  28.3 0.1 collective-permute-start.5
  28.4 0.5 collective-permute-start.9
  28.9 0.6 %collective-permute-done.5 = f32[3,8,128]{2,1,0:T(8,128)S(1)} collective-permute-done((f32[3,8,128]{2,1,0:T(8,128)S(1)}, f32[3,8,128]{2,1,0:T(8,128)S(1)}, u32[]{:S(2)}, u32[]{:S(2)}) %collective-permute-start.5) | collective-permute-done | bytes 12320 | tf_op jit(solution)/shard_map/ppermute | solution.py:411
  29.6 1.5 %collective-permute-start.6 = (f32[3,8,128]{2,1,0:T(8,128)S(1)}, f32[3,8,128]{2,1,0:T(8,128)S(1)}, u32[]{:S(2)}, u32[]{:S(2)}) collective-permute-start(f32[3,8,128]{2,1,0:T(8,128)S(1)} %add.18.same), channel_id=1, source_target_pairs={{0,16},{8,24},{16,0},{24,8},{1,17},{9,25},{17,1},{25,9},{2,18},{10... | collective-permute-start | bytes 36872 | tf_op jit(solution)/shard_map/ppermute | solution.py:413
  31.0 1.1 %collective-permute-done.9.yrecv = bf16[8,8,128]{2,1,0:T(8,128)(2,1)S(1)} collective-permute-done((bf16[8,8,128]{2,1,0:T(8,128)(2,1)S(1)}, bf16[8,8,128]{2,1,0:T(8,128)(2,1)S(1)}, u32[]{:S(2)}, u32[]{:S(2)}) %collective-permute-start.9) | collective-permute-done | bytes 16416 | tf_op jit(solution)/shard_map/ppermute | solution.py:406
  32.2 1.1 %collective-permute-done.6.other = f32[3,8,128]{2,1,0:T(8,128)S(1)} collective-permute-done((f32[3,8,128]{2,1,0:T(8,128)S(1)}, f32[3,8,128]{2,1,0:T(8,128)S(1)}, u32[]{:S(2)}, u32[]{:S(2)}) %collective-permute-start.6) | collective-permute-done | bytes 12320 | tf_op jit(solution)/shard_map/ppermute | solution.py:413
  33.2 0.0 collective-permute-done.7.pair0
  33.3 0.0 collective-permute-done.8.pair1
  33.3 2.9 %shard_map.66 = (f32[8,9,136,128]{3,2,1,0:T(8,128)S(1)}, bf16[4,128,128]{2,1,0:T(8,128)(2,1)S(1)}, bf16[4,128,128]{2,1,0:T(8,128)(2,1)S(1)}, bf16[8,8,128]{2,1,0:T(8,128)(2,1)S(1)}, f32[3,8,128]{2,1,0:T(8,128)S(1)}) custom-call(s32[6]{0:T(128)S(1)} %stack.47.info, s32[2,8]{1,0:T(2,128)S(1)} %copy-done.1, ...), custom_call_target="tpu_custom_call", output_to_operand_aliasing={{0}: (12, {})} | custom-call | tf_op jit(solution)/shard_map/pallas_call | solution.py:375
  36.1 1.8 %collective-permute-start.12 = (bf16[4,128,128]{2,1,0:T(8,128)(2,1)S(1)}, bf16[4,128,128]{2,1,0:T(8,128)(2,1)S(1)}, u32[]{:S(2)}, u32[]{:S(2)}) collective-permute-start(bf16[4,128,128]{2,1,0:T(8,128)(2,1)S(1)} %get-tuple-element.47), channel_id=1, source_target_pairs={{0,2},{4,6},{2,0},{6,4},{1,3},{5,7},{3,1},{7,5},{8,10},{12,14},{10... | collective-permute-start | bytes 393224 | tf_op jit(solution)/shard_map/ppermute | solution.py:403
  37.9 0.7 %collective-permute-start.13 = (bf16[4,128,128]{2,1,0:T(8,128)(2,1)S(1)}, bf16[4,128,128]{2,1,0:T(8,128)(2,1)S(1)}, u32[]{:S(2)}, u32[]{:S(2)}) collective-permute-start(bf16[4,128,128]{2,1,0:T(8,128)(2,1)S(1)} %get-tuple-element.48), channel_id=1, source_target_pairs={{2,4},{4,2},{3,5},{5,3},{10,12},{12,10},{11,13},{13,11},{18,20},{2... | collective-permute-start | bytes 393224 | tf_op jit(solution)/shard_map/ppermute | solution.py:403
  38.6 0.1 collective-permute-start.10
  38.7 1.0 %collective-permute-start.14 = (bf16[8,8,128]{2,1,0:T(8,128)(2,1)S(1)}, bf16[8,8,128]{2,1,0:T(8,128)(2,1)S(1)}, u32[]{:S(2)}, u32[]{:S(2)}) collective-permute-start(bf16[8,8,128]{2,1,0:T(8,128)(2,1)S(1)} %get-tuple-element.49), channel_id=1, source_target_pairs={{0,1},{1,0},{2,3},{3,2},{4,5},{5,4},{6,7},{7,6},{8,9},{9,8},{10,11... | collective-permute-start | bytes 49160 | tf_op jit(solution)/shard_map/ppermute | solution.py:406
  39.7 0.2 collective-permute-done.10
  39.8 1.5 %collective-permute-start.11 = (f32[3,8,128]{2,1,0:T(8,128)S(1)}, f32[3,8,128]{2,1,0:T(8,128)S(1)}, u32[]{:S(2)}, u32[]{:S(2)}) collective-permute-start(f32[3,8,128]{2,1,0:T(8,128)S(1)} %add.19.same), channel_id=1, source_target_pairs={{0,16},{8,24},{16,0},{24,8},{1,17},{9,25},{17,1},{25,9},{2,18},{10... | collective-permute-start | bytes 36872 | tf_op jit(solution)/shard_map/ppermute | solution.py:413
  41.3 1.2 %collective-permute-done.14.yrecv = bf16[8,8,128]{2,1,0:T(8,128)(2,1)S(1)} collective-permute-done((bf16[8,8,128]{2,1,0:T(8,128)(2,1)S(1)}, bf16[8,8,128]{2,1,0:T(8,128)(2,1)S(1)}, u32[]{:S(2)}, u32[]{:S(2)}) %collective-permute-start.14) | collective-permute-done | bytes 16416 | tf_op jit(solution)/shard_map/ppermute | solution.py:406
  42.5 1.1 %collective-permute-done.11.other = f32[3,8,128]{2,1,0:T(8,128)S(1)} collective-permute-done((f32[3,8,128]{2,1,0:T(8,128)S(1)}, f32[3,8,128]{2,1,0:T(8,128)S(1)}, u32[]{:S(2)}, u32[]{:S(2)}) %collective-permute-start.11) | collective-permute-done | bytes 12320 | tf_op jit(solution)/shard_map/ppermute | solution.py:413
  43.5 0.0 collective-permute-done.13.pair1
  43.5 2.9 %shard_map.67 = (f32[8,9,136,128]{3,2,1,0:T(8,128)S(1)}, bf16[4,128,128]{2,1,0:T(8,128)(2,1)S(1)}, bf16[4,128,128]{2,1,0:T(8,128)(2,1)S(1)}, bf16[8,8,128]{2,1,0:T(8,128)(2,1)S(1)}, f32[3,8,128]{2,1,0:T(8,128)S(1)}) custom-call(s32[6]{0:T(128)S(1)} %stack.47.info, s32[2,8]{1,0:T(2,128)S(1)} %copy-done.1, ...), custom_call_target="tpu_custom_call", output_to_operand_aliasing={{0}: (12, {})} | custom-call | tf_op jit(solution)/shard_map/pallas_call | solution.py:375
  46.4 2.8 %collective-permute-start.17 = (bf16[4,128,128]{2,1,0:T(8,128)(2,1)S(1)}, bf16[4,128,128]{2,1,0:T(8,128)(2,1)S(1)}, u32[]{:S(2)}, u32[]{:S(2)}) collective-permute-start(bf16[4,128,128]{2,1,0:T(8,128)(2,1)S(1)} %get-tuple-element.52), channel_id=1, source_target_pairs={{0,2},{4,6},{2,0},{6,4},{1,3},{5,7},{3,1},{7,5},{8,10},{12,14},{10... | collective-permute-start | bytes 393224 | tf_op jit(solution)/shard_map/ppermute | solution.py:403
  49.2 0.7 %collective-permute-start.18 = (bf16[4,128,128]{2,1,0:T(8,128)(2,1)S(1)}, bf16[4,128,128]{2,1,0:T(8,128)(2,1)S(1)}, u32[]{:S(2)}, u32[]{:S(2)}) collective-permute-start(bf16[4,128,128]{2,1,0:T(8,128)(2,1)S(1)} %get-tuple-element.53), channel_id=1, source_target_pairs={{2,4},{4,2},{3,5},{5,3},{10,12},{12,10},{11,13},{13,11},{18,20},{2... | collective-permute-start | bytes 393224 | tf_op jit(solution)/shard_map/ppermute | solution.py:403
  49.9 0.1 collective-permute-start.15
  49.9 1.0 %collective-permute-start.19 = (bf16[8,8,128]{2,1,0:T(8,128)(2,1)S(1)}, bf16[8,8,128]{2,1,0:T(8,128)(2,1)S(1)}, u32[]{:S(2)}, u32[]{:S(2)}) collective-permute-start(bf16[8,8,128]{2,1,0:T(8,128)(2,1)S(1)} %get-tuple-element.54), channel_id=1, source_target_pairs={{0,1},{1,0},{2,3},{3,2},{4,5},{5,4},{6,7},{7,6},{8,9},{9,8},{10,11... | collective-permute-start | bytes 49160 | tf_op jit(solution)/shard_map/ppermute | solution.py:406
  50.9 0.2 collective-permute-done.15
  51.1 1.5 %collective-permute-start.16 = (f32[3,8,128]{2,1,0:T(8,128)S(1)}, f32[3,8,128]{2,1,0:T(8,128)S(1)}, u32[]{:S(2)}, u32[]{:S(2)}) collective-permute-start(f32[3,8,128]{2,1,0:T(8,128)S(1)} %add.20.same), channel_id=1, source_target_pairs={{0,16},{8,24},{16,0},{24,8},{1,17},{9,25},{17,1},{25,9},{2,18},{10... | collective-permute-start | bytes 36872 | tf_op jit(solution)/shard_map/ppermute | solution.py:413
  52.6 1.1 %collective-permute-done.19.yrecv = bf16[8,8,128]{2,1,0:T(8,128)(2,1)S(1)} collective-permute-done((bf16[8,8,128]{2,1,0:T(8,128)(2,1)S(1)}, bf16[8,8,128]{2,1,0:T(8,128)(2,1)S(1)}, u32[]{:S(2)}, u32[]{:S(2)}) %collective-permute-start.19) | collective-permute-done | bytes 16416 | tf_op jit(solution)/shard_map/ppermute | solution.py:406
  53.7 1.1 %collective-permute-done.16.other = f32[3,8,128]{2,1,0:T(8,128)S(1)} collective-permute-done((f32[3,8,128]{2,1,0:T(8,128)S(1)}, f32[3,8,128]{2,1,0:T(8,128)S(1)}, u32[]{:S(2)}, u32[]{:S(2)}) %collective-permute-start.16) | collective-permute-done | bytes 12320 | tf_op jit(solution)/shard_map/ppermute | solution.py:413
  54.8 0.0 collective-permute-done.17.pair0
  54.8 5.0 %shard_map.68 = (bf16[8192,128]{1,0:T(8,128)(2,1)}, f32[8,9,136,128]{3,2,1,0:T(8,128)S(1)}) custom-call(s32[6]{0:T(128)S(1)} %stack.47.info, s32[2,8]{1,0:T(2,128)S(1)} %copy-done.1, f32[3,8,128]{2,1,0:T(8,128)S(1)} %add.20.same, f32[3,8,128]{2,1,0:T(8,128)S(1)} %collective-permute-done.16.other, ...), custom_call_target="tpu_custom_call", output_to_operand_aliasing={{1}: (12, {})} | custom-call | tf_op jit(solution)/shard_map/pallas_call | solution.py:375
  (15 shorter events, 0.1 us)
Async XLA Ops:
  0.0 14.9 %copy-start.1 = (s32[2,8]{1,0:T(2,128)S(1)}, s32[2,8]{1,0:T(2,128)}, u32[]{:S(2)}) copy-start(s32[2,8]{1,0:T(2,128)} %kindy.7) | copy-start | bytes 196
  0.0 14.9 %copy-start.3 = (s32[2,128]{1,0:T(2,128)S(1)}, s32[2,128]{1,0:T(2,128)}, u32[]{:S(2)}) copy-start(s32[2,128]{1,0:T(2,128)} %kindx.1) | copy-start | bytes 3076
  0.0 14.9 %copy-start.2 = (f32[8,128]{1,0:T(8,128)S(1)}, f32[8,128]{1,0:T(8,128)}, u32[]{:S(2)}) copy-start(f32[8,128]{1,0:T(8,128)} %relax.1) | copy-start | bytes 12292
  0.1 1.6 %copy-start = (bf16[1024,8,128]{2,1,0:T(8,128)(2,1)S(1)}, bf16[1024,8,128]{2,1,0:T(8,128)(2,1)}, u32[]{:S(2)}) copy-start(bf16[1024,8,128]{2,1,0:T(8,128)(2,1)} %param.6) | copy-start | bytes 6291460
  4.5 9.1 %collective-permute-start.4 = (bf16[2,8,512]{2,1,0:T(8,128)(2,1)S(1)}, bf16[2,8,512]{2,1,0:T(8,128)(2,1)S(1)}, u32[]{:S(2)}, u32[]{:S(2)}) collective-permute-start(bf16[2,8,512]{2,1,0:T(8,128)(2,1)S(1)} %get-tuple-element.35), channel_id=1, source_target_pairs={{0,1},{1,0},{2,3},{3,2},{4,5},{5,4},{6,7},{7,6},{8,9},{9,8},{10,11... | collective-permute-start | bytes 49160 | tf_op jit(solution)/shard_map/ppermute | solution.py:406
  7.5 3.3 %collective-permute-start = (f32[7,8,128]{2,1,0:T(8,128)S(1)}, f32[7,8,128]{2,1,0:T(8,128)S(1)}, u32[]{:S(2)}, u32[]{:S(2)}) collective-permute-start(f32[7,8,128]{2,1,0:T(8,128)S(1)} %get-tuple-element.31), channel_id=1, source_target_pairs={{0,8},{8,0},{16,24},{24,16},{1,9},{9,1},{17,25},{25,17},{2,10},{10... | collective-permute-start | bytes 86024 | tf_op jit(solution)/shard_map/ppermute | solution.py:411
  7.5 7.3 %collective-permute-start.2 = (bf16[512,128]{1,0:T(8,128)(2,1)S(1)}, bf16[512,128]{1,0:T(8,128)(2,1)S(1)}, u32[]{:S(2)}, u32[]{:S(2)}) collective-permute-start(bf16[512,128]{1,0:T(8,128)(2,1)S(1)} %get-tuple-element.33), channel_id=1, source_target_pairs={{0,2},{4,6},{2,0},{6,4},{1,3},{5,7},{3,1},{7,5},{8,10},{12,14},{10... | collective-permute-start | bytes 393224 | tf_op jit(solution)/shard_map/ppermute | solution.py:403
  9.1 5.7 %collective-permute-start.3 = (bf16[512,128]{1,0:T(8,128)(2,1)S(1)}, bf16[512,128]{1,0:T(8,128)(2,1)S(1)}, u32[]{:S(2)}, u32[]{:S(2)}) collective-permute-start(bf16[512,128]{1,0:T(8,128)(2,1)S(1)} %get-tuple-element.34), channel_id=1, source_target_pairs={{2,4},{4,2},{3,5},{5,3},{10,12},{12,10},{11,13},{13,11},{18,20},{2... | collective-permute-start | bytes 393224 | tf_op jit(solution)/shard_map/ppermute | solution.py:403
  10.9 3.9 %collective-permute-start.1 = (f32[7,8,128]{2,1,0:T(8,128)S(1)}, f32[7,8,128]{2,1,0:T(8,128)S(1)}, u32[]{:S(2)}, u32[]{:S(2)}) collective-permute-start(f32[7,8,128]{2,1,0:T(8,128)S(1)} %add.17.same), channel_id=1, source_target_pairs={{0,16},{8,24},{16,0},{24,8},{1,17},{9,25},{17,1},{25,9},{2,18},{10... | collective-permute-start | bytes 86024 | tf_op jit(solution)/shard_map/ppermute | solution.py:413
  23.2 10.1 %collective-permute-start.7 = (bf16[4,128,128]{2,1,0:T(8,128)(2,1)S(1)}, bf16[4,128,128]{2,1,0:T(8,128)(2,1)S(1)}, u32[]{:S(2)}, u32[]{:S(2)}) collective-permute-start(bf16[4,128,128]{2,1,0:T(8,128)(2,1)S(1)} %get-tuple-element.37), channel_id=1, source_target_pairs={{0,2},{4,6},{2,0},{6,4},{1,3},{5,7},{3,1},{7,5},{8,10},{12,14},{10... | collective-permute-start | bytes 393224 | tf_op jit(solution)/shard_map/ppermute | solution.py:403
  27.6 5.6 %collective-permute-start.8 = (bf16[4,128,128]{2,1,0:T(8,128)(2,1)S(1)}, bf16[4,128,128]{2,1,0:T(8,128)(2,1)S(1)}, u32[]{:S(2)}, u32[]{:S(2)}) collective-permute-start(bf16[4,128,128]{2,1,0:T(8,128)(2,1)S(1)} %get-tuple-element.38), channel_id=1, source_target_pairs={{2,4},{4,2},{3,5},{5,3},{10,12},{12,10},{11,13},{13,11},{18,20},{2... | collective-permute-start | bytes 393224 | tf_op jit(solution)/shard_map/ppermute | solution.py:403
  28.3 1.2 %collective-permute-start.5 = (f32[3,8,128]{2,1,0:T(8,128)S(1)}, f32[3,8,128]{2,1,0:T(8,128)S(1)}, u32[]{:S(2)}, u32[]{:S(2)}) collective-permute-start(f32[3,8,128]{2,1,0:T(8,128)S(1)} %get-tuple-element.36), channel_id=1, source_target_pairs={{0,8},{8,0},{16,24},{24,16},{1,9},{9,1},{17,25},{25,17},{2,10},{10... | collective-permute-start | bytes 36872 | tf_op jit(solution)/shard_map/ppermute | solution.py:411
  28.4 3.8 %collective-permute-start.9 = (bf16[8,8,128]{2,1,0:T(8,128)(2,1)S(1)}, bf16[8,8,128]{2,1,0:T(8,128)(2,1)S(1)}, u32[]{:S(2)}, u32[]{:S(2)}) collective-permute-start(bf16[8,8,128]{2,1,0:T(8,128)(2,1)S(1)} %get-tuple-element.39), channel_id=1, source_target_pairs={{0,1},{1,0},{2,3},{3,2},{4,5},{5,4},{6,7},{7,6},{8,9},{9,8},{10,11... | collective-permute-start | bytes 49160 | tf_op jit(solution)/shard_map/ppermute | solution.py:406
  29.6 3.7 %collective-permute-start.6 = (f32[3,8,128]{2,1,0:T(8,128)S(1)}, f32[3,8,128]{2,1,0:T(8,128)S(1)}, u32[]{:S(2)}, u32[]{:S(2)}) collective-permute-start(f32[3,8,128]{2,1,0:T(8,128)S(1)} %add.18.same), channel_id=1, source_target_pairs={{0,16},{8,24},{16,0},{24,8},{1,17},{9,25},{17,1},{25,9},{2,18},{10... | collective-permute-start | bytes 36872 | tf_op jit(solution)/shard_map/ppermute | solution.py:413
  36.1 7.4 %collective-permute-start.12 = (bf16[4,128,128]{2,1,0:T(8,128)(2,1)S(1)}, bf16[4,128,128]{2,1,0:T(8,128)(2,1)S(1)}, u32[]{:S(2)}, u32[]{:S(2)}) collective-permute-start(bf16[4,128,128]{2,1,0:T(8,128)(2,1)S(1)} %get-tuple-element.47), channel_id=1, source_target_pairs={{0,2},{4,6},{2,0},{6,4},{1,3},{5,7},{3,1},{7,5},{8,10},{12,14},{10... | collective-permute-start | bytes 393224 | tf_op jit(solution)/shard_map/ppermute | solution.py:403
  37.9 5.6 %collective-permute-start.13 = (bf16[4,128,128]{2,1,0:T(8,128)(2,1)S(1)}, bf16[4,128,128]{2,1,0:T(8,128)(2,1)S(1)}, u32[]{:S(2)}, u32[]{:S(2)}) collective-permute-start(bf16[4,128,128]{2,1,0:T(8,128)(2,1)S(1)} %get-tuple-element.48), channel_id=1, source_target_pairs={{2,4},{4,2},{3,5},{5,3},{10,12},{12,10},{11,13},{13,11},{18,20},{2... | collective-permute-start | bytes 393224 | tf_op jit(solution)/shard_map/ppermute | solution.py:403
  38.6 1.2 %collective-permute-start.10 = (f32[3,8,128]{2,1,0:T(8,128)S(1)}, f32[3,8,128]{2,1,0:T(8,128)S(1)}, u32[]{:S(2)}, u32[]{:S(2)}) collective-permute-start(f32[3,8,128]{2,1,0:T(8,128)S(1)} %get-tuple-element.46), channel_id=1, source_target_pairs={{0,8},{8,0},{16,24},{24,16},{1,9},{9,1},{17,25},{25,17},{2,10},{10... | collective-permute-start | bytes 36872 | tf_op jit(solution)/shard_map/ppermute | solution.py:411
  38.7 3.8 %collective-permute-start.14 = (bf16[8,8,128]{2,1,0:T(8,128)(2,1)S(1)}, bf16[8,8,128]{2,1,0:T(8,128)(2,1)S(1)}, u32[]{:S(2)}, u32[]{:S(2)}) collective-permute-start(bf16[8,8,128]{2,1,0:T(8,128)(2,1)S(1)} %get-tuple-element.49), channel_id=1, source_target_pairs={{0,1},{1,0},{2,3},{3,2},{4,5},{5,4},{6,7},{7,6},{8,9},{9,8},{10,11... | collective-permute-start | bytes 49160 | tf_op jit(solution)/shard_map/ppermute | solution.py:406
  39.8 3.7 %collective-permute-start.11 = (f32[3,8,128]{2,1,0:T(8,128)S(1)}, f32[3,8,128]{2,1,0:T(8,128)S(1)}, u32[]{:S(2)}, u32[]{:S(2)}) collective-permute-start(f32[3,8,128]{2,1,0:T(8,128)S(1)} %add.19.same), channel_id=1, source_target_pairs={{0,16},{8,24},{16,0},{24,8},{1,17},{9,25},{17,1},{25,9},{2,18},{10... | collective-permute-start | bytes 36872 | tf_op jit(solution)/shard_map/ppermute | solution.py:413
  46.4 8.4 %collective-permute-start.17 = (bf16[4,128,128]{2,1,0:T(8,128)(2,1)S(1)}, bf16[4,128,128]{2,1,0:T(8,128)(2,1)S(1)}, u32[]{:S(2)}, u32[]{:S(2)}) collective-permute-start(bf16[4,128,128]{2,1,0:T(8,128)(2,1)S(1)} %get-tuple-element.52), channel_id=1, source_target_pairs={{0,2},{4,6},{2,0},{6,4},{1,3},{5,7},{3,1},{7,5},{8,10},{12,14},{10... | collective-permute-start | bytes 393224 | tf_op jit(solution)/shard_map/ppermute | solution.py:403
  49.2 5.6 %collective-permute-start.18 = (bf16[4,128,128]{2,1,0:T(8,128)(2,1)S(1)}, bf16[4,128,128]{2,1,0:T(8,128)(2,1)S(1)}, u32[]{:S(2)}, u32[]{:S(2)}) collective-permute-start(bf16[4,128,128]{2,1,0:T(8,128)(2,1)S(1)} %get-tuple-element.53), channel_id=1, source_target_pairs={{2,4},{4,2},{3,5},{5,3},{10,12},{12,10},{11,13},{13,11},{18,20},{2... | collective-permute-start | bytes 393224 | tf_op jit(solution)/shard_map/ppermute | solution.py:403
  49.9 1.2 %collective-permute-start.15 = (f32[3,8,128]{2,1,0:T(8,128)S(1)}, f32[3,8,128]{2,1,0:T(8,128)S(1)}, u32[]{:S(2)}, u32[]{:S(2)}) collective-permute-start(f32[3,8,128]{2,1,0:T(8,128)S(1)} %get-tuple-element.51), channel_id=1, source_target_pairs={{0,8},{8,0},{16,24},{24,16},{1,9},{9,1},{17,25},{25,17},{2,10},{10... | collective-permute-start | bytes 36872 | tf_op jit(solution)/shard_map/ppermute | solution.py:411
  49.9 3.8 %collective-permute-start.19 = (bf16[8,8,128]{2,1,0:T(8,128)(2,1)S(1)}, bf16[8,8,128]{2,1,0:T(8,128)(2,1)S(1)}, u32[]{:S(2)}, u32[]{:S(2)}) collective-permute-start(bf16[8,8,128]{2,1,0:T(8,128)(2,1)S(1)} %get-tuple-element.54), channel_id=1, source_target_pairs={{0,1},{1,0},{2,3},{3,2},{4,5},{5,4},{6,7},{7,6},{8,9},{9,8},{10,11... | collective-permute-start | bytes 49160 | tf_op jit(solution)/shard_map/ppermute | solution.py:406
  51.1 3.7 %collective-permute-start.16 = (f32[3,8,128]{2,1,0:T(8,128)S(1)}, f32[3,8,128]{2,1,0:T(8,128)S(1)}, u32[]{:S(2)}, u32[]{:S(2)}) collective-permute-start(f32[3,8,128]{2,1,0:T(8,128)S(1)} %add.20.same), channel_id=1, source_target_pairs={{0,16},{8,24},{16,0},{24,8},{1,17},{9,25},{17,1},{25,9},{2,18},{10... | collective-permute-start | bytes 36872 | tf_op jit(solution)/shard_map/ppermute | solution.py:413

commit v2 on v1

--- a/solution.py
+++ b/solution.py
@@ -56,6 +56,14 @@
     return ix, iy
 
 
+def device_info(local_ky):
+    v, ix, iy = lax.axis_index("vel"), lax.axis_index("gx"), lax.axis_index("gy")
+    up = (v >= lax.axis_size("vel") // 2).astype(jnp.int32)
+    wall = jnp.where(iy == jnp.where(up == 1, 0, lax.axis_size("gy") - 1), 1, 0)
+    first, last = (ix == 0).astype(jnp.int32), (ix == lax.axis_size("gx") - 1).astype(jnp.int32)
+    return [v * local_ky, up, first, last, wall, 1 - lax.rem(ix, 2)]
+
+
 def flip_matrix(up, size):
     row, col = iota((size, size), 0), iota((size, size), 1)
     return (col == jnp.where(up, row, size - 1 - row)).astype(F32)
@@ -72,14 +80,28 @@
     return [high, middle, rest - middle]
 
 
-def moments_kernel(info, prev, pay, ymsg, pt, xmsg0, xmsg1, rows):
+def stacked(a):
+    return jnp.concatenate(pieces(a), axis=0).astype(BF16)
+
+
+def moments_kernel(prev, relax_far, kindx_far, pay, ymsg, pt, xmsg0, xmsg1, relax, kindx, rows, staged, sems, few):
     cells_x, _, count, cells_y = pt.shape
+    info = device_info(count // HALF)
     span = HALF * cells_x
+    copies = [pltpu.make_async_copy(prev.at[pl.ds(i * span, span), :], staged.at[pl.ds(i * span, span), :], sems.at[i])
+              for i in range(2 * count // HALF)]
+    order = [2 * i + sign for sign in range(2) for i in range(count // HALF)]
+    for i in order:
+        copies[i].start()
+    small = [pltpu.make_async_copy(relax_far, relax, few.at[0]), pltpu.make_async_copy(kindx_far, kindx, few.at[1])]
+    for copy in small:
+        copy.start()
     for sign in range(2):
         for at in range(count // LANES):
             for i in range(LANES // HALF):
-                start = ((at * (LANES // HALF) + i) * NVX + sign * HALF) * cells_x
-                rows[i * span : (i + 1) * span, :] = prev[start : start + span, :].astype(F32)
+                chunk = (at * (LANES // HALF) + i) * 2 + sign
+                copies[chunk].wait()
+                rows[i * span : (i + 1) * span, :] = staged[chunk * span : (chunk + 1) * span, :].astype(F32)
             for x in range(cells_x):
                 pt[x, sign, at * LANES : (at + 1) * LANES, :] = rows[pl.ds(x, LANES, stride=cells_x), :].astype(BF16)
     even = info[5]
@@ -116,7 +138,8 @@
         pay[3, x : x + 1, :] = total[3:4] + total[4:5]
     flip = flip_matrix(up, cells_y)
     fx = jnp.concatenate([out_row[0], out_row[1], jnp.zeros((6, cells_y), F32)], axis=0)
-    pay[4] = nt(fx, flip, HIGHEST)
+    turned = nt(stacked(fx), flip.astype(BF16))
+    pay[4] = turned[0:8] + turned[8:16] + turned[16:24]
     for sign in range(2):
         total = jnp.zeros((cells_x, LANES), F32)
         for at in range(count // LANES):
@@ -124,6 +147,8 @@
             total += jnp.abs(iy).astype(F32) * edge[sign][:cells_x, at * LANES : (at + 1) * LANES]
         pay[6 - sign] = total
         ymsg[sign] = edge[sign][:cells_x].astype(BF16)
+    for copy in small:
+        copy.wait()
 
 
 def newton_params(u0, u1, u2, u3):
@@ -131,21 +156,23 @@
     square = ux * ux + uy * uy
     temperature = u3 / u0 - square / 2.0
     p = [jnp.log(u0 / temperature) - square / (2.0 * temperature), ux / temperature, uy / temperature, -1.0 / temperature]
-    line = [float((i - (NVX - 1) / 2.0) * STEP) for i in range(NVX)]
+    last = (HALF - 0.5) * STEP
     for _ in range(NEWTON):
         half_p3 = p[3] * 0.5
         sums, tops = [], []
         for slope in (p[1], p[2]):
-            top = None
-            for value in line:
-                arg = value * (slope + value * half_p3)
-                top = arg if top is None else jnp.maximum(top, arg)
+            vertex = jnp.where(p[3] < 0.0, -slope / p[3], 0.0) * (1.0 / STEP)
+            node = (jnp.clip(jnp.floor(vertex), -HALF, HALF - 1.0) + 0.5) * STEP
+            end = (last * last) * half_p3 + last * jnp.abs(slope)
+            top = jnp.maximum(node * (slope + node * half_p3), end)
             total = [None] * 5
-            for value in line:
-                term = jnp.exp(value * (slope + value * half_p3) - top)
-                for power in range(5):
-                    total[power] = term if total[power] is None else total[power] + term
-                    term = term * value
+            for i in range(HALF):
+                value = (i + 0.5) * STEP
+                even, odd = (value * value) * half_p3 - top, value * slope
+                plus, minus = jnp.exp(even + odd), jnp.exp(even - odd)
+                even, odd = plus + minus, plus - minus
+                terms = [even, value * odd, value**2 * even, value**3 * odd, value**4 * even]
+                total = [t if old is None else old + t for old, t in zip(total, terms)]
             sums.append(total)
             tops.append(top)
         scale = jnp.exp(p[0] + (tops[0] + tops[1])) * WEIGHT
@@ -185,7 +212,10 @@
     per_sign = blocks // 2
     first_ky, up = info[0], info[1] == 1
     anti = flip_matrix(False, cells_y)
-    fx = (same[0] + nn(other[0], anti, HIGHEST)) * FLUX_SCALE
+    turned = nn(stacked(other[0]), anti.astype(BF16))
+    fx = (same[0] + (turned[0:8] + turned[8:16] + turned[16:24])) * FLUX_SCALE
+    lane = iota((24, 2 * LANES), 1) // LANES
+    columns = tn(stacked(fx), (iota((24, 2 * LANES), 0) % 8 == 1 - lane).astype(F32).astype(BF16))
     fy = jnp.sum(other[1], axis=1, keepdims=True) + reverse_rows(jnp.sum(other[2], axis=1, keepdims=True))
     fy = fy * FLUX_SCALE
     fy = [reverse_rows(fy), fy]
@@ -193,8 +223,7 @@
     cell = iota((cells_x, LANES), 0)
     y_wall = info[4] == 1
     for sign in range(2):
-        pick = (iota((8, LANES), 0) == 1 - sign).astype(F32)
-        column = tn(fx, pick, HIGHEST)
+        column = columns[:, sign * LANES : (sign + 1) * LANES]
         x_wall = info[3 - sign] == 1
         ky_kind = jnp.zeros((cells_x, LANES), jnp.int32)
         for x in range(cells_x):
@@ -212,23 +241,33 @@
                 g[block, 1 + x, 7:8, :] = value[x : x + 1]
 
 
-def sweep(info, g, s, r):
+def sweep(info, g, s, r, part="all"):
     blocks, slots, padded, _ = g.shape
     cells_x, cells_y = slots - 1, padded - 8
-    first_ky = info[0]
-
-    def step(block, carry):
-        ax, ay = block_speeds(first_ky, block, blocks // 2, (8, LANES))
-        for x in range(cells_x - 1, -1, -1):
-            for at in range(cells_y // 8 - 1, -1, -1):
-                here = pl.ds(8 * at, 8)
-                value = s[block, x, here, :] + ax * g[block, x, pl.ds(8 + 8 * at, 8), :]
-                value += ay * g[block, 1 + x, pl.ds(7 + 8 * at, 8), :]
-                value = (value * r[block, x, here, :]).astype(BF16).astype(F32)
-                g[block, 1 + x, pl.ds(8 + 8 * at, 8), :] = value
+    tile = 16
+    inner = [(x, at) for x in range(cells_x - 1, 0, -1) for at in range(cells_y - tile, 0, -tile)]
+    rim = [(x, 0) for x in range(cells_x - 1, 0, -1)] + [(0, at) for at in range(cells_y - tile, -1, -tile)]
+    todo = inner if part == "inner" else rim if part == "rim" else inner + rim
+
+    def step(both, carry):
+        for i in range(2):
+            block = 2 * both + i
+            half = slice(i * LANES, (i + 1) * LANES)
+            ax, ay = block_speeds(info[0], block, blocks // 2, (tile, LANES))
+            for x, at in todo:
+                here = pl.ds(at, tile)
+                value = s[block, x, here, :] + ax * g[block, x, pl.ds(8 + at, tile), :]
+                value += ay * g[block, 1 + x, pl.ds(7 + at, tile), :]
+                value = (value * r[both, x, here, half]).astype(BF16)
+                g[block, 1 + x, pl.ds(8 + at, tile), :] = value.astype(F32)
         return carry
 
-    lax.fori_loop(0, blocks, step, 0)
+    lax.fori_loop(0, blocks // 2, step, 0)
+
+
+def inner_kernel(s, r, g_in, g):
+    blocks = g.shape[0]
+    sweep(device_info(blocks // 2 * LANES // HALF), g, s, r, "inner")
 
 
 def send_out(info, g, xmsg, ymsg, flux):
@@ -251,73 +290,92 @@
         for at in range(per_sign):
             take = sign * (1 - info[5]) + (1 - sign) * info[5]
             xmsg[sign][at] = g[take * per_sign + at, cells_x, 8:, :].astype(BF16)
-        pick = (iota((8, LANES), 0) == sign).astype(F32)
-        part = nt(pick, total, HIGHEST)
+        pick = (iota((16, 3 * LANES), 0) == sign).astype(F32).astype(BF16)
+        part = nt(pick, jnp.concatenate(pieces(total), axis=1).astype(BF16))[0:8]
         fx = part if fx is None else fx + part
         flux[2 - sign] = total_y
     flux[0] = fx
 
 
-def first_kernel(info, kindy, same, other, relax, kindx, pt, pair0, pair1, yrecv, lri, bti,
-                 g, s, r, xw, yw, kx, xmsg0, xmsg1, ymsg, flux, ta, tb, tr, fa, fb):
+def spread(table, choice, size):
+    row = iota((3 * size, choice.shape[1]), 0) % size
+    return nn(table, (row == choice).astype(F32).astype(BF16))
+
+
+def transposed(flip, table, ref, x, cells_x, cells_y):
+    wide = nt(flip, stacked(table)).astype(BF16)
+    ref[1, x * cells_y : (x + 1) * cells_y, :] = wide
+    ref[0, (cells_x - 1 - x) * cells_y : (cells_x - x) * cells_y, :] = wide
+
+
+def table_kernel(relax, kindx, pt, lri, bti, g, r, xw, yw, kx, tr):
     cells_x, _, count, cells_y = pt.shape
     per_sign = count // LANES
-    blocks = 2 * per_sign
+    info = device_info(count // HALF)
+    flip = flip_matrix(info[1] == 1, cells_y).astype(BF16)
+    base = 1.0 / TIME_STEP + 1.0 / relax[...]
+    steps = iota((NVX, cells_y), 0).astype(F32) * STEP
+    for x in range(cells_x):
+        transposed(flip, 1.0 / (base[x : x + 1] + steps), tr, x, cells_x, cells_y)
+    kind = jnp.concatenate([kindx[1:2], kindx[0:1], jnp.zeros((6, cells_y), jnp.int32)], axis=0).astype(F32)
+    kind = nt(kind.astype(BF16), flip).astype(BF16)
+    for sign in range(2):
+        kx[sign] = tn(kind, (iota((8, LANES), 0) == sign).astype(F32).astype(BF16))
+        for at in range(per_sign):
+            block = sign * per_sign + at
+            chunk = [2 * ((at * (LANES // HALF) + i) * NVX + HALF * sign) for i in range(LANES // HALF)]
+            part = jnp.concatenate([lri[c : c + 2 * HALF, :] for c in chunk], axis=0)
+            pick = (iota((LANES, 2 * LANES), 1) == 2 * iota((LANES, 2 * LANES), 0) + 1 - sign).astype(F32).astype(BF16)
+            xw[block] = nt(flip, nn(pick, part).astype(BF16))
+            part = jnp.concatenate([bti[c : c + 2 * HALF, :] for c in chunk], axis=0)
+            row, col = iota((16, cells_x), 0), iota((16, cells_x), 1)
+            order = (col == (row if sign else cells_x - 1 - row)).astype(F32).astype(BF16)
+            pick = (iota((2 * LANES, LANES), 0) == 2 * iota((2 * LANES, LANES), 1) + 1 - info[1]).astype(F32).astype(BF16)
+            yw[block] = nn(nt(order, part).astype(BF16), pick)[:cells_x]
+        for at in range(0, per_sign, 2):
+            ix, iy = lane_ints(info[0], sign, at * LANES, (1, 2 * LANES))
+            both = (sign * per_sign + at) // 2
+            r[both] = spread(tr[sign], (jnp.abs(ix) + jnp.abs(iy)) // 2, NVX).reshape(cells_x, cells_y, 2 * LANES)
+            for xt in range(cells_x):
+                x = xt if sign else cells_x - 1 - xt
+                value = nt(flip, pt[x, sign, at * LANES : (at + 2) * LANES, :])
+                for i in range(2):
+                    g[2 * both + i, 1 + xt, 8:, :] = value[:, i * LANES : (i + 1) * LANES]
+
+
+def first_kernel(kindy, same, other, relax, pair0, pair1, yrecv, xw, yw, kx, r, g_in,
+                 g, s, xmsg0, xmsg1, ymsg, flux, ta, tb, fa, fb):
+    blocks, slots, padded, _ = g.shape
+    cells_x, cells_y = slots - 1, padded - 8
+    per_sign = blocks // 2
+    local_ky = per_sign * LANES // HALF
+    info = device_info(local_ky)
     first_ky, up = info[0], info[1] == 1
     total = [same[q] + other[q] for q in range(4)]
-    tau = relax[...]
     p = newton_params(total[0] * WEIGHT, total[1] * (WEIGHT * UNIT), total[2] * (WEIGHT * UNIT),
                       total[3] * (WEIGHT * UNIT * UNIT / 2.0))
-    lead = p[0] - jnp.log(tau)
+    lead = p[0] - jnp.log(relax[...])
     flip = flip_matrix(up, cells_y).astype(BF16)
-    local_ky = count // HALF
     vx = (2 * iota((NVX, cells_y), 0) - (NVX - 1)).astype(F32) * UNIT
     vy = (2 * (first_ky + iota((local_ky, cells_y), 0)) - (NVX - 1)).astype(F32) * UNIT
-    steps = iota((NVX, cells_y), 0).astype(F32) * STEP
     half_p3 = p[3] * 0.5
-    base = 1.0 / TIME_STEP + 1.0 / tau
     for x in range(cells_x):
         here = slice(x, x + 1)
         arg = vy * (p[2][here] + vy * half_p3[here])
         top = jnp.max(arg, axis=0, keepdims=True)
-        along_y = jnp.exp(arg - top)
-        along_x = jnp.exp((lead[here] + top) + vx * (p[1][here] + vx * half_p3[here]))
-        inverse = 1.0 / (base[here] + steps)
-        for table, ref in ((along_x, ta), (along_y, tb), (inverse, tr)):
-            wide = nt(flip, jnp.concatenate(pieces(table), axis=0).astype(BF16)).astype(BF16)
-            ref[1, x * cells_y : (x + 1) * cells_y, :] = wide
-            ref[0, (cells_x - 1 - x) * cells_y : (cells_x - x) * cells_y, :] = wide
-    kind = jnp.concatenate([kindx[1:2], kindx[0:1], jnp.zeros((6, cells_y), jnp.int32)], axis=0).astype(F32)
-    kind = nt(kind.astype(BF16), flip).astype(BF16)
-    for sign in range(2):
-        kx[sign] = tn(kind, (iota((8, LANES), 0) == sign).astype(F32).astype(BF16))
-        for at in range(per_sign):
+        transposed(flip, jnp.exp(arg - top), tb, x, cells_x, cells_y)
+        arg = (lead[here] + top) + vx * (p[1][here] + vx * half_p3[here])
+        transposed(flip, jnp.exp(arg), ta, x, cells_x, cells_y)
+    for sign in range(2):
+        fa[...] = spread(ta[sign], iota((1, LANES), 1) % HALF + HALF * sign, NVX)
+        for at in range(0, per_sign, 2):
             block = sign * per_sign + at
-            chunk = [(at * (LANES // HALF) + i) * NVX + HALF * sign for i in range(LANES // HALF)]
-            part = jnp.concatenate(
-                [lri[c : c + HALF, (1 - sign) * cells_y : (2 - sign) * cells_y] for c in chunk], axis=0)
-            xw[block] = nt(flip, part)
-            part = jnp.concatenate([bti[c : c + HALF, :] for c in chunk], axis=0)
-            row, col = iota((16, cells_x), 0), iota((16, cells_x), 1)
-            order = (col == (row if sign else cells_x - 1 - row)).astype(F32).astype(BF16)
-            yw[block] = nt(order, part)[:cells_x]
-    def spread(ref, sign, choice, size):
-        row = iota((3 * size, LANES), 0) % size
-        return nn(ref[sign], (row == choice).astype(F32).astype(BF16))
-
-    for sign in range(2):
-        fa[...] = spread(ta, sign, iota((1, LANES), 1) % HALF + HALF * sign, NVX)
-        for at in range(per_sign):
-            block = sign * per_sign + at
-            ix, iy = lane_ints(first_ky, sign, at * LANES, (1, LANES))
-            r[block] = spread(tr, sign, (jnp.abs(ix) + jnp.abs(iy)) // 2, NVX).reshape(cells_x, cells_y, LANES)
-            fb[...] = spread(tb, sign, iota((1, LANES), 1) // HALF + at * (LANES // HALF), local_ky)
+            fb[...] = spread(tb[sign], iota((1, 2 * LANES), 1) // HALF + at * (LANES // HALF), local_ky)
             for xt in range(cells_x):
-                x = xt if sign else cells_x - 1 - xt
                 here = slice(xt * cells_y, (xt + 1) * cells_y)
-                value = nt(flip, pt[x, sign, at * LANES : (at + 1) * LANES, :])
-                g[block, 1 + xt, 8:, :] = value
-                s[block, xt] = value * (1.0 / TIME_STEP) + fa[here, :] * fb[here, :]
+                for i in range(2):
+                    maxwell = fa[here, :] * fb[here, i * LANES : (i + 1) * LANES]
+                    s[block + i, xt] = g[block + i, 1 + xt, 8:, :] * (1.0 / TIME_STEP) + maxwell
 
     def xin(block):
         at = block % per_sign
@@ -334,11 +392,12 @@
     send_out(info, g, (xmsg0, xmsg1), ymsg, flux)
 
 
-def next_kernel(last, info, kindy, same, other, pair0, pair1, yrecv, xw, yw, kx, s, r, g_in, *outs):
+def next_kernel(last, kindy, same, other, pair0, pair1, yrecv, xw, yw, kx, s, r, g_in, *outs):
     blocks, slots, padded, _ = g_in.shape
     per_sign = blocks // 2
+    info = device_info(per_sign * LANES // HALF)
     if last:
-        out, g, rows = outs
+        out, g, rows, staged, sems = outs
     else:
         g, xmsg0, xmsg1, ymsg, flux = outs
 
@@ -350,7 +409,7 @@
         return yrecv[block].astype(F32)
 
     fill_inflow(info, kindy, same, other, g, xin, yin, xw, yw, kx)
-    sweep(info, g, s, r)
+    sweep(info, g, s, r, "rim")
     if not last:
         send_out(info, g, (xmsg0, xmsg1), ymsg, flux)
         return
@@ -358,6 +417,7 @@
     flip = flip_matrix(info[1] == 1, cells_y).astype(BF16)
 
     span = HALF * cells_x
+    copies = []
     for sign in range(2):
         for at in range(per_sign):
             for x in range(cells_x):
@@ -365,20 +425,27 @@
                 value = g[sign * per_sign + at, 1 + xt, 8:, :].astype(BF16)
                 rows[pl.ds(x, LANES, stride=cells_x), :] = tn(value, flip)
             for i in range(LANES // HALF):
-                start = ((at * (LANES // HALF) + i) * NVX + sign * HALF) * cells_x
-                out[start : start + span, :] = rows[i * span : (i + 1) * span, :].astype(BF16)
-
-
-def call(kernel, outs, n_smem, ins, scratch=(), aliases=None, mib=20):
-    vmem = pl.BlockSpec(memory_space=pltpu.VMEM)
-    smem = pl.BlockSpec(memory_space=pltpu.SMEM)
+                chunk = (at * (LANES // HALF) + i) * 2 + sign
+                staged[chunk * span : (chunk + 1) * span, :] = rows[i * span : (i + 1) * span, :].astype(BF16)
+                copies.append(pltpu.make_async_copy(
+                    staged.at[pl.ds(chunk * span, span), :], out.at[pl.ds(chunk * span, span), :], sems.at[chunk]))
+                copies[-1].start()
+    for copy in copies:
+        copy.wait()
+
+
+def call(kernel, outs, ins, smem=(), scratch=(), aliases=None, mib=20, far_in=(), far_out=(), cost=None):
+    here = pl.BlockSpec(memory_space=pltpu.VMEM)
+    scalar = pl.BlockSpec(memory_space=pltpu.SMEM)
+    far = pl.BlockSpec(memory_space=pltpu.HBM)
     return pl.pallas_call(
         kernel,
         out_shape=outs,
-        in_specs=[smem] * n_smem + [vmem] * (len(ins) - n_smem),
-        out_specs=jax.tree.map(lambda _: vmem, outs),
+        in_specs=[scalar if i in smem else far if i in far_in else here for i in range(len(ins))],
+        out_specs=tuple(far if i in far_out else here for i in range(len(outs))),
         scratch_shapes=list(scratch),
         input_output_aliases=aliases or {},
+        cost_estimate=cost,
         compiler_params=pltpu.CompilerParams(vmem_limit_bytes=mib << 20),
     )(*ins)
 
@@ -390,11 +457,6 @@
     per_sign = count // LANES
     blocks = 2 * per_sign
     nvel, ngx, ngy = lax.axis_size("vel"), lax.axis_size("gx"), lax.axis_size("gy")
-    v, ix, iy = lax.axis_index("vel"), lax.axis_index("gx"), lax.axis_index("gy")
-    up = v >= nvel // 2
-    y_wall = jnp.where(up, iy == 0, iy == ngy - 1)
-    info = jnp.stack([v * local_ky, up.astype(jnp.int32), (ix == 0).astype(jnp.int32),
-                      (ix == ngx - 1).astype(jnp.int32), y_wall.astype(jnp.int32), (ix % 2 == 0).astype(jnp.int32)])
     def pairs(count, start):
         low = range(start, count - 1, 2)
         return [(i, i + 1) for i in low] + [(i + 1, i) for i in low]
@@ -414,44 +476,53 @@
 
     assert ngy == 2 and nvel & (nvel - 1) == 0, "mesh shape"
     sds = jax.ShapeDtypeStruct
-    pay, ymsg, pt, xmsg0, xmsg1 = call(
+    staging = [pltpu.VMEM((LANES * cells_x, cells_y), F32), pltpu.VMEM((vel_rows * cells_x, cells_y), BF16),
+               pltpu.SemaphoreType.DMA((vel_rows // HALF,))]
+    def far(a):
+        return pltpu.with_memory_space_constraint(a, pltpu.HBM)
+
+    pay, ymsg, pt, xmsg0, xmsg1, relax, kindx = call(
         moments_kernel,
         (sds((7, 8, LANES), F32), sds((2, cells_x, count), BF16), sds((cells_x, 2, count, cells_y), BF16),
-         sds((count, cells_y), BF16), sds((count, cells_y), BF16)),
-        1, (info, previous.reshape(vel_rows * cells_x, cells_y)),
-        scratch=[pltpu.VMEM((LANES * cells_x, cells_y), F32)], mib=8)
+         sds((count, cells_y), BF16), sds((count, cells_y), BF16), sds(relax_time.shape, F32), sds(left_right_kind.shape, jnp.int32)),
+        (far(previous.reshape(vel_rows * cells_x, cells_y)), far(relax_time), far(left_right_kind)),
+        scratch=staging + [pltpu.SemaphoreType.DMA((2,))], mib=10, far_in=(0, 1, 2))
     halo = swap_x(xmsg0, xmsg1)
     yrecv = swap_y(ymsg)
     sums = sum_vel(pay)
-    lri = left_right_inflow.reshape(vel_rows, 2 * cells_y)
-    bti = jnp.where(up, bottom_top_inflow[:, 0, :], bottom_top_inflow[:, 1, :])
+    lri = left_right_inflow.reshape(2 * vel_rows, cells_y)
+    bti = bottom_top_inflow.reshape(2 * vel_rows, cells_x)
     g_shape = sds((blocks, cells_x + 1, cells_y + 8, LANES), F32)
     full = sds((blocks, cells_x, cells_y, LANES), F32)
+    wide = sds((blocks // 2, cells_x, cells_y, 2 * LANES), F32)
     messages = (sds((per_sign, cells_y, LANES), BF16), sds((per_sign, cells_y, LANES), BF16),
                 sds((blocks, cells_x, LANES), BF16), sds((3, 8, LANES), F32))
-    g, s, r, xw, yw, kx, xmsg0, xmsg1, ymsg, flux = call(
+    work = pl.CostEstimate(flops=8 * vel_rows * cells_x * cells_y, bytes_accessed=16 * vel_rows * cells_x * cells_y, transcendentals=0)
+    g, r, xw, yw, kx = call(
+        table_kernel,
+        (g_shape, wide, sds((blocks, cells_y, LANES), F32), sds((blocks, cells_x, LANES), F32), sds((2, cells_y, LANES), F32)),
+        (relax, kindx, pt, lri, bti),
+        scratch=[pltpu.VMEM((2, cells_x * cells_y, 3 * NVX), BF16)], mib=22, cost=work)
+    g, s, xmsg0, xmsg1, ymsg, flux = call(
         first_kernel,
-        (g_shape, full, full, sds((blocks, cells_y, LANES), F32), sds((blocks, cells_x, LANES), F32),
-         sds((2, cells_y, LANES), F32)) + messages,
-        2,
-        (info, bottom_top_kind, *sums, relax_time, left_right_kind, pt, *halo, yrecv, lri, bti),
+        (g_shape, full) + messages,
+        (bottom_top_kind, *sums, relax, *halo, yrecv, xw, yw, kx, r, g), smem=(0,), aliases={11: 0},
         scratch=[
             pltpu.VMEM((2, cells_x * cells_y, 3 * NVX), BF16), pltpu.VMEM((2, cells_x * cells_y, 3 * local_ky), BF16),
-            pltpu.VMEM((2, cells_x * cells_y, 3 * NVX), BF16), pltpu.VMEM((cells_x * cells_y, LANES), F32),
-            pltpu.VMEM((cells_x * cells_y, LANES), F32)], mib=24)
+            pltpu.VMEM((cells_x * cells_y, LANES), F32), pltpu.VMEM((cells_x * cells_y, 2 * LANES), F32)], mib=24)
     for number in range(1, SWEEPS):
         halo = swap_x(xmsg0, xmsg1)
         yrecv = swap_y(ymsg)
         sums = sum_vel(flux)
-        last = number == SWEEPS - 1
-        ins = (info, bottom_top_kind, *sums, *halo, yrecv, xw, yw, kx, s, r, g)
-        if last:
+        g = call(inner_kernel, (g_shape,), (s, r, g), aliases={2: 0}, mib=20, cost=work)[0]
+        ins = (bottom_top_kind, *sums, *halo, yrecv, xw, yw, kx, s, r, g)
+        if number == SWEEPS - 1:
             out, _ = call(functools.partial(next_kernel, True),
-                          (sds((vel_rows * cells_x, cells_y), BF16), g_shape), 2, ins, aliases={12: 1},
-                          scratch=[pltpu.VMEM((LANES * cells_x, cells_y), F32)], mib=22)
+                          (sds((vel_rows * cells_x, cells_y), BF16), g_shape), ins, smem=(0,), aliases={11: 1},
+                          scratch=staging, mib=22, far_out=(0,))
         else:
             g, xmsg0, xmsg1, ymsg, flux = call(
-                functools.partial(next_kernel, False), (g_shape,) + messages, 2, ins, aliases={12: 0}, mib=22)
+                functools.partial(next_kernel, False), (g_shape,) + messages, ins, smem=(0,), aliases={11: 0}, mib=22)
     return out.reshape(vel_rows, cells_x, cells_y)
 
 

time: 60.1 us -> 53.1 us (0.88)
  starting transfers between devices: 25 us -> 22.2 us
  Pallas kernels: 21.8 us -> 19.8 us
  local copies, waits for them, and re-layouts: 3.9 us -> 2.12 us
    ppermute x4, starting transfers between devices: 5.99 us -> 3.09 us  [sum_vel(): return (a, lax.ppermute(a, 'vel', [(i, i ^ reach) for i in range(nvel)]))]
    pallas_call x5 -> x9, Pallas kernels: 21.8 us -> 19.8 us  [call(): pl.pallas_call(kernel, out_shape=outs, in_specs=[scalar if i in smem else...]
    ppermute x4, starting transfers between devices: 5.57 us -> 4.07 us  [swap_y(): return lax.ppermute(a, 'gy', pairs(ngy, 0))]
    ppermute x4, starting transfers between devices: 10.6 us -> 12.1 us  [swap_x(): lax.ppermute(first, 'gx', pairs(ngx, 0))]
    ppermute x4, waiting for transfers between devices: 4.39 us -> 3.18 us  [sum_vel(): return (a, lax.ppermute(a, 'vel', [(i, i ^ reach) for i in range(nvel)]))]
    ppermute x4, waiting for transfers between devices: 0.98 us -> 2.13 us  [sum_vel(): a = a + lax.ppermute(a, 'vel', [(i, i ^ reach) for i in range(nvel)])]
    slice x3 -> x0, local copies, waits for them, and re-layouts: 1.08 us -> none  [body(): bti = jnp.where(up, bottom_top_inflow[:, 0, :], bottom_top_inflow[:, 1, :])]
    unnamed x9 -> x5, local copies, waits for them, and re-layouts: 2.73 us -> 2.12 us
  transfers between devices with their start and end apart: 20 -> 20, of which waited for: 10 -> 10; matrix products, arithmetic and copies ran while one was open for 4% -> 2% of each run, Pallas kernels for 0% -> 10%
where the time goes in v2:
time: 53.1 us; the launch traced here: 52.7 us
  starting transfers between devices  22.2 us (42%)
  Pallas kernels  19.8 us (37%)
  waiting for transfers between devices  8.47 us (16%)
  local copies, waits for them, and re-layouts  2.12 us (4%)
    pallas_call x9, Pallas kernels, call(): pl.pallas_call(kernel, out_shape=outs, in_specs=[scalar if i in smem else...  19.8 us
    ppermute x4, starting transfers between devices, swap_x(): lax.ppermute(first, 'gx', pairs(ngx, 0))  12.1 us
    ppermute x4, starting transfers between devices, swap_y(): return lax.ppermute(a, 'gy', pairs(ngy, 0))  4.07 us
    ppermute x4, waiting for transfers between devices, sum_vel(): return (a, lax.ppermute(a, 'vel', [(i, i ^ reach) for i in range(nvel)]))  3.18 us
    ppermute x4, waiting for transfers between devices, swap_y(): return lax.ppermute(a, 'gy', pairs(ngy, 0))  3.14 us
    ppermute x4, starting transfers between devices, sum_vel(): return (a, lax.ppermute(a, 'vel', [(i, i ^ reach) for i in range(nvel)]))  3.09 us
    ppermute x4, starting transfers between devices, swap_x(): lax.ppermute(second, 'gx', pairs(ngx, 1))  2.63 us
    ppermute x4, waiting for transfers between devices, sum_vel(): a = a + lax.ppermute(a, 'vel', [(i, i ^ reach) for i in range(nvel)])  2.13 us
  transfers between devices with their start and end apart: 20, of which 10 were waited for; matrix products, arithmetic and copies ran while one was open for 2% of the time, Pallas kernels for 10%

profile of v2, /device:TPU:0, one launch (start us, length us, event | category | flops | bytes accessed | tf_op | source)
XLA Modules:
  0.0 52.7 jit_solution(12180301226920982210)
XLA Ops:
  0.0 3.3 %shard_map.64 = (f32[7,8,128]{2,1,0:T(8,128)S(1)}, bf16[2,8,512]{2,1,0:T(8,128)(2,1)S(1)}, bf16[8,2,512,128]{3,2,1,0:T(8,128)(2,1)S(1)}, bf16[512,128]{1,0:T(8,1...) custom-call(bf16[8192,128]{1,0:T(8,128)(2,1)} %bitcast.6, ...), custom_call_target="tpu_custom_call" | custom-call | tf_op jit(solution)/shard_map/pallas_call | solution.py:441
  3.3 3.1 %collective-permute-start.2 = (bf16[512,128]{1,0:T(8,128)(2,1)S(1)}, bf16[512,128]{1,0:T(8,128)(2,1)S(1)}, u32[]{:S(2)}, u32[]{:S(2)}) collective-permute-start(bf16[512,128]{1,0:T(8,128)(2,1)S(1)} %get-tuple-element.36), channel_id=1, source_target_pairs={{0,2},{4,6},{2,0},{6,4},{1,3},{5,7},{3,1},{7,5},{8,10},{12,14},{10... | collective-permute-start | bytes 393224 | tf_op jit(solution)/shard_map/ppermute | solution.py:465
  6.4 0.7 %collective-permute-start.3 = (bf16[512,128]{1,0:T(8,128)(2,1)S(1)}, bf16[512,128]{1,0:T(8,128)(2,1)S(1)}, u32[]{:S(2)}, u32[]{:S(2)}) collective-permute-start(bf16[512,128]{1,0:T(8,128)(2,1)S(1)} %get-tuple-element.37), channel_id=1, source_target_pairs={{2,4},{4,2},{3,5},{5,3},{10,12},{12,10},{11,13},{13,11},{18,20},{2... | collective-permute-start | bytes 393224 | tf_op jit(solution)/shard_map/ppermute | solution.py:465
  7.1 0.1 collective-permute-start
  7.2 1.2 %collective-permute-done = f32[7,8,128]{2,1,0:T(8,128)S(1)} collective-permute-done((f32[7,8,128]{2,1,0:T(8,128)S(1)}, f32[7,8,128]{2,1,0:T(8,128)S(1)}, u32[]{:S(2)}, u32[]{:S(2)}) %collective-permute-start) | collective-permute-done | bytes 28704 | tf_op jit(solution)/shard_map/ppermute | solution.py:473
  8.3 1.5 %collective-permute-start.1 = (f32[7,8,128]{2,1,0:T(8,128)S(1)}, f32[7,8,128]{2,1,0:T(8,128)S(1)}, u32[]{:S(2)}, u32[]{:S(2)}) collective-permute-start(f32[7,8,128]{2,1,0:T(8,128)S(1)} %add.12.same), channel_id=1, source_target_pairs={{0,16},{8,24},{16,0},{24,8},{1,17},{9,25},{17,1},{25,9},{2,18},{10... | collective-permute-start | bytes 86024 | tf_op jit(solution)/shard_map/ppermute | solution.py:475
  9.8 1.5 %collective-permute-start.4 = (bf16[2,8,512]{2,1,0:T(8,128)(2,1)S(1)}, bf16[2,8,512]{2,1,0:T(8,128)(2,1)S(1)}, u32[]{:S(2)}, u32[]{:S(2)}) collective-permute-start(bf16[2,8,512]{2,1,0:T(8,128)(2,1)S(1)} %get-tuple-element.38), channel_id=1, source_target_pairs={{0,1},{1,0},{2,3},{3,2},{4,5},{5,4},{6,7},{7,6},{8,9},{9,8},{10,11... | collective-permute-start | bytes 49160 | tf_op jit(solution)/shard_map/ppermute | solution.py:468
  11.4 1.1 %copy.14 = bf16[1024,2,8]{2,1,0:T(2,128)(2,1)S(1)} copy(bf16[1024,2,8]{0,2,1:T(8,128)(2,1)} %param.11) | data formatting | bytes 65536 | tf_op args[5]
  12.4 0.0 copy-start
  12.5 1.0 %copy-done = bf16[1024,2,128]{2,1,0:T(2,128)(2,1)S(1)} copy-done((bf16[1024,2,128]{2,1,0:T(2,128)(2,1)S(1)}, bf16[1024,2,128]{2,1,0:T(2,128)(2,1)}, u32[]{:S(2)}) %copy-start) | copy-done | bytes 524312
  13.5 2.4 %shard_map.65 = (f32[8,9,136,128]{3,2,1,0:T(8,128)S(1)}, f32[4,8,128,256]{3,2,1,0:T(8,128)S(1)}, f32[8,128,128]{2,1,0:T(8,128)S(1)}, f32[8,8,128]{2,1,0:T(8,128)S(1)}, f32[2,128,128]{2,1,0:T(8,128)S(1)}) custom-call(f32[8,128]{1,0:T(8,128)S(1)} %get-tuple-element.35.relax, s32[2,128]{1,0:T(2,128)S(1)} %get-tuple-element.39.kindx, ...), custom_call_target="tpu_custom_call" | custom-call | flops 8388608 | bytes 16777216 | tf_op jit(solution)/shard_map/pallas_call | solution.py:441
  15.8 0.0 collective-permute-done.4.yrecv
  15.9 0.0 collective-permute-done.1.other
  15.9 0.0 collective-permute-done.3.pair1
  15.9 4.5 %shard_map.66 = (f32[8,9,136,128]{3,2,1,0:T(8,128)S(1)}, f32[8,8,128,128]{3,2,1,0:T(8,128)S(1)}, bf16[4,128,128]{2,1,0:T(8,128)(2,1)S(1)}, bf16[4,128,128]{2,1,0...) custom-call(s32[2,8]{1,0:T(2,128)S(1)} %copy-done.1, ...), custom_call_target="tpu_custom_call", output_to_operand_aliasing={{0}: (11, {})} | custom-call | tf_op jit(solution)/shard_map/pallas_call | solution.py:441
  20.4 4.4 %collective-permute-start.7 = (bf16[4,128,128]{2,1,0:T(8,128)(2,1)S(1)}, bf16[4,128,128]{2,1,0:T(8,128)(2,1)S(1)}, u32[]{:S(2)}, u32[]{:S(2)}) collective-permute-start(bf16[4,128,128]{2,1,0:T(8,128)(2,1)S(1)} %get-tuple-element.47), channel_id=1, source_target_pairs={{0,2},{4,6},{2,0},{6,4},{1,3},{5,7},{3,1},{7,5},{8,10},{12,14},{10... | collective-permute-start | bytes 393224 | tf_op jit(solution)/shard_map/ppermute | solution.py:465
  24.8 0.7 %collective-permute-start.8 = (bf16[4,128,128]{2,1,0:T(8,128)(2,1)S(1)}, bf16[4,128,128]{2,1,0:T(8,128)(2,1)S(1)}, u32[]{:S(2)}, u32[]{:S(2)}) collective-permute-start(bf16[4,128,128]{2,1,0:T(8,128)(2,1)S(1)} %get-tuple-element.48), channel_id=1, source_target_pairs={{2,4},{4,2},{3,5},{5,3},{10,12},{12,10},{11,13},{13,11},{18,20},{2... | collective-permute-start | bytes 393224 | tf_op jit(solution)/shard_map/ppermute | solution.py:465
  25.5 0.1 collective-permute-start.5
  25.6 0.6 %collective-permute-start.9 = (bf16[8,8,128]{2,1,0:T(8,128)(2,1)S(1)}, bf16[8,8,128]{2,1,0:T(8,128)(2,1)S(1)}, u32[]{:S(2)}, u32[]{:S(2)}) collective-permute-start(bf16[8,8,128]{2,1,0:T(8,128)(2,1)S(1)} %get-tuple-element.49), channel_id=1, source_target_pairs={{0,1},{1,0},{2,3},{3,2},{4,5},{5,4},{6,7},{7,6},{8,9},{9,8},{10,11... | collective-permute-start | bytes 49160 | tf_op jit(solution)/shard_map/ppermute | solution.py:468
  26.1 0.6 %collective-permute-done.5 = f32[3,8,128]{2,1,0:T(8,128)S(1)} collective-permute-done((f32[3,8,128]{2,1,0:T(8,128)S(1)}, f32[3,8,128]{2,1,0:T(8,128)S(1)}, u32[]{:S(2)}, u32[]{:S(2)}) %collective-permute-start.5) | collective-permute-done | bytes 12320 | tf_op jit(solution)/shard_map/ppermute | solution.py:473
  26.7 0.5 %collective-permute-start.6 = (f32[3,8,128]{2,1,0:T(8,128)S(1)}, f32[3,8,128]{2,1,0:T(8,128)S(1)}, u32[]{:S(2)}, u32[]{:S(2)}) collective-permute-start(f32[3,8,128]{2,1,0:T(8,128)S(1)} %add.13.same), channel_id=1, source_target_pairs={{0,16},{8,24},{16,0},{24,8},{1,17},{9,25},{17,1},{25,9},{2,18},{10... | collective-permute-start | bytes 36872 | tf_op jit(solution)/shard_map/ppermute | solution.py:475
  27.3 1.1 %shard_map.67.g_in = f32[8,9,136,128]{3,2,1,0:T(8,128)S(1)} custom-call(f32[8,8,128,128]{3,2,1,0:T(8,128)S(1)} %get-tuple-element.50.s, f32[4,8,128,256]{3,2,1,0:T(8,128)S(1)} %get-tuple-element.44.r, f32[8,9,136,128]{3,2,1,0:T(8,128)S(1)} %get-tuple-element.51.g_in), custom_call_target="tpu_custom_call", output_to_operand_aliasing={{}: (2, {})} | custom-call | flops 8388608 | bytes 16777216 | tf_op jit(solution)/shard_map/pallas_call | solution.py:441
  28.3 1.0 %collective-permute-done.9.yrecv = bf16[8,8,128]{2,1,0:T(8,128)(2,1)S(1)} collective-permute-done((bf16[8,8,128]{2,1,0:T(8,128)(2,1)S(1)}, bf16[8,8,128]{2,1,0:T(8,128)(2,1)S(1)}, u32[]{:S(2)}, u32[]{:S(2)}) %collective-permute-start.9) | collective-permute-done | bytes 16416 | tf_op jit(solution)/shard_map/ppermute | solution.py:468
  29.4 1.1 %collective-permute-done.6.other = f32[3,8,128]{2,1,0:T(8,128)S(1)} collective-permute-done((f32[3,8,128]{2,1,0:T(8,128)S(1)}, f32[3,8,128]{2,1,0:T(8,128)S(1)}, u32[]{:S(2)}, u32[]{:S(2)}) %collective-permute-start.6) | collective-permute-done | bytes 12320 | tf_op jit(solution)/shard_map/ppermute | solution.py:475
  30.4 0.0 collective-permute-done.7.pair0
  30.4 1.6 %shard_map.68 = (f32[8,9,136,128]{3,2,1,0:T(8,128)S(1)}, bf16[4,128,128]{2,1,0:T(8,128)(2,1)S(1)}, bf16[4,128,128]{2,1,0:T(8,128)(2,1)S(1)}, bf16[8,8,128]{2,1,0:T(8,128)(2,1)S(1)}, f32[3,8,128]{2,1,0:T(8,128)S(1)}) custom-call(s32[2,8]{1,0:T(2,128)S(1)} %copy-done.1, f32[3,8,128]{2,1,0:T(8,128)S(1)} %add.13.same, ...), custom_call_target="tpu_custom_call", output_to_operand_aliasing={{0}: (11, {})} | custom-call | tf_op jit(solution)/shard_map/pallas_call | solution.py:441
  32.0 1.3 %collective-permute-start.12 = (bf16[4,128,128]{2,1,0:T(8,128)(2,1)S(1)}, bf16[4,128,128]{2,1,0:T(8,128)(2,1)S(1)}, u32[]{:S(2)}, u32[]{:S(2)}) collective-permute-start(bf16[4,128,128]{2,1,0:T(8,128)(2,1)S(1)} %get-tuple-element.53), channel_id=1, source_target_pairs={{0,2},{4,6},{2,0},{6,4},{1,3},{5,7},{3,1},{7,5},{8,10},{12,14},{10... | collective-permute-start | bytes 393224 | tf_op jit(solution)/shard_map/ppermute | solution.py:465
  33.3 0.7 %collective-permute-start.13 = (bf16[4,128,128]{2,1,0:T(8,128)(2,1)S(1)}, bf16[4,128,128]{2,1,0:T(8,128)(2,1)S(1)}, u32[]{:S(2)}, u32[]{:S(2)}) collective-permute-start(bf16[4,128,128]{2,1,0:T(8,128)(2,1)S(1)} %get-tuple-element.54), channel_id=1, source_target_pairs={{2,4},{4,2},{3,5},{5,3},{10,12},{12,10},{11,13},{13,11},{18,20},{2... | collective-permute-start | bytes 393224 | tf_op jit(solution)/shard_map/ppermute | solution.py:465
  33.9 0.1 collective-permute-start.10
  34.0 1.0 %collective-permute-start.14 = (bf16[8,8,128]{2,1,0:T(8,128)(2,1)S(1)}, bf16[8,8,128]{2,1,0:T(8,128)(2,1)S(1)}, u32[]{:S(2)}, u32[]{:S(2)}) collective-permute-start(bf16[8,8,128]{2,1,0:T(8,128)(2,1)S(1)} %get-tuple-element.55), channel_id=1, source_target_pairs={{0,1},{1,0},{2,3},{3,2},{4,5},{5,4},{6,7},{7,6},{8,9},{9,8},{10,11... | collective-permute-start | bytes 49160 | tf_op jit(solution)/shard_map/ppermute | solution.py:468
  35.0 0.2 collective-permute-done.10
  35.2 0.5 %collective-permute-start.11 = (f32[3,8,128]{2,1,0:T(8,128)S(1)}, f32[3,8,128]{2,1,0:T(8,128)S(1)}, u32[]{:S(2)}, u32[]{:S(2)}) collective-permute-start(f32[3,8,128]{2,1,0:T(8,128)S(1)} %add.14.same), channel_id=1, source_target_pairs={{0,16},{8,24},{16,0},{24,8},{1,17},{9,25},{17,1},{25,9},{2,18},{10... | collective-permute-start | bytes 36872 | tf_op jit(solution)/shard_map/ppermute | solution.py:475
  35.7 1.1 %shard_map.69.g_in = f32[8,9,136,128]{3,2,1,0:T(8,128)S(1)} custom-call(f32[8,8,128,128]{3,2,1,0:T(8,128)S(1)} %get-tuple-element.50.s, f32[4,8,128,256]{3,2,1,0:T(8,128)S(1)} %get-tuple-element.44.r, f32[8,9,136,128]{3,2,1,0:T(8,128)S(1)} %get-tuple-element.56.g_in), custom_call_target="tpu_custom_call", output_to_operand_aliasing={{}: (2, {})} | custom-call | flops 8388608 | bytes 16777216 | tf_op jit(solution)/shard_map/pallas_call | solution.py:441
  36.8 1.1 %collective-permute-done.14.yrecv = bf16[8,8,128]{2,1,0:T(8,128)(2,1)S(1)} collective-permute-done((bf16[8,8,128]{2,1,0:T(8,128)(2,1)S(1)}, bf16[8,8,128]{2,1,0:T(8,128)(2,1)S(1)}, u32[]{:S(2)}, u32[]{:S(2)}) %collective-permute-start.14) | collective-permute-done | bytes 16416 | tf_op jit(solution)/shard_map/ppermute | solution.py:468
  37.8 1.1 %collective-permute-done.11.other = f32[3,8,128]{2,1,0:T(8,128)S(1)} collective-permute-done((f32[3,8,128]{2,1,0:T(8,128)S(1)}, f32[3,8,128]{2,1,0:T(8,128)S(1)}, u32[]{:S(2)}, u32[]{:S(2)}) %collective-permute-start.11) | collective-permute-done | bytes 12320 | tf_op jit(solution)/shard_map/ppermute | solution.py:475
  38.9 1.6 %shard_map.70 = (f32[8,9,136,128]{3,2,1,0:T(8,128)S(1)}, bf16[4,128,128]{2,1,0:T(8,128)(2,1)S(1)}, bf16[4,128,128]{2,1,0:T(8,128)(2,1)S(1)}, bf16[8,8,128]{2,1,0:T(8,128)(2,1)S(1)}, f32[3,8,128]{2,1,0:T(8,128)S(1)}) custom-call(s32[2,8]{1,0:T(2,128)S(1)} %copy-done.1, f32[3,8,128]{2,1,0:T(8,128)S(1)} %add.14.same, ...), custom_call_target="tpu_custom_call", output_to_operand_aliasing={{0}: (11, {})} | custom-call | tf_op jit(solution)/shard_map/pallas_call | solution.py:441
  40.5 3.3 %collective-permute-start.17 = (bf16[4,128,128]{2,1,0:T(8,128)(2,1)S(1)}, bf16[4,128,128]{2,1,0:T(8,128)(2,1)S(1)}, u32[]{:S(2)}, u32[]{:S(2)}) collective-permute-start(bf16[4,128,128]{2,1,0:T(8,128)(2,1)S(1)} %get-tuple-element.58), channel_id=1, source_target_pairs={{0,2},{4,6},{2,0},{6,4},{1,3},{5,7},{3,1},{7,5},{8,10},{12,14},{10... | collective-permute-start | bytes 393224 | tf_op jit(solution)/shard_map/ppermute | solution.py:465
  43.7 0.7 %collective-permute-start.18 = (bf16[4,128,128]{2,1,0:T(8,128)(2,1)S(1)}, bf16[4,128,128]{2,1,0:T(8,128)(2,1)S(1)}, u32[]{:S(2)}, u32[]{:S(2)}) collective-permute-start(bf16[4,128,128]{2,1,0:T(8,128)(2,1)S(1)} %get-tuple-element.59), channel_id=1, source_target_pairs={{2,4},{4,2},{3,5},{5,3},{10,12},{12,10},{11,13},{13,11},{18,20},{2... | collective-permute-start | bytes 393224 | tf_op jit(solution)/shard_map/ppermute | solution.py:465
  44.4 0.1 collective-permute-start.15
  44.5 1.0 %collective-permute-start.19 = (bf16[8,8,128]{2,1,0:T(8,128)(2,1)S(1)}, bf16[8,8,128]{2,1,0:T(8,128)(2,1)S(1)}, u32[]{:S(2)}, u32[]{:S(2)}) collective-permute-start(bf16[8,8,128]{2,1,0:T(8,128)(2,1)S(1)} %get-tuple-element.60), channel_id=1, source_target_pairs={{0,1},{1,0},{2,3},{3,2},{4,5},{5,4},{6,7},{7,6},{8,9},{9,8},{10,11... | collective-permute-start | bytes 49160 | tf_op jit(solution)/shard_map/ppermute | solution.py:468
  45.5 0.2 collective-permute-done.15
  45.6 0.5 %collective-permute-start.16 = (f32[3,8,128]{2,1,0:T(8,128)S(1)}, f32[3,8,128]{2,1,0:T(8,128)S(1)}, u32[]{:S(2)}, u32[]{:S(2)}) collective-permute-start(f32[3,8,128]{2,1,0:T(8,128)S(1)} %add.15.same), channel_id=1, source_target_pairs={{0,16},{8,24},{16,0},{24,8},{1,17},{9,25},{17,1},{25,9},{2,18},{10... | collective-permute-start | bytes 36872 | tf_op jit(solution)/shard_map/ppermute | solution.py:475
  46.2 1.1 %shard_map.71.g_in = f32[8,9,136,128]{3,2,1,0:T(8,128)S(1)} custom-call(f32[8,8,128,128]{3,2,1,0:T(8,128)S(1)} %get-tuple-element.50.s, f32[4,8,128,256]{3,2,1,0:T(8,128)S(1)} %get-tuple-element.44.r, f32[8,9,136,128]{3,2,1,0:T(8,128)S(1)} %get-tuple-element.61.g_in), custom_call_target="tpu_custom_call", output_to_operand_aliasing={{}: (2, {})} | custom-call | flops 8388608 | bytes 16777216 | tf_op jit(solution)/shard_map/pallas_call | solution.py:441
  47.2 1.0 %collective-permute-done.19.yrecv = bf16[8,8,128]{2,1,0:T(8,128)(2,1)S(1)} collective-permute-done((bf16[8,8,128]{2,1,0:T(8,128)(2,1)S(1)}, bf16[8,8,128]{2,1,0:T(8,128)(2,1)S(1)}, u32[]{:S(2)}, u32[]{:S(2)}) %collective-permute-start.19) | collective-permute-done | bytes 16416 | tf_op jit(solution)/shard_map/ppermute | solution.py:468
  48.3 1.1 %collective-permute-done.16.other = f32[3,8,128]{2,1,0:T(8,128)S(1)} collective-permute-done((f32[3,8,128]{2,1,0:T(8,128)S(1)}, f32[3,8,128]{2,1,0:T(8,128)S(1)}, u32[]{:S(2)}, u32[]{:S(2)}) %collective-permute-start.16) | collective-permute-done | bytes 12320 | tf_op jit(solution)/shard_map/ppermute | solution.py:475
  49.3 0.0 collective-permute-done.17.pair0
  49.3 0.0 collective-permute-done.18.pair1
  49.3 3.4 %shard_map.72 = (bf16[8192,128]{1,0:T(8,128)(2,1)}, f32[8,9,136,128]{3,2,1,0:T(8,128)S(1)}) custom-call(s32[2,8]{1,0:T(2,128)S(1)} %copy-done.1, f32[3,8,128]{2,1,0:T(8,128)S(1)} %add.15.same, f32[3,8,128]{2,1,0:T(8,128)S(1)} %collective-permute-done.16.other, ...), custom_call_target="tpu_custom_call", output_to_operand_aliasing={{1}: (11, {})} | custom-call | tf_op jit(solution)/shard_map/pallas_call | solution.py:441
  (10 shorter events, 0.0 us)
Async XLA Ops:
  0.0 15.9 %copy-start.1 = (s32[2,8]{1,0:T(2,128)S(1)}, s32[2,8]{1,0:T(2,128)}, u32[]{:S(2)}) copy-start(s32[2,8]{1,0:T(2,128)} %kindy.7) | copy-start | bytes 196
  3.3 12.6 %collective-permute-start.2 = (bf16[512,128]{1,0:T(8,128)(2,1)S(1)}, bf16[512,128]{1,0:T(8,128)(2,1)S(1)}, u32[]{:S(2)}, u32[]{:S(2)}) collective-permute-start(bf16[512,128]{1,0:T(8,128)(2,1)S(1)} %get-tuple-element.36), channel_id=1, source_target_pairs={{0,2},{4,6},{2,0},{6,4},{1,3},{5,7},{3,1},{7,5},{8,10},{12,14},{10... | collective-permute-start | bytes 393224 | tf_op jit(solution)/shard_map/ppermute | solution.py:465
  6.4 9.5 %collective-permute-start.3 = (bf16[512,128]{1,0:T(8,128)(2,1)S(1)}, bf16[512,128]{1,0:T(8,128)(2,1)S(1)}, u32[]{:S(2)}, u32[]{:S(2)}) collective-permute-start(bf16[512,128]{1,0:T(8,128)(2,1)S(1)} %get-tuple-element.37), channel_id=1, source_target_pairs={{2,4},{4,2},{3,5},{5,3},{10,12},{12,10},{11,13},{13,11},{18,20},{2... | collective-permute-start | bytes 393224 | tf_op jit(solution)/shard_map/ppermute | solution.py:465
  7.1 1.3 %collective-permute-start = (f32[7,8,128]{2,1,0:T(8,128)S(1)}, f32[7,8,128]{2,1,0:T(8,128)S(1)}, u32[]{:S(2)}, u32[]{:S(2)}) collective-permute-start(f32[7,8,128]{2,1,0:T(8,128)S(1)} %get-tuple-element.34), channel_id=1, source_target_pairs={{0,8},{8,0},{16,24},{24,16},{1,9},{9,1},{17,25},{25,17},{2,10},{10... | collective-permute-start | bytes 86024 | tf_op jit(solution)/shard_map/ppermute | solution.py:473
  8.3 7.5 %collective-permute-start.1 = (f32[7,8,128]{2,1,0:T(8,128)S(1)}, f32[7,8,128]{2,1,0:T(8,128)S(1)}, u32[]{:S(2)}, u32[]{:S(2)}) collective-permute-start(f32[7,8,128]{2,1,0:T(8,128)S(1)} %add.12.same), channel_id=1, source_target_pairs={{0,16},{8,24},{16,0},{24,8},{1,17},{9,25},{17,1},{25,9},{2,18},{10... | collective-permute-start | bytes 86024 | tf_op jit(solution)/shard_map/ppermute | solution.py:475
  9.8 6.0 %collective-permute-start.4 = (bf16[2,8,512]{2,1,0:T(8,128)(2,1)S(1)}, bf16[2,8,512]{2,1,0:T(8,128)(2,1)S(1)}, u32[]{:S(2)}, u32[]{:S(2)}) collective-permute-start(bf16[2,8,512]{2,1,0:T(8,128)(2,1)S(1)} %get-tuple-element.38), channel_id=1, source_target_pairs={{0,1},{1,0},{2,3},{3,2},{4,5},{5,4},{6,7},{7,6},{8,9},{9,8},{10,11... | collective-permute-start | bytes 49160 | tf_op jit(solution)/shard_map/ppermute | solution.py:468
  12.4 1.0 %copy-start = (bf16[1024,2,128]{2,1,0:T(2,128)(2,1)S(1)}, bf16[1024,2,128]{2,1,0:T(2,128)(2,1)}, u32[]{:S(2)}) copy-start(bf16[1024,2,128]{2,1,0:T(2,128)(2,1)} %param.10) | copy-start | bytes 1572868
  20.4 10.0 %collective-permute-start.7 = (bf16[4,128,128]{2,1,0:T(8,128)(2,1)S(1)}, bf16[4,128,128]{2,1,0:T(8,128)(2,1)S(1)}, u32[]{:S(2)}, u32[]{:S(2)}) collective-permute-start(bf16[4,128,128]{2,1,0:T(8,128)(2,1)S(1)} %get-tuple-element.47), channel_id=1, source_target_pairs={{0,2},{4,6},{2,0},{6,4},{1,3},{5,7},{3,1},{7,5},{8,10},{12,14},{10... | collective-permute-start | bytes 393224 | tf_op jit(solution)/shard_map/ppermute | solution.py:465
  24.8 5.6 %collective-permute-start.8 = (bf16[4,128,128]{2,1,0:T(8,128)(2,1)S(1)}, bf16[4,128,128]{2,1,0:T(8,128)(2,1)S(1)}, u32[]{:S(2)}, u32[]{:S(2)}) collective-permute-start(bf16[4,128,128]{2,1,0:T(8,128)(2,1)S(1)} %get-tuple-element.48), channel_id=1, source_target_pairs={{2,4},{4,2},{3,5},{5,3},{10,12},{12,10},{11,13},{13,11},{18,20},{2... | collective-permute-start | bytes 393224 | tf_op jit(solution)/shard_map/ppermute | solution.py:465
  25.5 1.2 %collective-permute-start.5 = (f32[3,8,128]{2,1,0:T(8,128)S(1)}, f32[3,8,128]{2,1,0:T(8,128)S(1)}, u32[]{:S(2)}, u32[]{:S(2)}) collective-permute-start(f32[3,8,128]{2,1,0:T(8,128)S(1)} %get-tuple-element.46), channel_id=1, source_target_pairs={{0,8},{8,0},{16,24},{24,16},{1,9},{9,1},{17,25},{25,17},{2,10},{10... | collective-permute-start | bytes 36872 | tf_op jit(solution)/shard_map/ppermute | solution.py:473
  25.6 3.8 %collective-permute-start.9 = (bf16[8,8,128]{2,1,0:T(8,128)(2,1)S(1)}, bf16[8,8,128]{2,1,0:T(8,128)(2,1)S(1)}, u32[]{:S(2)}, u32[]{:S(2)}) collective-permute-start(bf16[8,8,128]{2,1,0:T(8,128)(2,1)S(1)} %get-tuple-element.49), channel_id=1, source_target_pairs={{0,1},{1,0},{2,3},{3,2},{4,5},{5,4},{6,7},{7,6},{8,9},{9,8},{10,11... | collective-permute-start | bytes 49160 | tf_op jit(solution)/shard_map/ppermute | solution.py:468
  26.7 3.7 %collective-permute-start.6 = (f32[3,8,128]{2,1,0:T(8,128)S(1)}, f32[3,8,128]{2,1,0:T(8,128)S(1)}, u32[]{:S(2)}, u32[]{:S(2)}) collective-permute-start(f32[3,8,128]{2,1,0:T(8,128)S(1)} %add.13.same), channel_id=1, source_target_pairs={{0,16},{8,24},{16,0},{24,8},{1,17},{9,25},{17,1},{25,9},{2,18},{10... | collective-permute-start | bytes 36872 | tf_op jit(solution)/shard_map/ppermute | solution.py:475
  32.0 6.9 %collective-permute-start.12 = (bf16[4,128,128]{2,1,0:T(8,128)(2,1)S(1)}, bf16[4,128,128]{2,1,0:T(8,128)(2,1)S(1)}, u32[]{:S(2)}, u32[]{:S(2)}) collective-permute-start(bf16[4,128,128]{2,1,0:T(8,128)(2,1)S(1)} %get-tuple-element.53), channel_id=1, source_target_pairs={{0,2},{4,6},{2,0},{6,4},{1,3},{5,7},{3,1},{7,5},{8,10},{12,14},{10... | collective-permute-start | bytes 393224 | tf_op jit(solution)/shard_map/ppermute | solution.py:465
  33.3 5.6 %collective-permute-start.13 = (bf16[4,128,128]{2,1,0:T(8,128)(2,1)S(1)}, bf16[4,128,128]{2,1,0:T(8,128)(2,1)S(1)}, u32[]{:S(2)}, u32[]{:S(2)}) collective-permute-start(bf16[4,128,128]{2,1,0:T(8,128)(2,1)S(1)} %get-tuple-element.54), channel_id=1, source_target_pairs={{2,4},{4,2},{3,5},{5,3},{10,12},{12,10},{11,13},{13,11},{18,20},{2... | collective-permute-start | bytes 393224 | tf_op jit(solution)/shard_map/ppermute | solution.py:465
  33.9 1.2 %collective-permute-start.10 = (f32[3,8,128]{2,1,0:T(8,128)S(1)}, f32[3,8,128]{2,1,0:T(8,128)S(1)}, u32[]{:S(2)}, u32[]{:S(2)}) collective-permute-start(f32[3,8,128]{2,1,0:T(8,128)S(1)} %get-tuple-element.52), channel_id=1, source_target_pairs={{0,8},{8,0},{16,24},{24,16},{1,9},{9,1},{17,25},{25,17},{2,10},{10... | collective-permute-start | bytes 36872 | tf_op jit(solution)/shard_map/ppermute | solution.py:473
  34.0 3.8 %collective-permute-start.14 = (bf16[8,8,128]{2,1,0:T(8,128)(2,1)S(1)}, bf16[8,8,128]{2,1,0:T(8,128)(2,1)S(1)}, u32[]{:S(2)}, u32[]{:S(2)}) collective-permute-start(bf16[8,8,128]{2,1,0:T(8,128)(2,1)S(1)} %get-tuple-element.55), channel_id=1, source_target_pairs={{0,1},{1,0},{2,3},{3,2},{4,5},{5,4},{6,7},{7,6},{8,9},{9,8},{10,11... | collective-permute-start | bytes 49160 | tf_op jit(solution)/shard_map/ppermute | solution.py:468
  35.2 3.7 %collective-permute-start.11 = (f32[3,8,128]{2,1,0:T(8,128)S(1)}, f32[3,8,128]{2,1,0:T(8,128)S(1)}, u32[]{:S(2)}, u32[]{:S(2)}) collective-permute-start(f32[3,8,128]{2,1,0:T(8,128)S(1)} %add.14.same), channel_id=1, source_target_pairs={{0,16},{8,24},{16,0},{24,8},{1,17},{9,25},{17,1},{25,9},{2,18},{10... | collective-permute-start | bytes 36872 | tf_op jit(solution)/shard_map/ppermute | solution.py:475
  40.5 8.9 %collective-permute-start.17 = (bf16[4,128,128]{2,1,0:T(8,128)(2,1)S(1)}, bf16[4,128,128]{2,1,0:T(8,128)(2,1)S(1)}, u32[]{:S(2)}, u32[]{:S(2)}) collective-permute-start(bf16[4,128,128]{2,1,0:T(8,128)(2,1)S(1)} %get-tuple-element.58), channel_id=1, source_target_pairs={{0,2},{4,6},{2,0},{6,4},{1,3},{5,7},{3,1},{7,5},{8,10},{12,14},{10... | collective-permute-start | bytes 393224 | tf_op jit(solution)/shard_map/ppermute | solution.py:465
  43.7 5.6 %collective-permute-start.18 = (bf16[4,128,128]{2,1,0:T(8,128)(2,1)S(1)}, bf16[4,128,128]{2,1,0:T(8,128)(2,1)S(1)}, u32[]{:S(2)}, u32[]{:S(2)}) collective-permute-start(bf16[4,128,128]{2,1,0:T(8,128)(2,1)S(1)} %get-tuple-element.59), channel_id=1, source_target_pairs={{2,4},{4,2},{3,5},{5,3},{10,12},{12,10},{11,13},{13,11},{18,20},{2... | collective-permute-start | bytes 393224 | tf_op jit(solution)/shard_map/ppermute | solution.py:465
  44.4 1.2 %collective-permute-start.15 = (f32[3,8,128]{2,1,0:T(8,128)S(1)}, f32[3,8,128]{2,1,0:T(8,128)S(1)}, u32[]{:S(2)}, u32[]{:S(2)}) collective-permute-start(f32[3,8,128]{2,1,0:T(8,128)S(1)} %get-tuple-element.57), channel_id=1, source_target_pairs={{0,8},{8,0},{16,24},{24,16},{1,9},{9,1},{17,25},{25,17},{2,10},{10... | collective-permute-start | bytes 36872 | tf_op jit(solution)/shard_map/ppermute | solution.py:473
  44.5 3.8 %collective-permute-start.19 = (bf16[8,8,128]{2,1,0:T(8,128)(2,1)S(1)}, bf16[8,8,128]{2,1,0:T(8,128)(2,1)S(1)}, u32[]{:S(2)}, u32[]{:S(2)}) collective-permute-start(bf16[8,8,128]{2,1,0:T(8,128)(2,1)S(1)} %get-tuple-element.60), channel_id=1, source_target_pairs={{0,1},{1,0},{2,3},{3,2},{4,5},{5,4},{6,7},{7,6},{8,9},{9,8},{10,11... | collective-permute-start | bytes 49160 | tf_op jit(solution)/shard_map/ppermute | solution.py:468
  45.6 3.7 %collective-permute-start.16 = (f32[3,8,128]{2,1,0:T(8,128)S(1)}, f32[3,8,128]{2,1,0:T(8,128)S(1)}, u32[]{:S(2)}, u32[]{:S(2)}) collective-permute-start(f32[3,8,128]{2,1,0:T(8,128)S(1)} %add.15.same), channel_id=1, source_target_pairs={{0,16},{8,24},{16,0},{24,8},{1,17},{9,25},{17,1},{25,9},{2,18},{10... | collective-permute-start | bytes 36872 | tf_op jit(solution)/shard_map/ppermute | solution.py:475

commit v3 on v2

--- a/solution.py
+++ b/solution.py
@@ -8,6 +8,7 @@
 from jax.experimental import pallas as pl
 from jax.experimental.pallas import tpu as pltpu
 from jax.sharding import PartitionSpec as P
+
 
 NVX = 64
 HALF = NVX // 2
@@ -19,7 +20,6 @@
 WEIGHT = STEP * STEP / (2.0 * math.pi)
 TIME_STEP = COURANT / ((NVX - 1) * STEP)
 LANES = 128
-HIGHEST = lax.Precision.HIGHEST
 F32 = jnp.float32
 BF16 = jnp.bfloat16
 
@@ -84,7 +84,7 @@
     return jnp.concatenate(pieces(a), axis=0).astype(BF16)
 
 
-def moments_kernel(prev, relax_far, kindx_far, pay, ymsg, pt, xmsg0, xmsg1, relax, kindx, rows, staged, sems, few):
+def moments_kernel(prev, relax_far, kindx_far, lri_far, bti_far, pay, ymsg, pt, xmsg0, xmsg1, relax, kindx, lri, bti, rows, staged, sems, few):
     cells_x, _, count, cells_y = pt.shape
     info = device_info(count // HALF)
     span = HALF * cells_x
@@ -93,7 +93,8 @@
     order = [2 * i + sign for sign in range(2) for i in range(count // HALF)]
     for i in order:
         copies[i].start()
-    small = [pltpu.make_async_copy(relax_far, relax, few.at[0]), pltpu.make_async_copy(kindx_far, kindx, few.at[1])]
+    small = [pltpu.make_async_copy(source, target, few.at[i]) for i, (source, target) in enumerate(
+        ((relax_far, relax), (kindx_far, kindx), (lri_far, lri), (bti_far, bti)))]
     for copy in small:
         copy.start()
     for sign in range(2):
@@ -327,11 +328,12 @@
             part = jnp.concatenate([lri[c : c + 2 * HALF, :] for c in chunk], axis=0)
             pick = (iota((LANES, 2 * LANES), 1) == 2 * iota((LANES, 2 * LANES), 0) + 1 - sign).astype(F32).astype(BF16)
             xw[block] = nt(flip, nn(pick, part).astype(BF16))
-            part = jnp.concatenate([bti[c : c + 2 * HALF, :] for c in chunk], axis=0)
             row, col = iota((16, cells_x), 0), iota((16, cells_x), 1)
             order = (col == (row if sign else cells_x - 1 - row)).astype(F32).astype(BF16)
-            pick = (iota((2 * LANES, LANES), 0) == 2 * iota((2 * LANES, LANES), 1) + 1 - info[1]).astype(F32).astype(BF16)
-            yw[block] = nn(nt(order, part).astype(BF16), pick)[:cells_x]
+            part = nn(order, bti[1 - info[1], :, at * 2 * LANES : (at + 1) * 2 * LANES]).astype(BF16)
+            row, col = iota((2 * LANES, LANES), 0), iota((2 * LANES, LANES), 1)
+            pick = (row == col // HALF * NVX + HALF * sign + col % HALF).astype(F32).astype(BF16)
+            yw[block] = nn(part, pick)[:cells_x]
         for at in range(0, per_sign, 2):
             ix, iy = lane_ints(info[0], sign, at * LANES, (1, 2 * LANES))
             both = (sign * per_sign + at) // 2
@@ -457,41 +459,39 @@
     per_sign = count // LANES
     blocks = 2 * per_sign
     nvel, ngx, ngy = lax.axis_size("vel"), lax.axis_size("gx"), lax.axis_size("gy")
+
     def pairs(count, start):
         low = range(start, count - 1, 2)
         return [(i, i + 1) for i in low] + [(i + 1, i) for i in low]
 
-    def swap_x(first, second):
-        return lax.ppermute(first, "gx", pairs(ngx, 0)), lax.ppermute(second, "gx", pairs(ngx, 1))
-
-    def swap_y(a):
-        return lax.ppermute(a, "gy", pairs(ngy, 0))
-
-    def sum_vel(a):
+    def exchange(first, second, edge, part):
         reach = 1
         while reach < nvel // 2:
-            a = a + lax.ppermute(a, "vel", [(i, i ^ reach) for i in range(nvel)])
+            part = part + lax.ppermute(part, "vel", [(i, i ^ reach) for i in range(nvel)])
             reach *= 2
-        return a, lax.ppermute(a, "vel", [(i, i ^ reach) for i in range(nvel)])
+        other = lax.ppermute(part, "vel", [(i, i ^ reach) for i in range(nvel)])
+        edge = lax.ppermute(edge, "gy", pairs(ngy, 0))
+        first = lax.ppermute(first, "gx", pairs(ngx, 0))
+        second = lax.ppermute(second, "gx", pairs(ngx, 1))
+        return (first, second), edge, (part, other)
 
     assert ngy == 2 and nvel & (nvel - 1) == 0, "mesh shape"
     sds = jax.ShapeDtypeStruct
     staging = [pltpu.VMEM((LANES * cells_x, cells_y), F32), pltpu.VMEM((vel_rows * cells_x, cells_y), BF16),
                pltpu.SemaphoreType.DMA((vel_rows // HALF,))]
+
     def far(a):
         return pltpu.with_memory_space_constraint(a, pltpu.HBM)
 
-    pay, ymsg, pt, xmsg0, xmsg1, relax, kindx = call(
+    pay, ymsg, pt, xmsg0, xmsg1, relax, kindx, lri, bti = call(
         moments_kernel,
         (sds((7, 8, LANES), F32), sds((2, cells_x, count), BF16), sds((cells_x, 2, count, cells_y), BF16),
-         sds((count, cells_y), BF16), sds((count, cells_y), BF16), sds(relax_time.shape, F32), sds(left_right_kind.shape, jnp.int32)),
-        (far(previous.reshape(vel_rows * cells_x, cells_y)), far(relax_time), far(left_right_kind)),
-        scratch=staging + [pltpu.SemaphoreType.DMA((2,))], mib=10, far_in=(0, 1, 2))
-    halo = swap_x(xmsg0, xmsg1)
-    yrecv = swap_y(ymsg)
-    sums = sum_vel(pay)
-    lri = left_right_inflow.reshape(2 * vel_rows, cells_y)
-    bti = bottom_top_inflow.reshape(2 * vel_rows, cells_x)
+         sds((count, cells_y), BF16), sds((count, cells_y), BF16), sds(relax_time.shape, F32), sds(left_right_kind.shape, jnp.int32),
+         sds((2 * vel_rows, cells_y), BF16), sds((2, cells_x, vel_rows), BF16)),
+        (far(previous.reshape(vel_rows * cells_x, cells_y)), far(relax_time), far(left_right_kind),
+         far(left_right_inflow.reshape(2 * vel_rows, cells_y)), far(bottom_top_inflow.transpose(1, 2, 0))),
+        scratch=staging + [pltpu.SemaphoreType.DMA((4,))], mib=10, far_in=(0, 1, 2, 3, 4))
+    halo, yrecv, sums = exchange(xmsg0, xmsg1, ymsg, pay)
     g_shape = sds((blocks, cells_x + 1, cells_y + 8, LANES), F32)
     full = sds((blocks, cells_x, cells_y, LANES), F32)
     wide = sds((blocks // 2, cells_x, cells_y, 2 * LANES), F32)
@@ -511,9 +511,7 @@
             pltpu.VMEM((2, cells_x * cells_y, 3 * NVX), BF16), pltpu.VMEM((2, cells_x * cells_y, 3 * local_ky), BF16),
             pltpu.VMEM((cells_x * cells_y, LANES), F32), pltpu.VMEM((cells_x * cells_y, 2 * LANES), F32)], mib=24)
     for number in range(1, SWEEPS):
-        halo = swap_x(xmsg0, xmsg1)
-        yrecv = swap_y(ymsg)
-        sums = sum_vel(flux)
+        halo, yrecv, sums = exchange(xmsg0, xmsg1, ymsg, flux)
         g = call(inner_kernel, (g_shape,), (s, r, g), aliases={2: 0}, mib=20, cost=work)[0]
         ins = (bottom_top_kind, *sums, *halo, yrecv, xw, yw, kx, s, r, g)
         if number == SWEEPS - 1:

time: 53.1 us -> 51.1 us (0.962)
  local copies, waits for them, and re-layouts: 2.12 us -> 0.01 us
  starting transfers between devices: 22.2 us -> 23.4 us
  waiting for transfers between devices: 8.47 us -> 7.54 us
    unnamed x5 -> x2, local copies, waits for them, and re-layouts: 2.12 us -> 0.01 us
    ppermute x20, starting transfers between devices: 22.2 us -> 23.4 us  [the longest x4 12.1 us: exchange(): first = lax.ppermute(first, 'gx', pairs(ngx, 0))]
    ppermute x20, waiting for transfers between devices: 8.47 us -> 7.54 us  [the longest x4 3.43 us: exchange(): other = lax.ppermute(part, 'vel', [(i, i ^ reach) for i in range(nvel)])]
  transfers between devices with their start and end apart: 20 -> 20, of which waited for: 10 -> 7; matrix products, arithmetic and copies ran while one was open for 2% -> 0% of each run, Pallas kernels for 10% -> 11%
where the time goes in v3:
time: 51.1 us; the launch traced here: 50.9 us
  starting transfers between devices  23.4 us (46%)
  Pallas kernels  19.9 us (39%)
  waiting for transfers between devices  7.54 us (15%)
    pallas_call x9, Pallas kernels, call(): pl.pallas_call(kernel, out_shape=outs, in_specs=[scalar if i in smem else...  19.9 us
    ppermute x4, starting transfers between devices, exchange(): first = lax.ppermute(first, 'gx', pairs(ngx, 0))  12.1 us
    ppermute x4, starting transfers between devices, exchange(): edge = lax.ppermute(edge, 'gy', pairs(ngy, 0))  5.25 us
    ppermute x4, waiting for transfers between devices, exchange(): other = lax.ppermute(part, 'vel', [(i, i ^ reach) for i in range(nvel)])  3.43 us
    ppermute x4, starting transfers between devices, exchange(): other = lax.ppermute(part, 'vel', [(i, i ^ reach) for i in range(nvel)])  3.1 us
    ppermute x4, waiting for transfers between devices, exchange(): edge = lax.ppermute(edge, 'gy', pairs(ngy, 0))  2.89 us
    ppermute x4, starting transfers between devices, exchange(): second = lax.ppermute(second, 'gx', pairs(ngx, 1))  2.63 us
    ppermute x4, waiting for transfers between devices, exchange(): lax.ppermute(part, 'vel', [(i, i ^ reach) for i in range(nvel)])  1.2 us
  transfers between devices with their start and end apart: 20, of which 7 were waited for; matrix products, arithmetic and copies ran while one was open for 0% of the time, Pallas kernels for 11%

profile of v3, /device:TPU:0, one launch (start us, length us, event | category | flops | bytes accessed | tf_op | source)
XLA Modules:
  0.0 50.9 jit_solution(16364480196989130977)
XLA Ops:
  0.0 3.3 %shard_map.64 = (f32[7,8,128]{2,1,0:T(8,128)S(1)}, bf16[2,8,512]{2,1,0:T(8,128)(2,1)S(1)}, bf16[8,2,512,128]{3,2,1,0:T(8,128)(2,1)S(1)}, bf16[512,128]{1,0:T(8,1...) custom-call(bf16[8192,128]{1,0:T(8,128)(2,1)} %bitcast.4, ...), custom_call_target="tpu_custom_call" | custom-call | tf_op jit(solution)/shard_map/pallas_call | solution.py:443
  3.3 3.1 %collective-permute-start.2 = (bf16[512,128]{1,0:T(8,128)(2,1)S(1)}, bf16[512,128]{1,0:T(8,128)(2,1)S(1)}, u32[]{:S(2)}, u32[]{:S(2)}) collective-permute-start(bf16[512,128]{1,0:T(8,128)(2,1)S(1)} %get-tuple-element.38), channel_id=1, source_target_pairs={{0,2},{4,6},{2,0},{6,4},{1,3},{5,7},{3,1},{7,5},{8,10},{12,14},{10... | collective-permute-start | bytes 393224 | tf_op jit(solution)/shard_map/ppermute | solution.py:474
  6.4 0.7 %collective-permute-start.3 = (bf16[512,128]{1,0:T(8,128)(2,1)S(1)}, bf16[512,128]{1,0:T(8,128)(2,1)S(1)}, u32[]{:S(2)}, u32[]{:S(2)}) collective-permute-start(bf16[512,128]{1,0:T(8,128)(2,1)S(1)} %get-tuple-element.39), channel_id=1, source_target_pairs={{2,4},{4,2},{3,5},{5,3},{10,12},{12,10},{11,13},{13,11},{18,20},{2... | collective-permute-start | bytes 393224 | tf_op jit(solution)/shard_map/ppermute | solution.py:475
  7.1 0.1 collective-permute-start
  7.2 1.2 %collective-permute-done = f32[7,8,128]{2,1,0:T(8,128)S(1)} collective-permute-done((f32[7,8,128]{2,1,0:T(8,128)S(1)}, f32[7,8,128]{2,1,0:T(8,128)S(1)}, u32[]{:S(2)}, u32[]{:S(2)}) %collective-permute-start) | collective-permute-done | bytes 28704 | tf_op jit(solution)/shard_map/ppermute | solution.py:470
  8.4 1.5 %collective-permute-start.1 = (f32[7,8,128]{2,1,0:T(8,128)S(1)}, f32[7,8,128]{2,1,0:T(8,128)S(1)}, u32[]{:S(2)}, u32[]{:S(2)}) collective-permute-start(f32[7,8,128]{2,1,0:T(8,128)S(1)} %add.12.same), channel_id=1, source_target_pairs={{0,16},{8,24},{16,0},{24,8},{1,17},{9,25},{17,1},{25,9},{2,18},{10... | collective-permute-start | bytes 86024 | tf_op jit(solution)/shard_map/ppermute | solution.py:472
  9.9 1.5 %collective-permute-start.4 = (bf16[2,8,512]{2,1,0:T(8,128)(2,1)S(1)}, bf16[2,8,512]{2,1,0:T(8,128)(2,1)S(1)}, u32[]{:S(2)}, u32[]{:S(2)}) collective-permute-start(bf16[2,8,512]{2,1,0:T(8,128)(2,1)S(1)} %get-tuple-element.40), channel_id=1, source_target_pairs={{0,1},{1,0},{2,3},{3,2},{4,5},{5,4},{6,7},{7,6},{8,9},{9,8},{10,11... | collective-permute-start | bytes 49160 | tf_op jit(solution)/shard_map/ppermute | solution.py:473
  11.4 2.4 %shard_map.65 = (f32[8,9,136,128]{3,2,1,0:T(8,128)S(1)}, f32[4,8,128,256]{3,2,1,0:T(8,128)S(1)}, f32[8,128,128]{2,1,0:T(8,128)S(1)}, f32[8,8,128]{2,1,0:T(8,128)S(1)}, f32[2,128,128]{2,1,0:T(8,128)S(1)}) custom-call(f32[8,128]{1,0:T(8,128)S(1)} %get-tuple-element.37.relax, s32[2,128]{1,0:T(2,128)S(1)} %get-tuple-element.41.kindx, ...), custom_call_target="tpu_custom_call" | custom-call | flops 8388608 | bytes 16777216 | tf_op jit(solution)/shard_map/pallas_call | solution.py:443
  13.7 0.0 collective-permute-done.4.yrecv
  13.8 0.0 collective-permute-done.1.other
  13.8 0.0 collective-permute-done.2.pair0
  13.8 0.0 collective-permute-done.3.pair1
  13.8 4.5 %shard_map.66 = (f32[8,9,136,128]{3,2,1,0:T(8,128)S(1)}, f32[8,8,128,128]{3,2,1,0:T(8,128)S(1)}, bf16[4,128,128]{2,1,0:T(8,128)(2,1)S(1)}, bf16[4,128,128]{2,1,0...) custom-call(s32[2,8]{1,0:T(2,128)S(1)} %copy-done, ...), custom_call_target="tpu_custom_call", output_to_operand_aliasing={{0}: (11, {})} | custom-call | tf_op jit(solution)/shard_map/pallas_call | solution.py:443
  18.3 4.4 %collective-permute-start.7 = (bf16[4,128,128]{2,1,0:T(8,128)(2,1)S(1)}, bf16[4,128,128]{2,1,0:T(8,128)(2,1)S(1)}, u32[]{:S(2)}, u32[]{:S(2)}) collective-permute-start(bf16[4,128,128]{2,1,0:T(8,128)(2,1)S(1)} %get-tuple-element.51), channel_id=1, source_target_pairs={{0,2},{4,6},{2,0},{6,4},{1,3},{5,7},{3,1},{7,5},{8,10},{12,14},{10... | collective-permute-start | bytes 393224 | tf_op jit(solution)/shard_map/ppermute | solution.py:474
  22.7 0.7 %collective-permute-start.8 = (bf16[4,128,128]{2,1,0:T(8,128)(2,1)S(1)}, bf16[4,128,128]{2,1,0:T(8,128)(2,1)S(1)}, u32[]{:S(2)}, u32[]{:S(2)}) collective-permute-start(bf16[4,128,128]{2,1,0:T(8,128)(2,1)S(1)} %get-tuple-element.52), channel_id=1, source_target_pairs={{2,4},{4,2},{3,5},{5,3},{10,12},{12,10},{11,13},{13,11},{18,20},{2... | collective-permute-start | bytes 393224 | tf_op jit(solution)/shard_map/ppermute | solution.py:475
  23.4 0.1 collective-permute-start.5
  23.5 1.4 %collective-permute-start.9 = (bf16[8,8,128]{2,1,0:T(8,128)(2,1)S(1)}, bf16[8,8,128]{2,1,0:T(8,128)(2,1)S(1)}, u32[]{:S(2)}, u32[]{:S(2)}) collective-permute-start(bf16[8,8,128]{2,1,0:T(8,128)(2,1)S(1)} %get-tuple-element.53), channel_id=1, source_target_pairs={{0,1},{1,0},{2,3},{3,2},{4,5},{5,4},{6,7},{7,6},{8,9},{9,8},{10,11... | collective-permute-start | bytes 49160 | tf_op jit(solution)/shard_map/ppermute | solution.py:473
  24.9 0.0 collective-permute-done.5
  24.9 0.5 %collective-permute-start.6 = (f32[3,8,128]{2,1,0:T(8,128)S(1)}, f32[3,8,128]{2,1,0:T(8,128)S(1)}, u32[]{:S(2)}, u32[]{:S(2)}) collective-permute-start(f32[3,8,128]{2,1,0:T(8,128)S(1)} %add.13.same), channel_id=1, source_target_pairs={{0,16},{8,24},{16,0},{24,8},{1,17},{9,25},{17,1},{25,9},{2,18},{10... | collective-permute-start | bytes 36872 | tf_op jit(solution)/shard_map/ppermute | solution.py:472
  25.4 1.1 %shard_map.67.g_in = f32[8,9,136,128]{3,2,1,0:T(8,128)S(1)} custom-call(f32[8,8,128,128]{3,2,1,0:T(8,128)S(1)} %get-tuple-element.54.s, f32[4,8,128,256]{3,2,1,0:T(8,128)S(1)} %get-tuple-element.48.r, f32[8,9,136,128]{3,2,1,0:T(8,128)S(1)} %get-tuple-element.55.g_in), custom_call_target="tpu_custom_call", output_to_operand_aliasing={{}: (2, {})} | custom-call | flops 8388608 | bytes 16777216 | tf_op jit(solution)/shard_map/pallas_call | solution.py:443
  26.5 0.8 %collective-permute-done.9.yrecv = bf16[8,8,128]{2,1,0:T(8,128)(2,1)S(1)} collective-permute-done((bf16[8,8,128]{2,1,0:T(8,128)(2,1)S(1)}, bf16[8,8,128]{2,1,0:T(8,128)(2,1)S(1)}, u32[]{:S(2)}, u32[]{:S(2)}) %collective-permute-start.9) | collective-permute-done | bytes 16416 | tf_op jit(solution)/shard_map/ppermute | solution.py:473
  27.3 1.3 %collective-permute-done.6.other = f32[3,8,128]{2,1,0:T(8,128)S(1)} collective-permute-done((f32[3,8,128]{2,1,0:T(8,128)S(1)}, f32[3,8,128]{2,1,0:T(8,128)S(1)}, u32[]{:S(2)}, u32[]{:S(2)}) %collective-permute-start.6) | collective-permute-done | bytes 12320 | tf_op jit(solution)/shard_map/ppermute | solution.py:472
  28.6 0.0 collective-permute-done.7.pair0
  28.6 0.0 collective-permute-done.8.pair1
  28.6 1.6 %shard_map.68 = (f32[8,9,136,128]{3,2,1,0:T(8,128)S(1)}, bf16[4,128,128]{2,1,0:T(8,128)(2,1)S(1)}, bf16[4,128,128]{2,1,0:T(8,128)(2,1)S(1)}, bf16[8,8,128]{2,1,0:T(8,128)(2,1)S(1)}, f32[3,8,128]{2,1,0:T(8,128)S(1)}) custom-call(s32[2,8]{1,0:T(2,128)S(1)} %copy-done, f32[3,8,128]{2,1,0:T(8,128)S(1)} %add.13.same, ...), custom_call_target="tpu_custom_call", output_to_operand_aliasing={{0}: (11, {})} | custom-call | tf_op jit(solution)/shard_map/pallas_call | solution.py:443
  30.1 1.3 %collective-permute-start.12 = (bf16[4,128,128]{2,1,0:T(8,128)(2,1)S(1)}, bf16[4,128,128]{2,1,0:T(8,128)(2,1)S(1)}, u32[]{:S(2)}, u32[]{:S(2)}) collective-permute-start(bf16[4,128,128]{2,1,0:T(8,128)(2,1)S(1)} %get-tuple-element.57), channel_id=1, source_target_pairs={{0,2},{4,6},{2,0},{6,4},{1,3},{5,7},{3,1},{7,5},{8,10},{12,14},{10... | collective-permute-start | bytes 393224 | tf_op jit(solution)/shard_map/ppermute | solution.py:474
  31.4 0.7 %collective-permute-start.13 = (bf16[4,128,128]{2,1,0:T(8,128)(2,1)S(1)}, bf16[4,128,128]{2,1,0:T(8,128)(2,1)S(1)}, u32[]{:S(2)}, u32[]{:S(2)}) collective-permute-start(bf16[4,128,128]{2,1,0:T(8,128)(2,1)S(1)} %get-tuple-element.58), channel_id=1, source_target_pairs={{2,4},{4,2},{3,5},{5,3},{10,12},{12,10},{11,13},{13,11},{18,20},{2... | collective-permute-start | bytes 393224 | tf_op jit(solution)/shard_map/ppermute | solution.py:475
  32.1 0.1 collective-permute-start.10
  32.2 1.2 %collective-permute-start.14 = (bf16[8,8,128]{2,1,0:T(8,128)(2,1)S(1)}, bf16[8,8,128]{2,1,0:T(8,128)(2,1)S(1)}, u32[]{:S(2)}, u32[]{:S(2)}) collective-permute-start(bf16[8,8,128]{2,1,0:T(8,128)(2,1)S(1)} %get-tuple-element.59), channel_id=1, source_target_pairs={{0,1},{1,0},{2,3},{3,2},{4,5},{5,4},{6,7},{7,6},{8,9},{9,8},{10,11... | collective-permute-start | bytes 49160 | tf_op jit(solution)/shard_map/ppermute | solution.py:473
  33.3 0.0 collective-permute-done.10
  33.3 0.5 %collective-permute-start.11 = (f32[3,8,128]{2,1,0:T(8,128)S(1)}, f32[3,8,128]{2,1,0:T(8,128)S(1)}, u32[]{:S(2)}, u32[]{:S(2)}) collective-permute-start(f32[3,8,128]{2,1,0:T(8,128)S(1)} %add.14.same), channel_id=1, source_target_pairs={{0,16},{8,24},{16,0},{24,8},{1,17},{9,25},{17,1},{25,9},{2,18},{10... | collective-permute-start | bytes 36872 | tf_op jit(solution)/shard_map/ppermute | solution.py:472
  33.9 1.1 %shard_map.69.g_in = f32[8,9,136,128]{3,2,1,0:T(8,128)S(1)} custom-call(f32[8,8,128,128]{3,2,1,0:T(8,128)S(1)} %get-tuple-element.54.s, f32[4,8,128,256]{3,2,1,0:T(8,128)S(1)} %get-tuple-element.48.r, f32[8,9,136,128]{3,2,1,0:T(8,128)S(1)} %get-tuple-element.60.g_in), custom_call_target="tpu_custom_call", output_to_operand_aliasing={{}: (2, {})} | custom-call | flops 8388608 | bytes 16777216 | tf_op jit(solution)/shard_map/pallas_call | solution.py:443
  34.9 1.0 %collective-permute-done.14.yrecv = bf16[8,8,128]{2,1,0:T(8,128)(2,1)S(1)} collective-permute-done((bf16[8,8,128]{2,1,0:T(8,128)(2,1)S(1)}, bf16[8,8,128]{2,1,0:T(8,128)(2,1)S(1)}, u32[]{:S(2)}, u32[]{:S(2)}) %collective-permute-start.14) | collective-permute-done | bytes 16416 | tf_op jit(solution)/shard_map/ppermute | solution.py:473
  36.0 1.1 %collective-permute-done.11.other = f32[3,8,128]{2,1,0:T(8,128)S(1)} collective-permute-done((f32[3,8,128]{2,1,0:T(8,128)S(1)}, f32[3,8,128]{2,1,0:T(8,128)S(1)}, u32[]{:S(2)}, u32[]{:S(2)}) %collective-permute-start.11) | collective-permute-done | bytes 12320 | tf_op jit(solution)/shard_map/ppermute | solution.py:472
  37.0 0.0 collective-permute-done.12.pair0
  37.0 0.0 collective-permute-done.13.pair1
  37.0 1.6 %shard_map.70 = (f32[8,9,136,128]{3,2,1,0:T(8,128)S(1)}, bf16[4,128,128]{2,1,0:T(8,128)(2,1)S(1)}, bf16[4,128,128]{2,1,0:T(8,128)(2,1)S(1)}, bf16[8,8,128]{2,1,0:T(8,128)(2,1)S(1)}, f32[3,8,128]{2,1,0:T(8,128)S(1)}) custom-call(s32[2,8]{1,0:T(2,128)S(1)} %copy-done, f32[3,8,128]{2,1,0:T(8,128)S(1)} %add.14.same, ...), custom_call_target="tpu_custom_call", output_to_operand_aliasing={{0}: (11, {})} | custom-call | tf_op jit(solution)/shard_map/pallas_call | solution.py:443
  38.6 3.3 %collective-permute-start.17 = (bf16[4,128,128]{2,1,0:T(8,128)(2,1)S(1)}, bf16[4,128,128]{2,1,0:T(8,128)(2,1)S(1)}, u32[]{:S(2)}, u32[]{:S(2)}) collective-permute-start(bf16[4,128,128]{2,1,0:T(8,128)(2,1)S(1)} %get-tuple-element.62), channel_id=1, source_target_pairs={{0,2},{4,6},{2,0},{6,4},{1,3},{5,7},{3,1},{7,5},{8,10},{12,14},{10... | collective-permute-start | bytes 393224 | tf_op jit(solution)/shard_map/ppermute | solution.py:474
  41.9 0.7 %collective-permute-start.18 = (bf16[4,128,128]{2,1,0:T(8,128)(2,1)S(1)}, bf16[4,128,128]{2,1,0:T(8,128)(2,1)S(1)}, u32[]{:S(2)}, u32[]{:S(2)}) collective-permute-start(bf16[4,128,128]{2,1,0:T(8,128)(2,1)S(1)} %get-tuple-element.63), channel_id=1, source_target_pairs={{2,4},{4,2},{3,5},{5,3},{10,12},{12,10},{11,13},{13,11},{18,20},{2... | collective-permute-start | bytes 393224 | tf_op jit(solution)/shard_map/ppermute | solution.py:475
  42.6 0.1 collective-permute-start.15
  42.6 1.2 %collective-permute-start.19 = (bf16[8,8,128]{2,1,0:T(8,128)(2,1)S(1)}, bf16[8,8,128]{2,1,0:T(8,128)(2,1)S(1)}, u32[]{:S(2)}, u32[]{:S(2)}) collective-permute-start(bf16[8,8,128]{2,1,0:T(8,128)(2,1)S(1)} %get-tuple-element.64), channel_id=1, source_target_pairs={{0,1},{1,0},{2,3},{3,2},{4,5},{5,4},{6,7},{7,6},{8,9},{9,8},{10,11... | collective-permute-start | bytes 49160 | tf_op jit(solution)/shard_map/ppermute | solution.py:473
  43.8 0.0 collective-permute-done.15
  43.8 0.5 %collective-permute-start.16 = (f32[3,8,128]{2,1,0:T(8,128)S(1)}, f32[3,8,128]{2,1,0:T(8,128)S(1)}, u32[]{:S(2)}, u32[]{:S(2)}) collective-permute-start(f32[3,8,128]{2,1,0:T(8,128)S(1)} %add.15.same), channel_id=1, source_target_pairs={{0,16},{8,24},{16,0},{24,8},{1,17},{9,25},{17,1},{25,9},{2,18},{10... | collective-permute-start | bytes 36872 | tf_op jit(solution)/shard_map/ppermute | solution.py:472
  44.3 1.1 %shard_map.71.g_in = f32[8,9,136,128]{3,2,1,0:T(8,128)S(1)} custom-call(f32[8,8,128,128]{3,2,1,0:T(8,128)S(1)} %get-tuple-element.54.s, f32[4,8,128,256]{3,2,1,0:T(8,128)S(1)} %get-tuple-element.48.r, f32[8,9,136,128]{3,2,1,0:T(8,128)S(1)} %get-tuple-element.65.g_in), custom_call_target="tpu_custom_call", output_to_operand_aliasing={{}: (2, {})} | custom-call | flops 8388608 | bytes 16777216 | tf_op jit(solution)/shard_map/pallas_call | solution.py:443
  45.4 1.0 %collective-permute-done.19.yrecv = bf16[8,8,128]{2,1,0:T(8,128)(2,1)S(1)} collective-permute-done((bf16[8,8,128]{2,1,0:T(8,128)(2,1)S(1)}, bf16[8,8,128]{2,1,0:T(8,128)(2,1)S(1)}, u32[]{:S(2)}, u32[]{:S(2)}) %collective-permute-start.19) | collective-permute-done | bytes 16416 | tf_op jit(solution)/shard_map/ppermute | solution.py:473
  46.4 1.1 %collective-permute-done.16.other = f32[3,8,128]{2,1,0:T(8,128)S(1)} collective-permute-done((f32[3,8,128]{2,1,0:T(8,128)S(1)}, f32[3,8,128]{2,1,0:T(8,128)S(1)}, u32[]{:S(2)}, u32[]{:S(2)}) %collective-permute-start.16) | collective-permute-done | bytes 12320 | tf_op jit(solution)/shard_map/ppermute | solution.py:472
  47.5 0.0 collective-permute-done.17.pair0
  47.5 3.4 %shard_map.72 = (bf16[8192,128]{1,0:T(8,128)(2,1)}, f32[8,9,136,128]{3,2,1,0:T(8,128)S(1)}) custom-call(s32[2,8]{1,0:T(2,128)S(1)} %copy-done, f32[3,8,128]{2,1,0:T(8,128)S(1)} %add.15.same, f32[3,8,128]{2,1,0:T(8,128)S(1)} %collective-permute-done.16.other, ...), custom_call_target="tpu_custom_call", output_to_operand_aliasing={{1}: (11, {})} | custom-call | tf_op jit(solution)/shard_map/pallas_call | solution.py:443
  (7 shorter events, 0.0 us)
Async XLA Ops:
  0.0 13.8 %copy-start = (s32[2,8]{1,0:T(2,128)S(1)}, s32[2,8]{1,0:T(2,128)}, u32[]{:S(2)}) copy-start(s32[2,8]{1,0:T(2,128)} %kindy.7) | copy-start | bytes 196
  3.3 10.5 %collective-permute-start.2 = (bf16[512,128]{1,0:T(8,128)(2,1)S(1)}, bf16[512,128]{1,0:T(8,128)(2,1)S(1)}, u32[]{:S(2)}, u32[]{:S(2)}) collective-permute-start(bf16[512,128]{1,0:T(8,128)(2,1)S(1)} %get-tuple-element.38), channel_id=1, source_target_pairs={{0,2},{4,6},{2,0},{6,4},{1,3},{5,7},{3,1},{7,5},{8,10},{12,14},{10... | collective-permute-start | bytes 393224 | tf_op jit(solution)/shard_map/ppermute | solution.py:474
  6.4 7.4 %collective-permute-start.3 = (bf16[512,128]{1,0:T(8,128)(2,1)S(1)}, bf16[512,128]{1,0:T(8,128)(2,1)S(1)}, u32[]{:S(2)}, u32[]{:S(2)}) collective-permute-start(bf16[512,128]{1,0:T(8,128)(2,1)S(1)} %get-tuple-element.39), channel_id=1, source_target_pairs={{2,4},{4,2},{3,5},{5,3},{10,12},{12,10},{11,13},{13,11},{18,20},{2... | collective-permute-start | bytes 393224 | tf_op jit(solution)/shard_map/ppermute | solution.py:475
  7.1 1.3 %collective-permute-start = (f32[7,8,128]{2,1,0:T(8,128)S(1)}, f32[7,8,128]{2,1,0:T(8,128)S(1)}, u32[]{:S(2)}, u32[]{:S(2)}) collective-permute-start(f32[7,8,128]{2,1,0:T(8,128)S(1)} %get-tuple-element.36), channel_id=1, source_target_pairs={{0,8},{8,0},{16,24},{24,16},{1,9},{9,1},{17,25},{25,17},{2,10},{10... | collective-permute-start | bytes 86024 | tf_op jit(solution)/shard_map/ppermute | solution.py:470
  8.4 5.4 %collective-permute-start.1 = (f32[7,8,128]{2,1,0:T(8,128)S(1)}, f32[7,8,128]{2,1,0:T(8,128)S(1)}, u32[]{:S(2)}, u32[]{:S(2)}) collective-permute-start(f32[7,8,128]{2,1,0:T(8,128)S(1)} %add.12.same), channel_id=1, source_target_pairs={{0,16},{8,24},{16,0},{24,8},{1,17},{9,25},{17,1},{25,9},{2,18},{10... | collective-permute-start | bytes 86024 | tf_op jit(solution)/shard_map/ppermute | solution.py:472
  9.9 3.9 %collective-permute-start.4 = (bf16[2,8,512]{2,1,0:T(8,128)(2,1)S(1)}, bf16[2,8,512]{2,1,0:T(8,128)(2,1)S(1)}, u32[]{:S(2)}, u32[]{:S(2)}) collective-permute-start(bf16[2,8,512]{2,1,0:T(8,128)(2,1)S(1)} %get-tuple-element.40), channel_id=1, source_target_pairs={{0,1},{1,0},{2,3},{3,2},{4,5},{5,4},{6,7},{7,6},{8,9},{9,8},{10,11... | collective-permute-start | bytes 49160 | tf_op jit(solution)/shard_map/ppermute | solution.py:473
  18.3 10.3 %collective-permute-start.7 = (bf16[4,128,128]{2,1,0:T(8,128)(2,1)S(1)}, bf16[4,128,128]{2,1,0:T(8,128)(2,1)S(1)}, u32[]{:S(2)}, u32[]{:S(2)}) collective-permute-start(bf16[4,128,128]{2,1,0:T(8,128)(2,1)S(1)} %get-tuple-element.51), channel_id=1, source_target_pairs={{0,2},{4,6},{2,0},{6,4},{1,3},{5,7},{3,1},{7,5},{8,10},{12,14},{10... | collective-permute-start | bytes 393224 | tf_op jit(solution)/shard_map/ppermute | solution.py:474
  22.7 5.9 %collective-permute-start.8 = (bf16[4,128,128]{2,1,0:T(8,128)(2,1)S(1)}, bf16[4,128,128]{2,1,0:T(8,128)(2,1)S(1)}, u32[]{:S(2)}, u32[]{:S(2)}) collective-permute-start(bf16[4,128,128]{2,1,0:T(8,128)(2,1)S(1)} %get-tuple-element.52), channel_id=1, source_target_pairs={{2,4},{4,2},{3,5},{5,3},{10,12},{12,10},{11,13},{13,11},{18,20},{2... | collective-permute-start | bytes 393224 | tf_op jit(solution)/shard_map/ppermute | solution.py:475
  23.4 1.5 %collective-permute-start.5 = (f32[3,8,128]{2,1,0:T(8,128)S(1)}, f32[3,8,128]{2,1,0:T(8,128)S(1)}, u32[]{:S(2)}, u32[]{:S(2)}) collective-permute-start(f32[3,8,128]{2,1,0:T(8,128)S(1)} %get-tuple-element.50), channel_id=1, source_target_pairs={{0,8},{8,0},{16,24},{24,16},{1,9},{9,1},{17,25},{25,17},{2,10},{10... | collective-permute-start | bytes 36872 | tf_op jit(solution)/shard_map/ppermute | solution.py:470
  23.5 3.8 %collective-permute-start.9 = (bf16[8,8,128]{2,1,0:T(8,128)(2,1)S(1)}, bf16[8,8,128]{2,1,0:T(8,128)(2,1)S(1)}, u32[]{:S(2)}, u32[]{:S(2)}) collective-permute-start(bf16[8,8,128]{2,1,0:T(8,128)(2,1)S(1)} %get-tuple-element.53), channel_id=1, source_target_pairs={{0,1},{1,0},{2,3},{3,2},{4,5},{5,4},{6,7},{7,6},{8,9},{9,8},{10,11... | collective-permute-start | bytes 49160 | tf_op jit(solution)/shard_map/ppermute | solution.py:473
  24.9 3.7 %collective-permute-start.6 = (f32[3,8,128]{2,1,0:T(8,128)S(1)}, f32[3,8,128]{2,1,0:T(8,128)S(1)}, u32[]{:S(2)}, u32[]{:S(2)}) collective-permute-start(f32[3,8,128]{2,1,0:T(8,128)S(1)} %add.13.same), channel_id=1, source_target_pairs={{0,16},{8,24},{16,0},{24,8},{1,17},{9,25},{17,1},{25,9},{2,18},{10... | collective-permute-start | bytes 36872 | tf_op jit(solution)/shard_map/ppermute | solution.py:472
  30.1 6.9 %collective-permute-start.12 = (bf16[4,128,128]{2,1,0:T(8,128)(2,1)S(1)}, bf16[4,128,128]{2,1,0:T(8,128)(2,1)S(1)}, u32[]{:S(2)}, u32[]{:S(2)}) collective-permute-start(bf16[4,128,128]{2,1,0:T(8,128)(2,1)S(1)} %get-tuple-element.57), channel_id=1, source_target_pairs={{0,2},{4,6},{2,0},{6,4},{1,3},{5,7},{3,1},{7,5},{8,10},{12,14},{10... | collective-permute-start | bytes 393224 | tf_op jit(solution)/shard_map/ppermute | solution.py:474
  31.4 5.6 %collective-permute-start.13 = (bf16[4,128,128]{2,1,0:T(8,128)(2,1)S(1)}, bf16[4,128,128]{2,1,0:T(8,128)(2,1)S(1)}, u32[]{:S(2)}, u32[]{:S(2)}) collective-permute-start(bf16[4,128,128]{2,1,0:T(8,128)(2,1)S(1)} %get-tuple-element.58), channel_id=1, source_target_pairs={{2,4},{4,2},{3,5},{5,3},{10,12},{12,10},{11,13},{13,11},{18,20},{2... | collective-permute-start | bytes 393224 | tf_op jit(solution)/shard_map/ppermute | solution.py:475
  32.1 1.2 %collective-permute-start.10 = (f32[3,8,128]{2,1,0:T(8,128)S(1)}, f32[3,8,128]{2,1,0:T(8,128)S(1)}, u32[]{:S(2)}, u32[]{:S(2)}) collective-permute-start(f32[3,8,128]{2,1,0:T(8,128)S(1)} %get-tuple-element.56), channel_id=1, source_target_pairs={{0,8},{8,0},{16,24},{24,16},{1,9},{9,1},{17,25},{25,17},{2,10},{10... | collective-permute-start | bytes 36872 | tf_op jit(solution)/shard_map/ppermute | solution.py:470
  32.2 3.8 %collective-permute-start.14 = (bf16[8,8,128]{2,1,0:T(8,128)(2,1)S(1)}, bf16[8,8,128]{2,1,0:T(8,128)(2,1)S(1)}, u32[]{:S(2)}, u32[]{:S(2)}) collective-permute-start(bf16[8,8,128]{2,1,0:T(8,128)(2,1)S(1)} %get-tuple-element.59), channel_id=1, source_target_pairs={{0,1},{1,0},{2,3},{3,2},{4,5},{5,4},{6,7},{7,6},{8,9},{9,8},{10,11... | collective-permute-start | bytes 49160 | tf_op jit(solution)/shard_map/ppermute | solution.py:473
  33.3 3.7 %collective-permute-start.11 = (f32[3,8,128]{2,1,0:T(8,128)S(1)}, f32[3,8,128]{2,1,0:T(8,128)S(1)}, u32[]{:S(2)}, u32[]{:S(2)}) collective-permute-start(f32[3,8,128]{2,1,0:T(8,128)S(1)} %add.14.same), channel_id=1, source_target_pairs={{0,16},{8,24},{16,0},{24,8},{1,17},{9,25},{17,1},{25,9},{2,18},{10... | collective-permute-start | bytes 36872 | tf_op jit(solution)/shard_map/ppermute | solution.py:472
  38.6 8.9 %collective-permute-start.17 = (bf16[4,128,128]{2,1,0:T(8,128)(2,1)S(1)}, bf16[4,128,128]{2,1,0:T(8,128)(2,1)S(1)}, u32[]{:S(2)}, u32[]{:S(2)}) collective-permute-start(bf16[4,128,128]{2,1,0:T(8,128)(2,1)S(1)} %get-tuple-element.62), channel_id=1, source_target_pairs={{0,2},{4,6},{2,0},{6,4},{1,3},{5,7},{3,1},{7,5},{8,10},{12,14},{10... | collective-permute-start | bytes 393224 | tf_op jit(solution)/shard_map/ppermute | solution.py:474
  41.9 5.6 %collective-permute-start.18 = (bf16[4,128,128]{2,1,0:T(8,128)(2,1)S(1)}, bf16[4,128,128]{2,1,0:T(8,128)(2,1)S(1)}, u32[]{:S(2)}, u32[]{:S(2)}) collective-permute-start(bf16[4,128,128]{2,1,0:T(8,128)(2,1)S(1)} %get-tuple-element.63), channel_id=1, source_target_pairs={{2,4},{4,2},{3,5},{5,3},{10,12},{12,10},{11,13},{13,11},{18,20},{2... | collective-permute-start | bytes 393224 | tf_op jit(solution)/shard_map/ppermute | solution.py:475
  42.6 1.2 %collective-permute-start.15 = (f32[3,8,128]{2,1,0:T(8,128)S(1)}, f32[3,8,128]{2,1,0:T(8,128)S(1)}, u32[]{:S(2)}, u32[]{:S(2)}) collective-permute-start(f32[3,8,128]{2,1,0:T(8,128)S(1)} %get-tuple-element.61), channel_id=1, source_target_pairs={{0,8},{8,0},{16,24},{24,16},{1,9},{9,1},{17,25},{25,17},{2,10},{10... | collective-permute-start | bytes 36872 | tf_op jit(solution)/shard_map/ppermute | solution.py:470
  42.6 3.8 %collective-permute-start.19 = (bf16[8,8,128]{2,1,0:T(8,128)(2,1)S(1)}, bf16[8,8,128]{2,1,0:T(8,128)(2,1)S(1)}, u32[]{:S(2)}, u32[]{:S(2)}) collective-permute-start(bf16[8,8,128]{2,1,0:T(8,128)(2,1)S(1)} %get-tuple-element.64), channel_id=1, source_target_pairs={{0,1},{1,0},{2,3},{3,2},{4,5},{5,4},{6,7},{7,6},{8,9},{9,8},{10,11... | collective-permute-start | bytes 49160 | tf_op jit(solution)/shard_map/ppermute | solution.py:473
  43.8 3.7 %collective-permute-start.16 = (f32[3,8,128]{2,1,0:T(8,128)S(1)}, f32[3,8,128]{2,1,0:T(8,128)S(1)}, u32[]{:S(2)}, u32[]{:S(2)}) collective-permute-start(f32[3,8,128]{2,1,0:T(8,128)S(1)} %add.15.same), channel_id=1, source_target_pairs={{0,16},{8,24},{16,0},{24,8},{1,17},{9,25},{17,1},{25,9},{2,18},{10... | collective-permute-start | bytes 36872 | tf_op jit(solution)/shard_map/ppermute | solution.py:472
